TPU v7x, 32 devices: a whole 2x2x4 slice. The times are simulated.
32 devices in a mesh: group: 4 (over y, x), tile: 8 (over z, core).
Axes of the slice: x: 2, y: 2, z: 4, core: 2. Of those that a mesh axis runs over, the one named last changes fastest.
Arguments:
- velocity_u: float32 [4, 1024, 1024], P('group', 'tile'), may hold values from -6 to 6
- velocity_v: float32 [4, 1024, 1024], P('group', 'tile'), may hold values from -6 to 6
- tracer: float32 [4, 1024, 1024], P('group', 'tile'), may hold values from -6 to 6
- land: int32 [1024, 1024], P('tile'), may hold values 0 or 1
- tile_depth: int32 [64], replicated, may hold values from 1 to 4, 96 in all
- conv_one: bfloat16 [64, 3, 3, 3], replicated, may hold values from -1.25 to 1.25
- bias_one: float32 [64], replicated, may hold values from -3 to 3
- conv_two: bfloat16 [64, 64, 3, 3], replicated, may hold values from -0.25 to 0.25
- bias_two: float32 [64], replicated, may hold values from -3 to 3
- conv_three: bfloat16 [3, 64, 3, 3], replicated, may hold values from -0.25 to 0.25
- bias_three: float32 [3], replicated, may hold values from -3 to 3
Outputs:
- east_two: float32 [4, 1024, 1024], P('group', 'tile')
- north_two: float32 [4, 1024, 1024], P('group', 'tile')
- tracer_one: float32 [4, 1024, 1024], P('group', 'tile')
Inputs may be any that keep to these rules, and one draw needn't show every extreme that they name: `land`: 1 marks water. `tile_depth`: the entries sum to exactly 96; some column is 4 levels deep.
All inputs are finite; a program needn't handle non-finite values. No bound on the sum of `land` on one device may be relied on, other than what follows from the above.
Results may differ from a plain program's by a relative error of at most 0.00083.
Values may be sent and summed in bfloat16 or wider, within the bound.
No kernel may reach another device: no remote copies, remote signals or barrier semaphores. Data moves between devices by JAX's collectives and lax.ppermute only.
A program may use at most 128 MiB of HBM per device.

v0:
```python
import jax
import jax.numpy as jnp
from jax import lax
from jax.sharding import PartitionSpec as P

WET_DEV = 3


time_step = 0.1
viscosity = 0.5
diffusivity = 0.5
eddy_gain = 0.5
coriolis_base = 0.2
coriolis_slope = 0.6


def extended_2(block, sides, width):
    for axis, dim in sides:
        count = lax.axis_size(axis)
        forward = [(i, i + 1) for i in range(count - 1)]
        backward = [(target, source) for source, target in forward]
        low = lax.ppermute(
            lax.slice_in_dim(block, block.shape[dim] - width, None, axis=dim), axis, forward
        )
        high = lax.ppermute(lax.slice_in_dim(block, 0, width, axis=dim), axis, backward)
        block = jnp.concatenate([low, block, high], axis=dim)
    return block


def east_diff(field):
    return 0.5 * (field[..., 2:, 1:-1] - field[..., :-2, 1:-1])


def north_diff(field):
    return 0.5 * (field[..., 1:-1, 2:] - field[..., 1:-1, :-2])


def laplace(field):
    return (
        field[..., 2:, 1:-1]
        + field[..., :-2, 1:-1]
        + field[..., 1:-1, 2:]
        + field[..., 1:-1, :-2]
        - 4.0 * field[..., 1:-1, 1:-1]
    )


def advance(padded_east, padded_north, padded_tracer, active, coriolis):
    inner_east = padded_east[..., 1:-1, 1:-1]
    inner_north = padded_north[..., 1:-1, 1:-1]
    inner_tracer = padded_tracer[..., 1:-1, 1:-1]
    grad_east = east_diff(padded_tracer)
    grad_north = north_diff(padded_tracer)
    new_east = inner_east + time_step * active * (
        coriolis * inner_north - grad_east + viscosity * laplace(padded_east)
    )
    new_north = inner_north + time_step * active * (
        -coriolis * inner_east - grad_north + viscosity * laplace(padded_north)
    )
    new_tracer = inner_tracer + time_step * active * (
        -(inner_east * grad_east + inner_north * grad_north) + diffusivity * laplace(padded_tracer)
    )
    return (new_east, new_north, new_tracer)


def latitude(first_row, row_count, total_rows):
    places = (first_row + jnp.arange(row_count, dtype=jnp.int32)).astype(jnp.float32)
    return (coriolis_base + coriolis_slope * (places + 0.5) / total_rows)[:, None]


def convolve(source, kernel):
    return lax.conv_general_dilated(
        source,
        kernel,
        (1, 1),
        "VALID",
        dimension_numbers=("NCHW", "OIHW", "NCHW"),
        preferred_element_type=jnp.float32,
    )


def make_closure(conv_one, bias_one, conv_two, bias_two, conv_three, bias_three):

    def closure(window):
        hidden_one = jax.nn.silu(
            convolve(window[None], conv_one) + bias_one[None, :, None, None]
        ).astype(jnp.bfloat16)
        hidden_two = jax.nn.silu(
            convolve(hidden_one, conv_two) + bias_two[None, :, None, None]
        ).astype(jnp.bfloat16)
        return (convolve(hidden_two, conv_three) + bias_three[None, :, None, None]).astype(
            jnp.bfloat16
        )[0]

    return closure


def body(
    velocity_u,
    velocity_v,
    tracer,
    land,
    tile_depth,
    conv_one,
    bias_one,
    conv_two,
    bias_two,
    conv_three,
    bias_three,
):
    levels_here, rows, cols = velocity_u.shape
    across = cols // rows
    group_index = lax.axis_index("group")
    tile_index = lax.axis_index("tile")
    group_count = lax.axis_size("group")
    tile_count = lax.axis_size("tile")
    devices = group_count * tile_count
    total_rows = rows * tile_count
    depth_grid = tile_depth.reshape(tile_count, across)
    my_depth = lax.dynamic_index_in_dim(depth_grid, tile_index, 0, keepdims=False)
    my_levels = group_index * levels_here + jnp.arange(levels_here, dtype=jnp.int32)
    wet_tiles = my_levels[:, None] < my_depth[None, :]
    wet_cells = jnp.repeat(wet_tiles, rows, axis=1)
    active = ((land == 1)[None] & wet_cells[:, None, :]).astype(jnp.float32)
    stacked = jnp.stack([velocity_u, velocity_v, tracer])
    extended = extended_2(stacked, (("tile", 2),), 1)
    extended = jnp.pad(extended, ((0, 0), (0, 0), (0, 0), (1, 1)))
    coriolis = latitude(tile_index * rows, rows, total_rows)
    east_one, north_one, tracer_one = advance(
        extended[0], extended[1], extended[2], active, coriolis
    )
    features = (jnp.stack([east_one, north_one, tracer_one], axis=1) * active[:, None]).astype(
        jnp.bfloat16
    )
    framed = extended_2(features, (("tile", 2),), 3)
    framed = jnp.pad(framed, ((0, 0), (0, 0), (0, 0), (3, 3)))
    windows = jnp.stack(
        [framed[:, :, :, column * rows : column * rows + rows + 6] for column in range(across)],
        axis=1,
    )
    windows = windows.reshape((levels_here * across,) + windows.shape[2:])
    wet_flat = wet_tiles.reshape(-1)
    closure = make_closure(conv_one, bias_one, conv_two, bias_two, conv_three, bias_three)
    level_table = (
        jnp.arange(group_count, dtype=jnp.int32)[:, None] * levels_here
        + jnp.arange(levels_here, dtype=jnp.int32)[None, :]
    )
    wet_count = wet_flat.astype(jnp.int32)
    counts = jnp.sum(
        (level_table[:, :, None, None] < depth_grid[None, None]).astype(jnp.int32), axis=(1, 3)
    ).reshape(-1)
    reaching = jnp.cumsum(counts)
    myself = group_index * tile_count + tile_index
    first_rank = reaching[myself] - counts[myself]
    ranks = first_rank + jnp.cumsum(wet_count) - wet_count
    owners = ranks % devices
    targets = jnp.where(wet_flat, owners, devices)
    outgoing = (
        jnp.zeros((devices,) + windows.shape[1:], jnp.bfloat16)
        .at[targets]
        .set(windows, mode="drop")
    )
    arriving = lax.all_to_all(outgoing, ("group", "tile"), split_axis=0, concat_axis=0, tiled=True)
    wanted = myself + devices * jnp.arange(WET_DEV, dtype=jnp.int32)
    senders = jnp.sum((reaching[None, :] <= wanted[:, None]).astype(jnp.int32), axis=1)
    results = lax.map(closure, arriving[senders])
    returning = jnp.zeros((devices,) + results.shape[1:], jnp.bfloat16).at[senders].set(results)
    landed = lax.all_to_all(returning, ("group", "tile"), split_axis=0, concat_axis=0, tiled=True)
    picked = landed[jnp.where(wet_flat, owners, 0)]
    mine = jnp.where(wet_flat[:, None, None, None], picked, jnp.zeros_like(picked))
    components = mine.shape[1]
    stress = mine.reshape(levels_here, across, components, rows, rows).transpose(0, 2, 3, 1, 4)
    stress = stress.reshape(levels_here, components, rows, cols)
    masked = (stress.astype(jnp.float32) * active[:, None]).astype(jnp.bfloat16)
    framed_stress = extended_2(masked, (("tile", 2),), 1)
    framed_stress = jnp.pad(framed_stress.astype(jnp.float32), ((0, 0), (0, 0), (0, 0), (1, 1)))
    push_east = east_diff(framed_stress[:, 0]) + north_diff(framed_stress[:, 1])
    push_north = east_diff(framed_stress[:, 1]) + north_diff(framed_stress[:, 2])
    east_two = east_one + eddy_gain * active * push_east
    north_two = north_one + eddy_gain * active * push_north
    return (east_two, north_two, tracer_one)


def solution(mesh):
    in_specs = (
        P("group", "tile", None),
        P("group", "tile", None),
        P("group", "tile", None),
        P("tile", None),
        P(),
        P(),
        P(),
        P(),
        P(),
        P(),
        P(),
    )
    out_specs = (P("group", "tile", None), P("group", "tile", None), P("group", "tile", None))
    return jax.shard_map(body, mesh=mesh, in_specs=in_specs, out_specs=out_specs, check_vma=False)
```

profile of v0, /device:TPU:1, one launch (start us, length us, event | category | flops | bytes accessed | tf_op | source)
XLA Modules:
  0.0 720.3 jit_solution(2473400631177405082)
XLA Ops:
  1.6 4.6 collective-permute-start
  6.2 1.9 collective-permute-start.1
  17.4 3.6 collective-permute-start.2
  23.0 3.2 collective-permute-done.3
  27.5 3.3 broadcast_in_dim.34
  30.8 5.0 scatter_fusion
  35.8 3.6 all-to-all-start
  41.0 146.3 %all-to-all-done = bf16[32,3,134,134]{3,2,1,0:T(8,128)(2,1)} async-done(((bf16[32,3,134,134]{3,2,1,0:T(8,128)(2,1)}), bf16[32,3,134,134]{3,2,1,0:T(8,128)(2,1)}, u32[]{:S(2)}, u32[]{:S(2)}) %all-to-all-start) | async-done | bytes 3447584 | tf_op jit(solution)/shard_map/all_to_all | solution.py:163
  187.3 3.5 gather_fusion
  190.8 429.8 %while.10 = (s32[]{:T(128)}, bf16[3,3,128,128]{3,2,1,0:T(8,128)(2,1)S(1)}, bf16[3,3,134,134]{3,2,1,0:T(8,128)(2,1)S(1)}, bf16[64,3,3,3]{0,1,3,2:T(4,128)(2,1)}, ...) while((s32[]{:T(128)}, ...), condition=%wide.region_6.7_spmd, body=%wide.region_5.6_spmd.sunk | while | flops 1458590720 | bytes 14098451 | solution.py:166
  210.9 10.2 %copy.85 = bf16[3,134,1,8,17]{3,0,4,1,2:T(4,128)(2,1)S(1)} copy(bf16[3,134,1,8,17]{1,4,3,0,2:T(8,128)(2,1)S(1)} %reshape.394) | data formatting | bytes 218688 | tf_op jit(solution)/shard_map/while/body/eval_jaxpr/conv_general_dilated | solution.py:72
  221.4 10.1 %select_bitcast_fusion.4 = bf16[132,1,8,17,64]{4,2,3,0,1:T(8,128)(2,1)S(1)} fusion(f32[64]{0:T(128)} %get-tuple-element.232, pred[8,17]{0,1:T(8,128)(4,1)} %get-tuple-element.239, bf16[64,3,3,3]{0,1,3,2:T(4,128)(2,1)} %get-tuple-element.231, bf16[3,134,1,7,2]{3,0,4,1,2:T(4,128)(2,1)S(1)} %slice.360, bf16[3,134,1,8,17]{3,0,4,1,2:T(4,128)(2,1)S(1)} %copy.85), kind=kOutput, calls=%fused_computation.24.clone.1 | convolution fusion | flops 71600160 | bytes 2422304 | tf_op jit(solution)/shard_map/while/body/eval_jaxpr/conv_general_dilated | solution.py:72
  231.7 12.1 %select_bitcast_fusion.5 = bf16[130,1,8,17,64]{4,2,3,0,1:T(8,128)(2,1)S(1)} fusion(f32[64]{0:T(128)S(1)} %copy-done.23, pred[8,17]{0,1:T(8,128)(4,1)S(1)} %copy-done.24, bf16[64,64,3,3]{1,0,3,2:T(8,128)(2,1)S(1)} %copy-done.22, bf16[132,1,7,2,64]{4,2,3,0,1:T(8,128)(2,1)S(1)} %slice.361, bf16[132,1,8,17,64]{4,2,3,0,1:T(8,128)(2,1)S(1)} %select_bitcast_fusion.4), kind=kOutput, calls=%fused_computation.25.clone.1 | convolution fusion | flops 1319136256 | bytes 4871560 | tf_op jit(solution)/shard_map/while/body/eval_jaxpr/conv_general_dilated | solution.py:72
  243.9 99.3 %fusion.100 = f32[128,8,17,3]{1,3,2,0:T(4,128)} fusion(bf16[3,64,3,3]{1,0,3,2:T(4,128)(2,1)S(1)} %copy-done.16, bf16[130,1,7,2,64]{4,2,3,0,1:T(8,128)(2,1)S(1)} %slice.362, bf16[130,1,8,17,64]{4,2,3,0,1:T(8,128)(2,1)S(1)} %select_bitcast_fusion.5), kind=kOutput, calls=%fused_computation.20.clone.1 | convolution fusion | flops 67749888 | bytes 2708352 | tf_op jit(solution)/shard_map/while/body/eval_jaxpr/conv_general_dilated | solution.py:72
  343.2 3.6 copy.86
  347.5 10.2 %copy.85 = bf16[3,134,1,8,17]{3,0,4,1,2:T(4,128)(2,1)S(1)} copy(bf16[3,134,1,8,17]{1,4,3,0,2:T(8,128)(2,1)S(1)} %reshape.394) | data formatting | bytes 218688 | tf_op jit(solution)/shard_map/while/body/eval_jaxpr/conv_general_dilated | solution.py:72
  358.0 10.1 %select_bitcast_fusion.4 = bf16[132,1,8,17,64]{4,2,3,0,1:T(8,128)(2,1)S(1)} fusion(f32[64]{0:T(128)} %get-tuple-element.232, pred[8,17]{0,1:T(8,128)(4,1)} %get-tuple-element.239, bf16[64,3,3,3]{0,1,3,2:T(4,128)(2,1)} %get-tuple-element.231, bf16[3,134,1,7,2]{3,0,4,1,2:T(4,128)(2,1)S(1)} %slice.360, bf16[3,134,1,8,17]{3,0,4,1,2:T(4,128)(2,1)S(1)} %copy.85), kind=kOutput, calls=%fused_computation.24.clone.1 | convolution fusion | flops 71600160 | bytes 2422304 | tf_op jit(solution)/shard_map/while/body/eval_jaxpr/conv_general_dilated | solution.py:72
  368.3 12.1 %select_bitcast_fusion.5 = bf16[130,1,8,17,64]{4,2,3,0,1:T(8,128)(2,1)S(1)} fusion(f32[64]{0:T(128)S(1)} %copy-done.23, pred[8,17]{0,1:T(8,128)(4,1)S(1)} %copy-done.24, bf16[64,64,3,3]{1,0,3,2:T(8,128)(2,1)S(1)} %copy-done.22, bf16[132,1,7,2,64]{4,2,3,0,1:T(8,128)(2,1)S(1)} %slice.361, bf16[132,1,8,17,64]{4,2,3,0,1:T(8,128)(2,1)S(1)} %select_bitcast_fusion.4), kind=kOutput, calls=%fused_computation.25.clone.1 | convolution fusion | flops 1319136256 | bytes 4871560 | tf_op jit(solution)/shard_map/while/body/eval_jaxpr/conv_general_dilated | solution.py:72
  380.5 99.3 %fusion.100 = f32[128,8,17,3]{1,3,2,0:T(4,128)} fusion(bf16[3,64,3,3]{1,0,3,2:T(4,128)(2,1)S(1)} %copy-done.16, bf16[130,1,7,2,64]{4,2,3,0,1:T(8,128)(2,1)S(1)} %slice.362, bf16[130,1,8,17,64]{4,2,3,0,1:T(8,128)(2,1)S(1)} %select_bitcast_fusion.5), kind=kOutput, calls=%fused_computation.20.clone.1 | convolution fusion | flops 67749888 | bytes 2708352 | tf_op jit(solution)/shard_map/while/body/eval_jaxpr/conv_general_dilated | solution.py:72
  479.8 3.6 copy.86
  484.1 10.2 %copy.85 = bf16[3,134,1,8,17]{3,0,4,1,2:T(4,128)(2,1)S(1)} copy(bf16[3,134,1,8,17]{1,4,3,0,2:T(8,128)(2,1)S(1)} %reshape.394) | data formatting | bytes 218688 | tf_op jit(solution)/shard_map/while/body/eval_jaxpr/conv_general_dilated | solution.py:72
  494.6 10.1 %select_bitcast_fusion.4 = bf16[132,1,8,17,64]{4,2,3,0,1:T(8,128)(2,1)S(1)} fusion(f32[64]{0:T(128)} %get-tuple-element.232, pred[8,17]{0,1:T(8,128)(4,1)} %get-tuple-element.239, bf16[64,3,3,3]{0,1,3,2:T(4,128)(2,1)} %get-tuple-element.231, bf16[3,134,1,7,2]{3,0,4,1,2:T(4,128)(2,1)S(1)} %slice.360, bf16[3,134,1,8,17]{3,0,4,1,2:T(4,128)(2,1)S(1)} %copy.85), kind=kOutput, calls=%fused_computation.24.clone.1 | convolution fusion | flops 71600160 | bytes 2422304 | tf_op jit(solution)/shard_map/while/body/eval_jaxpr/conv_general_dilated | solution.py:72
  504.9 12.1 %select_bitcast_fusion.5 = bf16[130,1,8,17,64]{4,2,3,0,1:T(8,128)(2,1)S(1)} fusion(f32[64]{0:T(128)S(1)} %copy-done.23, pred[8,17]{0,1:T(8,128)(4,1)S(1)} %copy-done.24, bf16[64,64,3,3]{1,0,3,2:T(8,128)(2,1)S(1)} %copy-done.22, bf16[132,1,7,2,64]{4,2,3,0,1:T(8,128)(2,1)S(1)} %slice.361, bf16[132,1,8,17,64]{4,2,3,0,1:T(8,128)(2,1)S(1)} %select_bitcast_fusion.4), kind=kOutput, calls=%fused_computation.25.clone.1 | convolution fusion | flops 1319136256 | bytes 4871560 | tf_op jit(solution)/shard_map/while/body/eval_jaxpr/conv_general_dilated | solution.py:72
  517.1 99.3 %fusion.100 = f32[128,8,17,3]{1,3,2,0:T(4,128)} fusion(bf16[3,64,3,3]{1,0,3,2:T(4,128)(2,1)S(1)} %copy-done.16, bf16[130,1,7,2,64]{4,2,3,0,1:T(8,128)(2,1)S(1)} %slice.362, bf16[130,1,8,17,64]{4,2,3,0,1:T(8,128)(2,1)S(1)} %select_bitcast_fusion.5), kind=kOutput, calls=%fused_computation.20.clone.1 | convolution fusion | flops 67749888 | bytes 2708352 | tf_op jit(solution)/shard_map/while/body/eval_jaxpr/conv_general_dilated | solution.py:72
  616.4 3.6 copy.86
  620.6 2.4 broadcast_in_dim.29
  623.0 2.3 scatter_fusion.1
  625.4 3.3 all-to-all-start.1
  628.7 72.2 %all-to-all-done.1 = bf16[32,3,128,128]{3,2,1,0:T(8,128)(2,1)S(1)} async-done(((bf16[32,3,128,128]{3,2,1,0:T(8,128)(2,1)}), bf16[32,3,128,128]{3,2,1,0:T(8,128)(2,1)S(1)}, u32[]{:S(2)}, u32[]{:S(2)}) %all-to-all-start.1) | async-done | bytes 3145760 | tf_op jit(solution)/shard_map/all_to_all | solution.py:168
  711.2 2.4 collective-permute-start.5
  713.8 2.4 collective-permute-done.5
  718.0 1.9 fusion.50
  (160 shorter events, 29.2 us)
Async XLA Ops:
  0.6 13.1 %copy-start.9 = (f32[1,128,1024]{2,1,0:T(8,128)S(1)}, f32[1,128,1024]{2,1,0:T(8,128)}, u32[]{:S(2)}) copy-start(f32[1,128,1024]{2,1,0:T(8,128)} %param.13) | copy-start | bytes 1572868
  0.6 13.1 %copy-start.8 = (f32[1,128,1024]{2,1,0:T(8,128)S(1)}, f32[1,128,1024]{2,1,0:T(8,128)}, u32[]{:S(2)}) copy-start(f32[1,128,1024]{2,1,0:T(8,128)} %param.14) | copy-start | bytes 1572868
  0.7 13.1 %copy-start.7 = (f32[1,128,1024]{2,1,0:T(8,128)S(1)}, f32[1,128,1024]{2,1,0:T(8,128)}, u32[]{:S(2)}) copy-start(f32[1,128,1024]{2,1,0:T(8,128)} %param.15) | copy-start | bytes 1572868
  1.6 12.1 %collective-permute-start = (f32[3,1,1,1024]{3,2,1,0:T(1,128)S(1)}, f32[3,1,1,1024]{3,2,1,0:T(1,128)S(1)}, u32[]{:S(2)}, u32[]{:S(2)}) collective-permute-start(f32[3,1,1,1024]{3,2,1,0:T(1,128)S(1)} %get-tuple-element.137), channel_id=1, source_target_pairs={{0,1},{1,2},{2,3},{3,4},{4,5},{5,6},{6,7},{8,9},{9,10},{10,11},{11... | collective-permute-start | bytes 36872 | tf_op jit(solution)/shard_map/ppermute | solution.py:22
  6.2 7.5 %collective-permute-start.1 = (f32[3,1,1,1024]{3,2,1,0:T(1,128)S(1)}, f32[3,1,1,1024]{3,2,1,0:T(1,128)S(1)}, u32[]{:S(2)}, u32[]{:S(2)}) collective-permute-start(f32[3,1,1,1024]{3,2,1,0:T(1,128)S(1)} %get-tuple-element.138), channel_id=1, source_target_pairs={{1,0},{2,1},{3,2},{4,3},{5,4},{6,5},{7,6},{9,8},{10,9},{11,10},{12... | collective-permute-start | bytes 36872 | tf_op jit(solution)/shard_map/ppermute | solution.py:25
  9.2 13.8 %copy-start.17 = (pred[1,8]{1,0:T(4,128)(4,1)}, pred[1,8]{1,0:T(4,128)(4,1)S(1)}, u32[]{:S(2)}) copy-start(pred[1,8]{1,0:T(4,128)(4,1)S(1)} %get-tuple-element.128) | copy-start | bytes 28
  11.8 4.2 copy-start.10
  11.8 5.3 copy-start
  17.1 9.3 %copy-start.3 = (f32[1,128,1024]{2,1,0:T(8,128)}, f32[1,128,1024]{2,1,0:T(8,128)S(1)}, u32[]{:S(2)}) copy-start(f32[1,128,1024]{2,1,0:T(8,128)S(1)} %fusion.64) | copy-start | bytes 1572868
  17.4 5.6 collective-permute-start.2
  21.1 5.1 collective-permute-start.3
  35.8 4.3 copy-start.15
  35.8 154.9 %copy-start.13 = (f32[3]{0:T(128)S(1)}, f32[3]{0:T(128)}, u32[]{:S(2)}) copy-start(f32[3]{0:T(128)} %param.23) | copy-start | bytes 40
  35.8 151.4 %all-to-all-start = ((bf16[32,3,134,134]{3,2,1,0:T(8,128)(2,1)}), bf16[32,3,134,134]{3,2,1,0:T(8,128)(2,1)}, u32[]{:S(2)}, u32[]{:S(2)}) async-start(bf16[32,3,134,134]{3,2,1,0:T(8,128)(2,1)} %scatter_fusion), calls=%async_computation | async-start | bytes 13369344 | tf_op jit(solution)/shard_map/all_to_all | solution.py:163
  40.9 149.8 %copy-start.19 = (s32[3]{0:T(128)}, s32[3]{0:T(128)S(1)}, u32[]{:S(2)}) copy-start(s32[3]{0:T(128)S(1)} %fusion.77) | copy-start | bytes 40
  221.3 10.3 %copy-start.22 = (bf16[64,64,3,3]{1,0,3,2:T(8,128)(2,1)S(1)}, bf16[64,64,3,3]{1,0,3,2:T(8,128)(2,1)}, u32[]{:S(2)}) copy-start(bf16[64,64,3,3]{1,0,3,2:T(8,128)(2,1)} %get-tuple-element.233) | copy-start | bytes 221188 | tf_op jit(solution)/shard_map/while
  221.3 10.3 %copy-start.23 = (f32[64]{0:T(128)S(1)}, f32[64]{0:T(128)}, u32[]{:S(2)}) copy-start(f32[64]{0:T(128)} %get-tuple-element.234) | copy-start | bytes 772 | tf_op jit(solution)/shard_map/while
  221.3 10.3 %copy-start.24 = (pred[8,17]{0,1:T(8,128)(4,1)S(1)}, pred[8,17]{0,1:T(8,128)(4,1)}, u32[]{:S(2)}) copy-start(pred[8,17]{0,1:T(8,128)(4,1)} %get-tuple-element.238) | copy-start | bytes 412 | tf_op jit(solution)/shard_map/while
  231.7 12.2 %copy-start.16 = (bf16[3,64,3,3]{1,0,3,2:T(4,128)(2,1)S(1)}, bf16[3,64,3,3]{1,0,3,2:T(4,128)(2,1)}, u32[]{:S(2)}) copy-start(bf16[3,64,3,3]{1,0,3,2:T(4,128)(2,1)} %get-tuple-element.235) | copy-start | bytes 10372 | tf_op jit(solution)/shard_map/while
  357.9 10.3 %copy-start.22 = (bf16[64,64,3,3]{1,0,3,2:T(8,128)(2,1)S(1)}, bf16[64,64,3,3]{1,0,3,2:T(8,128)(2,1)}, u32[]{:S(2)}) copy-start(bf16[64,64,3,3]{1,0,3,2:T(8,128)(2,1)} %get-tuple-element.233) | copy-start | bytes 221188 | tf_op jit(solution)/shard_map/while
  357.9 10.3 %copy-start.23 = (f32[64]{0:T(128)S(1)}, f32[64]{0:T(128)}, u32[]{:S(2)}) copy-start(f32[64]{0:T(128)} %get-tuple-element.234) | copy-start | bytes 772 | tf_op jit(solution)/shard_map/while
  358.0 10.3 %copy-start.24 = (pred[8,17]{0,1:T(8,128)(4,1)S(1)}, pred[8,17]{0,1:T(8,128)(4,1)}, u32[]{:S(2)}) copy-start(pred[8,17]{0,1:T(8,128)(4,1)} %get-tuple-element.238) | copy-start | bytes 412 | tf_op jit(solution)/shard_map/while
  368.3 12.2 %copy-start.16 = (bf16[3,64,3,3]{1,0,3,2:T(4,128)(2,1)S(1)}, bf16[3,64,3,3]{1,0,3,2:T(4,128)(2,1)}, u32[]{:S(2)}) copy-start(bf16[3,64,3,3]{1,0,3,2:T(4,128)(2,1)} %get-tuple-element.235) | copy-start | bytes 10372 | tf_op jit(solution)/shard_map/while
  494.5 10.3 %copy-start.22 = (bf16[64,64,3,3]{1,0,3,2:T(8,128)(2,1)S(1)}, bf16[64,64,3,3]{1,0,3,2:T(8,128)(2,1)}, u32[]{:S(2)}) copy-start(bf16[64,64,3,3]{1,0,3,2:T(8,128)(2,1)} %get-tuple-element.233) | copy-start | bytes 221188 | tf_op jit(solution)/shard_map/while
  494.6 10.3 %copy-start.23 = (f32[64]{0:T(128)S(1)}, f32[64]{0:T(128)}, u32[]{:S(2)}) copy-start(f32[64]{0:T(128)} %get-tuple-element.234) | copy-start | bytes 772 | tf_op jit(solution)/shard_map/while
  494.6 10.3 %copy-start.24 = (pred[8,17]{0,1:T(8,128)(4,1)S(1)}, pred[8,17]{0,1:T(8,128)(4,1)}, u32[]{:S(2)}) copy-start(pred[8,17]{0,1:T(8,128)(4,1)} %get-tuple-element.238) | copy-start | bytes 412 | tf_op jit(solution)/shard_map/while
  504.9 12.2 %copy-start.16 = (bf16[3,64,3,3]{1,0,3,2:T(4,128)(2,1)S(1)}, bf16[3,64,3,3]{1,0,3,2:T(4,128)(2,1)}, u32[]{:S(2)}) copy-start(bf16[3,64,3,3]{1,0,3,2:T(4,128)(2,1)} %get-tuple-element.235) | copy-start | bytes 10372 | tf_op jit(solution)/shard_map/while
  625.4 77.0 %copy-start.18 = (pred[1,8]{1,0:T(4,128)(4,1)S(1)}, pred[1,8]{1,0:T(4,128)(4,1)}, u32[]{:S(2)}) copy-start(pred[1,8]{1,0:T(4,128)(4,1)} %copy-done.17) | copy-start | bytes 28
  625.4 75.5 %all-to-all-start.1 = ((bf16[32,3,128,128]{3,2,1,0:T(8,128)(2,1)}), bf16[32,3,128,128]{3,2,1,0:T(8,128)(2,1)S(1)}, u32[]{:S(2)}, u32[]{:S(2)}) async-start(bf16[32,3,128,128]{3,2,1,0:T(8,128)(2,1)} %scatter_fusion.1), calls=%async_computation.1 | async-start | bytes 6291456 | tf_op jit(solution)/shard_map/all_to_all | solution.py:168
  707.5 6.1 copy-start.2
  709.2 4.6 collective-permute-start.4
  711.2 5.0 collective-permute-start.5
  (9 other events, 16.8 us)
where the time goes:
time: 726 us; the launch traced here: 720 us
  matrix products  364 us (50%)
  waiting for transfers between devices  224 us (31%)
  local copies, waits for them, and re-layouts  72.1 us (10%)
  starting transfers between devices  23.2 us (3%)
  loops' own time  20.6 us (3%)
  other arithmetic  13.1 us (2%)
    conv_general_dilated x9, matrix products, convolve(): lax.conv_general_dilated(source, kernel, (1, 1), 'VALID', dimension_numbe...  364 us
    all_to_all x1, waiting for transfers between devices, body(): lax.all_to_all(outgoing, ('group', 'tile'), split_axis=0, concat_axis=0,...  146 us
    all_to_all x1, waiting for transfers between devices, body(): lax.all_to_all(returning, ('group', 'tile'), split_axis=0, concat_axis=0,...  72.2 us
    conv_general_dilated x12, local copies, waits for them, and re-layouts, convolve(): lax.conv_general_dilated(source, kernel, (1, 1), 'VALID', dimension_numbe...  42.3 us
    another operation x1, loops' own time, body(): results = lax.map(closure, arriving[senders])  20.6 us
  transfers between devices with their start and end apart: 8, of which 4 were waited for; matrix products, arithmetic and copies ran while one was open for 1% of the time, Pallas kernels for 0%

commit v1 on v0

v1 whole, which is shorter than its diff:
```python
import functools

import jax
import jax.numpy as jnp
import numpy as np
from jax import lax
from jax.experimental import pallas as pl
from jax.experimental.pallas import tpu as pltpu
from jax.sharding import PartitionSpec as P

time_step = 0.1
viscosity = 0.5
diffusivity = 0.5
eddy_gain = 0.5
coriolis_base = 0.2
coriolis_slope = 0.6

LANES = 128
PITCH = 80
HALO = 4
WIN = 8


def east_diff(field):
    return 0.5 * (field[..., 2:, 1:-1] - field[..., :-2, 1:-1])


def north_diff(field):
    return 0.5 * (field[..., 1:-1, 2:] - field[..., 1:-1, :-2])


def laplace(field):
    return (
        field[..., 2:, 1:-1]
        + field[..., :-2, 1:-1]
        + field[..., 1:-1, 2:]
        + field[..., 1:-1, :-2]
        - 4.0 * field[..., 1:-1, 1:-1]
    )


def advance(padded_east, padded_north, padded_tracer, active, coriolis):
    inner_east = padded_east[..., 1:-1, 1:-1]
    inner_north = padded_north[..., 1:-1, 1:-1]
    inner_tracer = padded_tracer[..., 1:-1, 1:-1]
    grad_east = east_diff(padded_tracer)
    grad_north = north_diff(padded_tracer)
    new_east = inner_east + time_step * active * (
        coriolis * inner_north - grad_east + viscosity * laplace(padded_east)
    )
    new_north = inner_north + time_step * active * (
        -coriolis * inner_east - grad_north + viscosity * laplace(padded_north)
    )
    new_tracer = inner_tracer + time_step * active * (
        -(inner_east * grad_east + inner_north * grad_north) + diffusivity * laplace(padded_tracer)
    )
    return (new_east, new_north, new_tracer)


def extend_rows(block, width):
    count = lax.axis_size("tile")
    forward = [(i, i + 1) for i in range(count - 1)]
    backward = [(target, source) for source, target in forward]
    low = lax.ppermute(block[:, -width:], "tile", forward)
    high = lax.ppermute(block[:, :width], "tile", backward)
    return jnp.concatenate([low, block, high], axis=1)


def operators(rows_out):
    j = np.arange(LANES)
    w = np.arange(3 * LANES)
    rows_in = rows_out + 2 * HALO
    block_rows = rows_out // 2 + 1
    split = np.concatenate([w[:, None] == (2 * j - 5 + s + LANES)[None] for s in range(4)], axis=1)
    place = np.concatenate([2 * (j - 1) + par for par in range(2)])
    mask_columns = w[:, None] == (place + LANES)[None]
    merge = (place[:, None] == j[None]).astype(np.float32)
    slope = 0.5 * eddy_gain
    north = slope * (
        (place[:, None] == j[None] + 1).astype(np.float32)
        - (place[:, None] == j[None] - 1).astype(np.float32)
    )
    padded = -(-block_rows * 8 // 16) * 16
    index = np.arange(padded)
    row = 2 * (index // 8) - 1 + (index % 8) // 4
    comp = np.where(index < block_rows * 8, index % 4, 3)
    spread = row[:, None] == (np.arange(rows_in) - HALO)[None]
    out = np.arange(rows_out)
    first, second = [], []
    for output in range(2):
        ours = (comp == output)[None]
        first.append(
            slope
            * (
                (ours & (row[None] == out[:, None] + 1)).astype(np.float32)
                - (ours & (row[None] == out[:, None] - 1)).astype(np.float32)
            )
        )
        second.append(((comp == output + 1)[None] & (row[None] == out[:, None])).astype(np.float32))
    return [
        jnp.asarray(np.asarray(table, np.float32), jnp.bfloat16)
        for table in (split, mask_columns, merge, north, spread, np.concatenate(first), np.concatenate(second))
    ]


def taps(kernel):
    return jnp.stack(
        [
            jnp.stack(
                [
                    jnp.pad(kernel.transpose(2, 3, 0, 1), ((p, 1 - p), (par, 1 - par), (0, 0), (0, 0)))
                    for par in range(2)
                ],
                axis=2,
            )
            for p in range(2)
        ],
        axis=2,
    )


def arranged_weights(conv_one, bias_one, conv_two, bias_two, conv_three, bias_three):
    hidden, inputs = conv_one.shape[:2]
    outputs = conv_three.shape[0]
    half = jnp.asarray(0.5, jnp.bfloat16)
    one = taps(conv_one * half).transpose(1, 5, 0, 2, 3, 4)
    one = jnp.pad(one, ((0, 0), (0, 0), (0, WIN - 4), (0, 0), (0, 0), (0, 0)))
    one = one.reshape(4 * inputs * WIN, 4 * hidden)
    two = taps(conv_two * half).reshape(2, 2, 2, 2, 2, 2, hidden, hidden)
    two = two.transpose(0, 2, 1, 3, 7, 4, 5, 6).reshape(16 * hidden, 4 * hidden)
    three = jnp.pad(taps(conv_three), ((0, 0),) * 4 + ((0, 4 - outputs), (0, 0)))
    three = three.reshape(2, 2, 2, 2, 2, 2, 4, hidden).transpose(0, 2, 5, 4, 6, 1, 3, 7)
    three = three.reshape(64, 4 * hidden)
    low = jnp.tile(0.5 * bias_one, 4)[None]
    mid = jnp.tile(0.5 * bias_two, 4)[None]
    high = jnp.tile(jnp.pad(bias_three, (0, 4 - outputs)), 4)[:, None]
    return one, low, two, mid, three, high


def gate(value):
    return value + value * jnp.tanh(value)


def closure_kernel(
    depth_ref,
    features_ref,
    reach_ref,
    one_ref,
    low_ref,
    two_ref,
    mid_ref,
    three_ref,
    high_ref,
    split_ref,
    mask_ref,
    merge_ref,
    north_ref,
    spread_ref,
    first_ref,
    second_ref,
    out_ref,
    parts,
    hidden,
    shifted,
    top,
    stress,
):
    levels, rows3, cols = features_ref.shape
    rows_in = rows3 // 3
    rows_out = rows_in - 2 * HALO
    tiles = cols // LANES
    block_rows = rows_out // 2 + 1
    f32 = jnp.float32
    out_ref[...] = jnp.zeros_like(out_ref)
    parts[...] = jnp.zeros_like(parts)
    top[...] = jnp.zeros_like(top)
    stress[...] = jnp.zeros_like(stress)

    def window(ref, lead, col):
        at = lambda c: ref[lead + (slice(None), pl.ds(pl.multiple_of(c * LANES, LANES), LANES))]
        here = at(col)
        zero = jnp.zeros_like(here)
        before = jnp.where(col > 0, at(jnp.maximum(col - 1, 0)), zero)
        after = jnp.where(col < tiles - 1, at(jnp.minimum(col + 1, tiles - 1)), zero)
        return jnp.concatenate([before, here, after], axis=1)

    def unit(level, col):
        source = window(features_ref, (level,), col)
        pieces = jnp.dot(source, split_ref[...], preferred_element_type=f32)
        for s in range(4):
            parts[s, 0:rows3, :] = pieces[:, s * LANES : (s + 1) * LANES]
        for block in range(block_rows + 2):
            stack = jnp.concatenate(
                [
                    parts[s, c * rows_in + 2 * block : c * rows_in + 2 * block + WIN, :]
                    for s in range(4)
                    for c in range(3)
                ],
                axis=0,
            )
            rows = stack.T[0:PITCH].astype(jnp.bfloat16)
            value = jnp.dot(rows, one_ref[...], preferred_element_type=f32) + low_ref[...]
            value = gate(value)
            hidden[block * PITCH : (block + 1) * PITCH, :] = value.astype(jnp.bfloat16)
            shifted[block * PITCH : (block + 1) * PITCH, :] = pltpu.roll(
                value, PITCH - 1, 0
            ).astype(jnp.bfloat16)
        step = 6
        for block in range(0, block_rows + 1, step):
            count = min(step, block_rows + 1 - block)
            here = slice(block * PITCH, (block + count) * PITCH)
            below = slice((block + 1) * PITCH, (block + 1 + count) * PITCH)
            rows = jnp.concatenate(
                [hidden[here, :], shifted[here, :], hidden[below, :], shifted[below, :]], axis=1
            )
            value = jnp.dot(rows, two_ref[...], preferred_element_type=f32) + mid_ref[...]
            top[here, :] = gate(value).astype(jnp.bfloat16)
        earlier = None
        for block in range(block_rows + 1):
            rows = top[block * PITCH : block * PITCH + LANES, :]
            sums = lax.dot_general(
                three_ref[...], rows, (((1,), (1,)), ((), ())), preferred_element_type=f32
            )
            if earlier is not None:
                value = (
                    earlier[0:16]
                    + sums[32:48]
                    + pltpu.roll(earlier[16:32] + sums[48:64], LANES - 1, 1)
                    + high_ref[...]
                )
                stress[(block - 1) * 8 : block * 8, 0:LANES] = value[0:8]
                stress[(block - 1) * 8 : block * 8, LANES : 2 * LANES] = value[8:16]
            earlier = sums
        reach = window(reach_ref, (), col)
        active = jnp.where(reach > level.astype(f32), 1.0, 0.0)
        wide = jnp.dot(active.astype(jnp.bfloat16), mask_ref[...], preferred_element_type=f32)
        wide = jnp.dot(spread_ref[...], wide.astype(jnp.bfloat16), preferred_element_type=f32)
        masked = jnp.where(wide > 0.5, stress[...], 0.0).astype(jnp.bfloat16)
        natural = jnp.dot(masked, merge_ref[...], preferred_element_type=f32).astype(jnp.bfloat16)
        chosen = jnp.dot(second_ref[...], masked, preferred_element_type=f32).astype(jnp.bfloat16)
        push = jnp.dot(first_ref[...], natural, preferred_element_type=f32) + jnp.dot(
            chosen, north_ref[...], preferred_element_type=f32
        )
        own = active[HALO : HALO + rows_out, LANES : 2 * LANES]
        push = push * jnp.concatenate([own, own], axis=0)
        out_ref[level, :, pl.ds(pl.multiple_of(col * LANES, LANES), LANES)] = push.astype(jnp.bfloat16)

    def visit(index, carry):
        level, col = index // tiles, index % tiles

        @pl.when(level < depth_ref[col])
        def _():
            unit(level, col)

        return carry

    lax.fori_loop(0, levels * tiles, visit, 0)


def closure(depth, features, reach, weights, tables):
    levels, rows3, cols = features.shape
    rows_in = rows3 // 3
    rows_out = rows_in - 2 * HALO
    block_rows = rows_out // 2 + 1
    width = weights[2].shape[1]
    vmem = pl.BlockSpec(memory_space=pltpu.VMEM)
    operands = (features, reach) + tuple(weights) + tuple(tables)
    return pl.pallas_call(
        closure_kernel,
        out_shape=jax.ShapeDtypeStruct((levels, 2 * rows_out, cols), jnp.bfloat16),
        in_specs=[pl.BlockSpec(memory_space=pltpu.SMEM)] + [vmem] * len(operands),
        out_specs=vmem,
        scratch_shapes=[
            pltpu.VMEM((4, rows3 + WIN, LANES), jnp.float32),
            pltpu.VMEM(((block_rows + 2) * PITCH, width), jnp.bfloat16),
            pltpu.VMEM(((block_rows + 2) * PITCH, width), jnp.bfloat16),
            pltpu.VMEM(((block_rows + 1) * PITCH + LANES, width), jnp.bfloat16),
            pltpu.VMEM((tables[4].shape[0], 2 * LANES), jnp.float32),
        ],
        compiler_params=pltpu.CompilerParams(vmem_limit_bytes=48 * 1024 * 1024),
        name="closure",
    )(depth, *operands)


def body(
    velocity_u,
    velocity_v,
    tracer,
    land,
    tile_depth,
    conv_one,
    bias_one,
    conv_two,
    bias_two,
    conv_three,
    bias_three,
):
    levels_here, rows, cols = velocity_u.shape
    across = cols // rows
    group_index = lax.axis_index("group")
    tile_index = lax.axis_index("tile")
    group_count = lax.axis_size("group")
    tile_count = lax.axis_size("tile")
    total_rows = rows * tile_count
    share = rows // group_count
    edge = HALO + 1
    depth_grid = tile_depth.reshape(tile_count, across)
    my_depth = lax.dynamic_index_in_dim(depth_grid, tile_index, 0, keepdims=False)
    reach_here = jnp.where(land == 1, jnp.repeat(my_depth, rows)[None], 0).astype(jnp.float32)
    stacked = jnp.concatenate([velocity_u, velocity_v, tracer, reach_here[None]], axis=0)
    extended = extend_rows(stacked, edge)
    reach = extended[-1]
    fields = extended[:-1].reshape(3, levels_here, rows + 2 * edge, cols)
    fields = jnp.pad(fields, ((0, 0), (0, 0), (0, 0), (1, 1)))
    my_levels = (group_index * levels_here + jnp.arange(levels_here, dtype=jnp.int32)).astype(jnp.float32)
    active = (my_levels[:, None, None] < reach[None, 1:-1]).astype(jnp.float32)
    places = (tile_index * rows - HALO + jnp.arange(rows + 2 * HALO, dtype=jnp.int32)).astype(jnp.float32)
    coriolis = (coriolis_base + coriolis_slope * (places + 0.5) / total_rows)[:, None]
    east, north, new_tracer = advance(fields[0], fields[1], fields[2], active, coriolis)
    features = (jnp.stack([east, north, new_tracer], axis=1) * active[:, None]).astype(jnp.bfloat16)
    shares = jnp.stack(
        [features[:, :, q * share : (q + 1) * share + 2 * HALO] for q in range(group_count)]
    )
    shares = shares.reshape(group_count, levels_here, 3 * (share + 2 * HALO), cols)
    arriving = lax.all_to_all(shares, "group", split_axis=0, concat_axis=0, tiled=True)
    arriving = arriving.reshape((group_count * levels_here,) + arriving.shape[2:])
    my_reach = lax.dynamic_slice_in_dim(reach, group_index * share + 1, share + 2 * HALO, 0)
    weights = arranged_weights(conv_one, bias_one, conv_two, bias_two, conv_three, bias_three)
    push = closure(my_depth, arriving, my_reach, weights, operators(share))
    push = push.reshape(group_count, levels_here, 2, share, cols)
    landed = lax.all_to_all(push, "group", split_axis=0, concat_axis=0, tiled=True)
    added = landed.transpose(2, 1, 0, 3, 4).reshape(2, levels_here, rows, cols).astype(jnp.float32)
    inner = slice(HALO, HALO + rows)
    return (east[:, inner] + added[0], north[:, inner] + added[1], new_tracer[:, inner])


def solution(mesh):
    field = P("group", "tile", None)
    in_specs = (field, field, field, P("tile", None)) + (P(),) * 7
    return jax.shard_map(
        body, mesh=mesh, in_specs=in_specs, out_specs=(field,) * 3, check_vma=False
    )
```

time: 726 us -> 92.2 us (0.13)
  the two profiles are of different devices: /device:TPU:1 before, /device:TPU:9 now
where the time goes in v1:
time: 92.2 us; the launch traced here: 92.8 us
  Pallas kernels  44.9 us (49%)
  other arithmetic  13.9 us (15%)
  local copies, waits for them, and re-layouts  13 us (14%)
  starting transfers between devices  12.8 us (14%)
  waiting for transfers between devices  7.07 us (8%)
  between operations  1.13 us (1%)
    pallas_call x1, Pallas kernels, closure(): pl.pallas_call(closure_kernel, out_shape=jax.ShapeDtypeStruct((levels, 2...  44.9 us
    transpose x1, other arithmetic, arranged_weights(): two = two.transpose(0, 2, 1, 3, 7, 4, 5, 6).reshape(16 * hidden, 4 * hidden)  5.29 us
    another operation x6, local copies, waits for them, and re-layouts, taps(): jnp.stack([jnp.pad(kernel.transpose(2, 3, 0, 1), ((p, 1 - p), (par, 1 - p...  4.06 us
    ppermute x1, starting transfers between devices, extend_rows(): low = lax.ppermute(block[:, -width:], 'tile', forward)  3.77 us
    all_to_all x1, starting transfers between devices, body(): lax.all_to_all(push, 'group', split_axis=0, concat_axis=0, tiled=True)  3.63 us
    all_to_all x1, waiting for transfers between devices, body(): lax.all_to_all(push, 'group', split_axis=0, concat_axis=0, tiled=True)  3.58 us
    all_to_all x1, starting transfers between devices, body(): lax.all_to_all(shares, 'group', split_axis=0, concat_axis=0, tiled=True)  3.51 us
    ppermute x1, waiting for transfers between devices, extend_rows(): high = lax.ppermute(block[:, :width], 'tile', backward)  3.48 us
  transfers between devices with their start and end apart: 4, of which 2 were waited for; matrix products, arithmetic and copies ran while one was open for 17% of the time, Pallas kernels for 0%

profile of v1, /device:TPU:9, one launch (start us, length us, event | category | flops | bytes accessed | tf_op | source)
XLA Modules:
  0.0 92.8 jit_solution(10654899203706297531)
XLA Ops:
  0.7 0.8 reshape.163
  1.5 1.2 %convert_bitcast_fusion.2 = f32[1,128,1024]{2,1,0:T(8,128)S(1)} fusion(s32[128,1024]{1,0:T(8,128)} %param.21, s32[1024]{0:T(1024)S(1)} %broadcast_bitcast_fusion), kind=kLoop, calls=%fused_computation.43 | loop fusion | flops 393216 | bytes 1052672 | tf_op jit(solution)/shard_map/broadcast_in_dim | solution.py:310
  2.8 0.9 pad_maximum_fusion.5
  3.6 3.8 %collective-permute-start = (f32[4,5,1024]{2,1,0:T(8,128)S(1)}, f32[4,5,1024]{2,1,0:T(8,128)S(1)}, u32[]{:S(2)}, u32[]{:S(2)}) collective-permute-start(f32[4,5,1024]{2,1,0:T(8,128)S(1)} %get-tuple-element.7), channel_id=1, source_target_pairs={{0,1},{1,2},{2,3},{3,4},{4,5},{5,6},{6,7},{8,9},{9,10},{10,11},{11... | collective-permute-start | bytes 245768 | tf_op jit(solution)/shard_map/ppermute | solution.py:64
  7.4 1.9 %collective-permute-start.1 = (f32[4,5,1024]{2,1,0:T(8,128)S(1)}, f32[4,5,1024]{2,1,0:T(8,128)S(1)}, u32[]{:S(2)}, u32[]{:S(2)}) collective-permute-start(f32[4,5,1024]{2,1,0:T(8,128)S(1)} %get-tuple-element.8), channel_id=1, source_target_pairs={{1,0},{2,1},{3,2},{4,3},{5,4},{6,5},{7,6},{9,8},{10,9},{11,10},{12... | collective-permute-start | bytes 245768 | tf_op jit(solution)/shard_map/ppermute | solution.py:65
  9.9 0.1 reshape.166.one_ref
  10.2 3.5 %collective-permute-done.1 = f32[4,5,1024]{2,1,0:T(8,128)S(1)} collective-permute-done((f32[4,5,1024]{2,1,0:T(8,128)S(1)}, f32[4,5,1024]{2,1,0:T(8,128)S(1)}, u32[]{:S(2)}, u32[]{:S(2)}) %collective-permute-start.1) | collective-permute-done | bytes 81952 | tf_op jit(solution)/shard_map/ppermute | solution.py:65
  13.7 0.3 pad_maximum_fusion
  14.0 0.2 slice_bitcast_fusion
  14.2 0.6 fusion.1
  14.8 0.1 convert_bitcast_fusion.1
  15.0 1.0 %fusion.5 = f32[1,136,1024]{2,1,0:T(8,128)S(1)} fusion(pred[1,136,1024]{2,1,0:T(8,128)(4,1)S(1)} %get-tuple-element.4, f32[1,138,1026]{2,1,0:T(8,128)S(1)} %get-tuple-element.10, f32[1,138,1026]{2,1,0:T(8,128)S(1)} %get-tuple-element.11, f32[1,138,1026]{2,1,0:T(8,128)S(1)} %get-tuple-element.9, f32[136]{0:T(256)S(1)} %get-tuple-element.31), kind=kLoop, calls=%fused_computation.23 | loop fusion | flops 1949696 | bytes 5153312 | tf_op jit(solution)/shard_map/add | solution.py:51
  16.0 1.5 %fusion.4 = (f32[1,136,1024]{2,1,0:T(8,128)S(1)}, f32[1,136,1024]{2,1,0:T(8,128)S(1)}) fusion(pred[1,136,1024]{2,1,0:T(8,128)(4,1)S(1)} %get-tuple-element.4, f32[1,138,1026]{2,1,0:T(8,128)S(1)} %get-tuple-element.9, f32[1,138,1026]{2,1,0:T(8,128)S(1)} %get-tuple-element.11, f32[1,138,1026]{2,1,0:T(8,128)S(1)} %get-tuple-element.10, f32[136]{0:T(256)S(1)} %get-tuple-element.30), kind=kLoop, calls=%fused_computation.22 | loop fusion | flops 4038656 | bytes 7381536 | tf_op jit(solution)/shard_map/add | solution.py:48
  17.5 0.2 fusion
  17.9 0.4 copy-done.10
  18.3 0.2 copy-done.12
  18.5 1.1 %pad_maximum_fusion.1 = bf16[4,1,120,1024]{3,2,1,0:T(8,128)(2,1)} fusion(bf16[1,1,120,1024]{3,2,1,0:T(8,128)(2,1)S(1)} %bitcast.85, bf16[1,1,120,1024]{3,2,1,0:T(8,128)(2,1)S(1)} %bitcast.86, bf16[1,1,120,1024]{3,2,1,0:T(8,128)(2,1)S(1)} %bitcast.87, bf16[1,1,120,1024]{3,2,1,0:T(8,128)(2,1)S(1)} %bitcast.84), kind=kLoop, calls=%fused_computation.9 | loop fusion | flops 1474560 | bytes 1966080 | tf_op jit(solution)/shard_map/stack | solution.py:321
  19.6 3.5 %all-to-all-start = ((bf16[4,1,120,1024]{3,2,1,0:T(8,128)(2,1)}), bf16[4,1,120,1024]{3,2,1,0:T(8,128)(2,1)S(1)}, u32[]{:S(2)}, u32[]{:S(2)}) async-start(bf16[4,1,120,1024]{3,2,1,0:T(8,128)(2,1)} %pad_maximum_fusion.1), calls=%async_computation | async-start | bytes 1966080 | tf_op jit(solution)/shard_map/all_to_all | solution.py:325
  23.2 0.1 reshape.169.three_ref
  23.3 1.0 %fusion.26 = (bf16[4,4,64,64]{3,2,1,0:T(8,128)(2,1)S(1)}, bf16[4,4,64,64]{3,2,1,0:T(8,128)(2,1)S(1)}, bf16[4,4,64,64]{3,2,1,0:T(8,128)(2,1)}, bf16[4,4,64,64]{3,2,1,0:T(8,128)(2,1)}) fusion(bf16[3,3,64,64]{3,2,1,0:T(8,128)(2,1)S(1)} %multiply_bitcast_fusion), kind=kLoop, calls=%fused_computation.83 | loop fusion | bytes 598016 | tf_op jit(solution)/shard_map/jit(_pad)/pad | solution.py:111
  24.3 0.4 copy.32
  24.7 0.4 copy.29
  25.1 1.3 %copy.31 = bf16[2,2,2,2,1,1,64,64]{6,5,4,7,3,1,2,0:T(2,128)(2,1)S(1)} copy(bf16[2,2,2,2,1,1,64,64]{7,6,3,2,1,0,5,4:T(8,128)(2,1)} %bitcast.81) | data formatting | bytes 262144 | tf_op jit(solution)/shard_map/stack | solution.py:109
  26.4 2.0 %copy.30 = bf16[2,2,2,2,1,1,64,64]{6,5,4,7,3,1,2,0:T(2,128)(2,1)} copy(bf16[2,2,2,2,1,1,64,64]{7,6,3,2,1,0,5,4:T(8,128)(2,1)} %bitcast.80) | data formatting | bytes 262144 | tf_op jit(solution)/shard_map/stack | solution.py:109
  28.4 5.3 %maximum_bitcast_fusion = bf16[2,2,2,2,64,2,2,64]{7,6,5,4,3,2,1,0:T(2,128)(2,1)} fusion(bf16[2,2,2,2,1,1,64,64]{6,5,4,7,3,1,2,0:T(2,128)(2,1)S(1)} %copy.32, bf16[2,2,2,2,1,1,64,64]{6,5,4,7,3,1,2,0:T(2,128)(2,1)S(1)} %copy.31, bf16[2,2,2,2,1,1,64,64]{6,5,4,7,3,1,2,0:T(2,128)(2,1)} %copy.30, bf16[2,2,2,2,1,1,64,64]{6,5,4,7,3,1,2,0:T(2,128)(2,1)S(1)} %copy.29), kind=kLoop, calls=%fused_computation.7 | loop fusion | flops 2097152 | bytes 1048576 | tf_op jit(solution)/shard_map/transpose | solution.py:130
  33.7 2.8 %reshape.167.two_ref = bf16[1024,256]{1,0:T(8,128)(2,1)S(1)} reshape(bf16[2,2,2,2,64,2,2,64]{7,6,5,4,3,2,1,0:T(2,128)(2,1)} %maximum_bitcast_fusion) | data formatting | bytes 1048576 | tf_op jit(solution)/shard_map/reshape | solution.py:130
  36.7 44.9 %closure.1 = bf16[4,64,1024]{2,1,0:T(8,128)(2,1)} custom-call(s32[8]{0:T(128)S(1)} %fusion.22.depth_ref, bf16[4,120,1024]{2,1,0:T(8,128)(2,1)S(1)} %bitcast.74, f32[40,1024]{1,0:T(8,128)S(1)} %fusion.18.reach_ref, bf16[96,256]{1,0:T(8,128)(2,1)S(1)} %reshape.166.one_ref, f32[1,256]{1,0:T(1,128)S(1)} %broadcast_in_dim_tile.9.low_ref, ...), custom_call_target="tpu_custom_call" | custom-call | tf_op jit(solution)/shard_map/closure/pallas_call | solution.py:268
  81.6 3.6 %all-to-all-start.1 = ((bf16[4,1,2,32,1024]{4,3,2,1,0:T(8,128)(2,1)}), bf16[4,1,2,32,1024]{4,3,2,1,0:T(8,128)(2,1)S(1)}, u32[]{:S(2)}, u32[]{:S(2)}) async-start(bf16[4,1,2,32,1024]{4,3,2,1,0:T(8,128)(2,1)} %bitcast.41), calls=%async_computation.1 | async-start | bytes 1048576 | tf_op jit(solution)/shard_map/all_to_all | solution.py:331
  85.3 1.9 %slice.163 = f32[1,128,1024]{2,1,0:T(8,128)} slice(f32[1,136,1024]{2,1,0:T(8,128)} %copy-done.12), slice={[0:1], [4:132], [0:1024]} | slice | bytes 1048576 | tf_op jit(solution)/shard_map/slice | solution.py:334
  87.2 3.6 %all-to-all-done.1 = bf16[4,1,2,32,1024]{4,3,2,1,0:T(8,128)(2,1)S(1)} async-done(((bf16[4,1,2,32,1024]{4,3,2,1,0:T(8,128)(2,1)}), bf16[4,1,2,32,1024]{4,3,2,1,0:T(8,128)(2,1)S(1)}, u32[]{:S(2)}, u32[]{:S(2)}) %all-to-all-start.1) | async-done | bytes 524320 | tf_op jit(solution)/shard_map/all_to_all | solution.py:331
  91.0 0.9 slice_add_fusion.6
  91.9 0.9 slice_add_fusion.7
  (69 shorter events, 1.3 us)
Async XLA Ops:
  0.6 8.7 %copy-start.18 = (f32[64]{0:T(128)S(1)}, f32[64]{0:T(128)}, u32[]{:S(2)}) copy-start(f32[64]{0:T(128)} %param.24) | copy-start | bytes 772
  0.6 8.7 %copy-start.19 = (f32[64]{0:T(128)S(1)}, f32[64]{0:T(128)}, u32[]{:S(2)}) copy-start(f32[64]{0:T(128)} %param.26) | copy-start | bytes 772
  0.7 8.9 %copy-start.20 = (f32[3]{0:T(128)S(1)}, f32[3]{0:T(128)}, u32[]{:S(2)}) copy-start(f32[3]{0:T(128)} %param.28) | copy-start | bytes 40
  0.7 9.0 %copy-start.17 = (bf16[64,3,3,3]{0,3,2,1:T(4,128)(2,1)S(1)}, bf16[64,3,3,3]{0,3,2,1:T(4,128)(2,1)}, u32[]{:S(2)}) copy-start(bf16[64,3,3,3]{0,3,2,1:T(4,128)(2,1)} %param.23) | copy-start | bytes 10372
  0.7 9.4 %copy-start.16 = (bf16[3,64,3,3]{1,3,2,0:T(4,128)(2,1)S(1)}, bf16[3,64,3,3]{1,3,2,0:T(4,128)(2,1)}, u32[]{:S(2)}) copy-start(bf16[3,64,3,3]{1,3,2,0:T(4,128)(2,1)} %param.27) | copy-start | bytes 10372
  1.5 8.6 %copy-start.15 = (bf16[64,64,3,3]{1,0,3,2:T(8,128)(2,1)S(1)}, bf16[64,64,3,3]{1,0,3,2:T(8,128)(2,1)}, u32[]{:S(2)}) copy-start(bf16[64,64,3,3]{1,0,3,2:T(8,128)(2,1)} %param.25) | copy-start | bytes 221188
  1.5 12.2 %copy-start.7 = (f32[1,128,1024]{2,1,0:T(8,128)S(1)}, f32[1,128,1024]{2,1,0:T(8,128)}, u32[]{:S(2)}) copy-start(f32[1,128,1024]{2,1,0:T(8,128)} %param.20) | copy-start | bytes 1572868
  1.5 12.2 %copy-start.8 = (f32[1,128,1024]{2,1,0:T(8,128)S(1)}, f32[1,128,1024]{2,1,0:T(8,128)}, u32[]{:S(2)}) copy-start(f32[1,128,1024]{2,1,0:T(8,128)} %param.19) | copy-start | bytes 1572868
  1.5 12.2 %copy-start.9 = (f32[1,128,1024]{2,1,0:T(8,128)S(1)}, f32[1,128,1024]{2,1,0:T(8,128)}, u32[]{:S(2)}) copy-start(f32[1,128,1024]{2,1,0:T(8,128)} %param.18) | copy-start | bytes 1572868
  3.6 6.6 %collective-permute-start = (f32[4,5,1024]{2,1,0:T(8,128)S(1)}, f32[4,5,1024]{2,1,0:T(8,128)S(1)}, u32[]{:S(2)}, u32[]{:S(2)}) collective-permute-start(f32[4,5,1024]{2,1,0:T(8,128)S(1)} %get-tuple-element.7), channel_id=1, source_target_pairs={{0,1},{1,2},{2,3},{3,4},{4,5},{5,6},{6,7},{8,9},{9,10},{10,11},{11... | collective-permute-start | bytes 245768 | tf_op jit(solution)/shard_map/ppermute | solution.py:64
  7.4 6.3 %collective-permute-start.1 = (f32[4,5,1024]{2,1,0:T(8,128)S(1)}, f32[4,5,1024]{2,1,0:T(8,128)S(1)}, u32[]{:S(2)}, u32[]{:S(2)}) collective-permute-start(f32[4,5,1024]{2,1,0:T(8,128)S(1)} %get-tuple-element.8), channel_id=1, source_target_pairs={{1,0},{2,1},{3,2},{4,3},{5,4},{6,5},{7,6},{9,8},{10,9},{11,10},{12... | collective-permute-start | bytes 245768 | tf_op jit(solution)/shard_map/ppermute | solution.py:65
  16.0 1.5 %copy-start.13 = (f32[1,136,1024]{2,1,0:T(8,128)}, f32[1,136,1024]{2,1,0:T(8,128)S(1)}, u32[]{:S(2)}) copy-start(f32[1,136,1024]{2,1,0:T(8,128)S(1)} %fusion.5) | copy-start | bytes 1671172
  17.5 0.8 copy-start.10
  17.5 1.0 %copy-start.12 = (f32[1,136,1024]{2,1,0:T(8,128)}, f32[1,136,1024]{2,1,0:T(8,128)S(1)}, u32[]{:S(2)}) copy-start(f32[1,136,1024]{2,1,0:T(8,128)S(1)} %get-tuple-element.6) | copy-start | bytes 1671172
  19.6 17.1 %all-to-all-start = ((bf16[4,1,120,1024]{3,2,1,0:T(8,128)(2,1)}), bf16[4,1,120,1024]{3,2,1,0:T(8,128)(2,1)S(1)}, u32[]{:S(2)}, u32[]{:S(2)}) async-start(bf16[4,1,120,1024]{3,2,1,0:T(8,128)(2,1)} %pad_maximum_fusion.1), calls=%async_computation | async-start | bytes 1966080 | tf_op jit(solution)/shard_map/all_to_all | solution.py:325
  33.7 3.0 %copy-start = (bf16[384,512]{1,0:T(8,128)(2,1)S(1)}, bf16[384,512]{1,0:T(8,128)(2,1)}, u32[]{:S(2)}) copy-start(bf16[384,512]{1,0:T(8,128)(2,1)} %constant.67.clone.split_ref) | copy-start | bytes 1179652
  33.7 3.0 %copy-start.1 = (bf16[384,256]{1,0:T(8,128)(2,1)S(1)}, bf16[384,256]{1,0:T(8,128)(2,1)}, u32[]{:S(2)}) copy-start(bf16[384,256]{1,0:T(8,128)(2,1)} %constant.68.clone.mask_ref) | copy-start | bytes 589828
  33.7 3.0 %copy-start.2 = (bf16[256,128]{1,0:T(8,128)(2,1)S(1)}, bf16[256,128]{1,0:T(8,128)(2,1)}, u32[]{:S(2)}) copy-start(bf16[256,128]{1,0:T(8,128)(2,1)} %constant.70.clone.north_ref) | copy-start | bytes 196612
  33.7 3.0 %copy-start.3 = (bf16[256,128]{1,0:T(8,128)(2,1)S(1)}, bf16[256,128]{1,0:T(8,128)(2,1)}, u32[]{:S(2)}) copy-start(bf16[256,128]{1,0:T(8,128)(2,1)} %constant.69.clone.merge_ref) | copy-start | bytes 196612
  33.7 3.0 %copy-start.4 = (bf16[144,40]{1,0:T(8,128)(2,1)S(1)}, bf16[144,40]{1,0:T(8,128)(2,1)}, u32[]{:S(2)}) copy-start(bf16[144,40]{1,0:T(8,128)(2,1)} %constant.71.clone.spread_ref) | copy-start | bytes 34564
  33.7 3.0 %copy-start.5 = (bf16[64,144]{1,0:T(8,128)(2,1)S(1)}, bf16[64,144]{1,0:T(8,128)(2,1)}, u32[]{:S(2)}) copy-start(bf16[64,144]{1,0:T(8,128)(2,1)} %constant.73.clone.second_ref) | copy-start | bytes 55300
  33.7 3.0 %copy-start.6 = (bf16[64,144]{1,0:T(8,128)(2,1)S(1)}, bf16[64,144]{1,0:T(8,128)(2,1)}, u32[]{:S(2)}) copy-start(bf16[64,144]{1,0:T(8,128)(2,1)} %constant.72.clone.first_ref) | copy-start | bytes 55300
  81.6 9.1 %all-to-all-start.1 = ((bf16[4,1,2,32,1024]{4,3,2,1,0:T(8,128)(2,1)}), bf16[4,1,2,32,1024]{4,3,2,1,0:T(8,128)(2,1)S(1)}, u32[]{:S(2)}, u32[]{:S(2)}) async-start(bf16[4,1,2,32,1024]{4,3,2,1,0:T(8,128)(2,1)} %bitcast.41), calls=%async_computation.1 | async-start | bytes 1048576 | tf_op jit(solution)/shard_map/all_to_all | solution.py:331
  87.2 3.8 %copy-start.14 = (f32[1,136,1024]{2,1,0:T(8,128)S(1)}, f32[1,136,1024]{2,1,0:T(8,128)}, u32[]{:S(2)}) copy-start(f32[1,136,1024]{2,1,0:T(8,128)} %copy-done.13) | copy-start | bytes 1671172
  90.9 1.1 %copy-start.11 = (f32[1,136,1024]{2,1,0:T(8,128)S(1)}, f32[1,136,1024]{2,1,0:T(8,128)}, u32[]{:S(2)}) copy-start(f32[1,136,1024]{2,1,0:T(8,128)} %copy-done.10) | copy-start | bytes 1671172

commit v2 on v0

v2 whole, which is shorter than its diff:
```python
import jax
import jax.numpy as jnp
import numpy as np
from jax import lax
from jax.experimental import pallas as pl
from jax.experimental.pallas import tpu as pltpu
from jax.sharding import PartitionSpec as P

time_step = 0.1
viscosity = 0.5
diffusivity = 0.5
eddy_gain = 0.5
coriolis_base = 0.2
coriolis_slope = 0.6

LANES = 128
STRIPS = 16
HALO = 4
PAD = 16
LEAD = 8


def taps(kernel):
    return jnp.stack(
        [
            jnp.stack(
                [
                    jnp.pad(kernel.transpose(2, 3, 0, 1), ((p, 1 - p), (par, 1 - par), (0, 0), (0, 0)))
                    for par in range(2)
                ],
                axis=2,
            )
            for p in range(2)
        ],
        axis=2,
    )


def arranged_weights(conv_one, bias_one, conv_two, bias_two, conv_three, bias_three):
    hidden, inputs = conv_one.shape[:2]
    outputs = conv_three.shape[0]
    half = jnp.asarray(0.5, jnp.bfloat16)
    one = taps(conv_one * half).transpose(5, 1, 0, 2, 3, 4).reshape(16 * inputs, 4 * hidden)
    one = jnp.pad(one, ((0, LANES - one.shape[0]), (0, 0)))
    two = (conv_two * half).transpose(2, 3, 1, 0)
    two = jnp.concatenate(
        [jnp.pad(two, ((0, 0), (par, 1 - par), (0, 0), (0, 0))) for par in range(2)], axis=3
    )
    three = jnp.pad(taps(conv_three), ((0, 0),) * 4 + ((0, 4 - outputs), (0, 0)))
    three = three.reshape(2, 2, 2, 2, 2, 2, 4, hidden).transpose(0, 2, 5, 4, 6, 1, 3, 7)
    three = three.reshape(64, 4 * hidden)
    low = jnp.tile(0.5 * bias_one, 4)[None]
    mid = jnp.tile(0.5 * bias_two, 4)[None]
    high = jnp.tile(jnp.pad(bias_three, (0, 4 - outputs)), 4)[:, None]
    return one, low, two, mid, three, high


def tables(cols):
    w, lane = np.arange(3 * LANES), np.arange(LANES)
    split = np.concatenate([w[:, None] == (2 * lane - 3 + s + LANES)[None] for s in range(4)], axis=1)
    groups = cols // 2 // STRIPS
    index = np.arange(cols)
    par, rest = index // (cols // 2), index % (cols // 2)
    place = 2 * (groups * (rest % STRIPS) + rest // STRIPS) + par
    merge = place[:, None] == index[None]
    return [jnp.asarray(np.asarray(t, np.float32), jnp.bfloat16) for t in (split, merge)]


def gate(value):
    return value + value * jnp.tanh(value)


def step_kernel(
    depth_ref,
    where_ref,
    east_ref,
    north_ref,
    tracer_ref,
    land_ref,
    upper_ref,
    lower_ref,
    one_ref,
    low_ref,
    taps_ref,
    mid_ref,
    three_ref,
    high_ref,
    split_ref,
    merge_ref,
    out_east,
    out_north,
    out_tracer,
    fields,
    sheet,
    depths,
    parts,
    turned,
    ready,
    two,
    hidden,
    top,
    sums,
    stress,
    natural,
):
    levels_here, rows, cols = east_ref.shape
    edge = upper_ref.shape[1]
    f32, bf16 = jnp.float32, jnp.bfloat16
    groups = cols // 2 // STRIPS
    half = cols // 2
    rows_one, rows_two = (groups + 2) * STRIPS, (groups + 1) * STRIPS
    pitch = sheet.shape[0] // 3
    windows = -(-(half + 2) // LANES)
    turns = (rows + 4) // 4
    lane = lax.broadcasted_iota(jnp.int32, (8, cols), 1)
    sub = lax.broadcasted_iota(jnp.int32, (8, LANES), 0)

    channels = taps_ref.shape[2]
    for k in range(16):
        by, bx, py, px = k // 8, k // 4 % 2, k // 2 % 2, k % 2
        for p in range(2):
            tap = 2 * by + py - p
            at = (slice(k * channels, (k + 1) * channels), slice(p * LANES, (p + 1) * LANES))
            two[at] = taps_ref[tap, 2 * bx + px] if 0 <= tap < 3 else jnp.zeros((channels, LANES), bf16)
    parts[...] = jnp.zeros_like(parts)
    turned[...] = jnp.zeros_like(turned)
    sheet[...] = jnp.zeros_like(sheet)
    sums[...] = jnp.zeros_like(sums)
    top[...] = jnp.zeros_like(top)

    for tile in range(cols // LANES):
        depths[:, tile * LANES : (tile + 1) * LANES] = jnp.full(
            (8, LANES), depth_ref[tile * LANES // rows], jnp.int32
        ).astype(f32)

    def frame(slot, source, inner):
        fields[slot, 0:PAD, :] = jnp.zeros((PAD, cols), f32)
        fields[slot, PAD + rows :, :] = jnp.zeros((PAD, cols), f32)
        fields[slot, PAD - edge : PAD, :] = upper_ref[source]
        fields[slot, PAD + rows : PAD + rows + edge, :] = lower_ref[source]
        for r in range(0, rows, 8):
            fields[slot, PAD + r : PAD + r + 8, :] = inner(r)

    frame(3, 3 * levels_here, lambda r: jnp.where(land_ref[r : r + 8, :] == 1, depths[...], 0.0))

    def sideways(value):
        left = jnp.where(lane > 0, pltpu.roll(value, 1, 1), 0.0)
        right = jnp.where(lane < cols - 1, pltpu.roll(value, cols - 1, 1), 0.0)
        return left, right

    def wet(number, at):
        return jnp.where(number < fields[3, at : at + 8, :], 1.0, 0.0)

    def advance(level, number):
        for f, ref in enumerate((east_ref, north_ref, tracer_ref)):
            frame(f, f * levels_here + level, lambda r: ref[level, r : r + 8, :])
        saved = [None] * 3
        for start in range(-8, rows + 8, 8):
            at = start + PAD

            def around(slot):
                here = fields[slot, at : at + 8, :]
                return (here, fields[slot, at - 1 : at + 7, :], fields[slot, at + 1 : at + 9, :]) + sideways(here)

            def curvature(a):
                return a[2] + a[1] + a[4] + a[3] - 4.0 * a[0]

            east, north, tracer = around(0), around(1), around(2)
            active = wet(number, at)
            row = where_ref[1] + start + lax.broadcasted_iota(jnp.int32, (8, cols), 0)
            coriolis = coriolis_base + coriolis_slope * (row.astype(f32) + 0.5) / where_ref[2].astype(f32)
            grad_east = 0.5 * (tracer[2] - tracer[1])
            grad_north = 0.5 * (tracer[4] - tracer[3])
            rate = time_step * active
            news = (
                east[0] + rate * (coriolis * north[0] - grad_east + viscosity * curvature(east)),
                north[0] + rate * (-coriolis * east[0] - grad_north + viscosity * curvature(north)),
                tracer[0]
                + rate * (-(east[0] * grad_east + north[0] * grad_north) + diffusivity * curvature(tracer)),
            )
            for f, (new, out) in enumerate(zip(news, (out_east, out_north, out_tracer), strict=True)):
                if 0 <= start < rows:
                    out[level, start : start + 8, :] = new
                new = new * active
                first, last = max(start, -HALO), min(start + 8, rows + HALO)
                sheet[f * pitch + first + HALO : f * pitch + last + HALO, LANES : LANES + cols] = new[
                    first - start : last - start
                ]

    def split_columns():
        for m in range(windows):
            source = sheet[:, 2 * m * LANES : (2 * m + 3) * LANES].astype(bf16)
            pieces = jnp.dot(source, split_ref[...], preferred_element_type=f32)
            for s in range(4):
                parts[s, m, LEAD : LEAD + 3 * pitch, :] = pieces[:, s * LANES : (s + 1) * LANES]

    def prepare(slot, base, offset):
        for m in range(windows):
            at = lambda s, first: parts[s, m, pl.ds(base + first, 8), :]
            stack = jnp.concatenate(
                [
                    jnp.where(
                        sub < 4,
                        at(s, LEAD + c * pitch + offset),
                        at(s + 1, LEAD + c * pitch + offset - 4),
                    )
                    for c in range(3)
                    for s in (0, 2)
                ],
                axis=0,
            )
            turned[slot, m * LANES : (m + 1) * LANES, 0:48] = stack.T
        for t in range(groups + 2):
            ready[slot, t * STRIPS : (t + 1) * STRIPS, :] = turned[slot, pl.ds(t, STRIPS, groups), :].astype(bf16)

    def layer_one(slot, target):
        value = jnp.dot(ready[slot], one_ref[...], preferred_element_type=f32)
        hidden[target] = gate(value + low_ref[...]).astype(bf16)

    def layer_two(slot):
        gathered = jnp.concatenate(
            [hidden[slot + by, bx * STRIPS : bx * STRIPS + rows_two, :] for by in range(2) for bx in range(2)],
            axis=1,
        )
        value = jnp.dot(gathered, two[...], preferred_element_type=f32)
        top[slot, 0:rows_two, :] = gate(value + mid_ref[...]).astype(bf16)

    def layer_three(slot, base, offset):
        new = lax.dot_general(
            three_ref[...], top[slot], (((1,), (1,)), ((), ())), preferred_element_type=f32
        )
        old = sums[...]
        wide = pltpu.roll(old[16:32] + new[48:64], new.shape[1] - STRIPS, 1)
        value = old[0:16, 0:half] + new[32:48, 0:half] + wide[:, 0:half] + high_ref[...]
        stress[pl.ds(base + offset, 8), 0:half] = value[0:8]
        stress[pl.ds(base + offset, 8), half:cols] = value[8:16]
        sums[...] = new

    def finish(level, number):
        merged = jnp.dot(stress[24:, :].astype(bf16), merge_ref[...], preferred_element_type=f32)
        for tile in range(cols // LANES):
            natural[tile] = merged[:, tile * LANES : (tile + 1) * LANES]

        def field(start, shift, comp):
            at = pl.ds(4 * (start + 1 + shift) + comp, 8, 4)
            value = jnp.concatenate([natural[tile, at, :] for tile in range(cols // LANES)], axis=1)
            return value * wet(number, start + PAD + shift)

        for start in range(0, rows, 8):
            rate = eddy_gain * wet(number, start + PAD)
            east_left, east_right = sideways(field(start, 0, 1))
            north_left, north_right = sideways(field(start, 0, 2))
            push_east = 0.5 * (field(start, 1, 0) - field(start, -1, 0)) + 0.5 * (east_right - east_left)
            push_north = 0.5 * (field(start, 1, 1) - field(start, -1, 1)) + 0.5 * (north_right - north_left)
            out_east[level, start : start + 8, :] += rate * push_east
            out_north[level, start : start + 8, :] += rate * push_north

    for level in range(levels_here):
        number = (where_ref[0] + level).astype(f32)
        advance(level, number)
        split_columns()
        for slot in range(3):
            prepare(slot % 2, 0, 2 * slot)
            layer_one(slot % 2, slot)
        prepare(0, 0, 6)
        prepare(1, 0, 8)

        def turn(k, carry):
            layer_three(0, pl.multiple_of(16 * k, 16), 0)
            layer_three(1, pl.multiple_of(16 * k, 16), 8)
            layer_two(0)
            layer_two(1)
            hidden[0] = hidden[2]
            layer_one(0, 1)
            layer_one(1, 2)
            prepare(0, 4 * k, 10)
            prepare(1, 4 * k, 12)
            return carry

        lax.fori_loop(0, turns, turn, 0)
        layer_three(0, 16 * turns, 0)
        layer_three(1, 16 * turns, 8)
        finish(level, number)


def ocean_step(depth, where, fields, land, upper, lower, weights):
    levels_here, rows, cols = fields[0].shape
    width = weights[1].shape[1]
    half = cols // 2
    groups = half // STRIPS
    windows = -(-(half + 2) // LANES)
    turns = (rows + 4) // 4
    pitch = rows + 4 * HALO
    vmem = pl.BlockSpec(memory_space=pltpu.VMEM)
    smem = pl.BlockSpec(memory_space=pltpu.SMEM)
    operands = tuple(fields) + (land, upper, lower) + tuple(weights) + tuple(tables(cols))
    field = jax.ShapeDtypeStruct(fields[0].shape, jnp.float32)
    top_rows = -(-(groups + 1) * STRIPS // LANES) * LANES
    return pl.pallas_call(
        step_kernel,
        out_shape=(field,) * 3,
        in_specs=[smem, smem] + [vmem] * len(operands),
        out_specs=(vmem,) * 3,
        scratch_shapes=[
            pltpu.VMEM((4, rows + 2 * PAD, cols), jnp.float32),
            pltpu.VMEM((3 * pitch, (2 * windows + 1) * LANES), jnp.float32),
            pltpu.VMEM((8, cols), jnp.float32),
            pltpu.VMEM((4, windows, LEAD + 3 * pitch + 24, LANES), jnp.float32),
            pltpu.VMEM((2, windows * LANES, LANES), jnp.float32),
            pltpu.VMEM((2, (groups + 2) * STRIPS, LANES), jnp.bfloat16),
            pltpu.VMEM((4 * width, width), jnp.bfloat16),
            pltpu.VMEM((3, (groups + 2) * STRIPS, width), jnp.bfloat16),
            pltpu.VMEM((2, top_rows, width), jnp.bfloat16),
            pltpu.VMEM((64, top_rows), jnp.float32),
            pltpu.VMEM((16 * (turns + 1), cols), jnp.float32),
            pltpu.VMEM((cols // LANES, 16 * (turns + 1) - 24, LANES), jnp.float32),
        ],
        compiler_params=pltpu.CompilerParams(vmem_limit_bytes=60 * 1024 * 1024),
        name="step",
    )(depth, where, *operands)


def body(
    velocity_u,
    velocity_v,
    tracer,
    land,
    tile_depth,
    conv_one,
    bias_one,
    conv_two,
    bias_two,
    conv_three,
    bias_three,
):
    levels_here, rows, cols = velocity_u.shape
    across = cols // rows
    group_index = lax.axis_index("group")
    tile_index = lax.axis_index("tile")
    tile_count = lax.axis_size("tile")
    edge = HALO + 1
    depth_grid = tile_depth.reshape(tile_count, across)
    my_depth = lax.dynamic_index_in_dim(depth_grid, tile_index, 0, keepdims=False)
    column_depth = jnp.repeat(my_depth, rows)[None]

    def border(at):
        reach = jnp.where(land[at] == 1, column_depth, 0).astype(jnp.float32)
        return jnp.concatenate([velocity_u[:, at], velocity_v[:, at], tracer[:, at], reach[None]], axis=0)

    forward = [(i, i + 1) for i in range(tile_count - 1)]
    backward = [(target, source) for source, target in forward]
    upper = lax.ppermute(border(slice(rows - edge, rows)), "tile", forward)
    lower = lax.ppermute(border(slice(0, edge)), "tile", backward)
    where = jnp.stack(
        [
            jnp.asarray(group_index * levels_here, jnp.int32),
            jnp.asarray(tile_index * rows, jnp.int32),
            jnp.asarray(tile_count * rows, jnp.int32),
        ]
    )
    weights = arranged_weights(conv_one, bias_one, conv_two, bias_two, conv_three, bias_three)
    return ocean_step(my_depth, where, (velocity_u, velocity_v, tracer), land, upper, lower, weights)


def solution(mesh):
    field = P("group", "tile", None)
    in_specs = (field, field, field, P("tile", None)) + (P(),) * 7
    return jax.shard_map(
        body, mesh=mesh, in_specs=in_specs, out_specs=(field,) * 3, check_vma=False
    )
```

time: 726 us -> 77.5 us (0.11)
  matrix products: 364 us -> 0 us
  waiting for transfers between devices: 224 us -> 0.01 us
  local copies, waits for them, and re-layouts: 72.1 us -> 8.98 us
  Pallas kernels: 0 us -> 56.2 us
  loops' own time: 20.6 us -> 0 us
  starting transfers between devices: 23.2 us -> 6.5 us
  other arithmetic: 13.1 us -> 4.47 us
    conv_general_dilated x9 -> x0, matrix products: 364 us -> none  [convolve(): lax.conv_general_dilated(source, kernel, (1, 1), 'VALID', dimension_numbe...]
    all_to_all x2 -> x0, waiting for transfers between devices: 218 us -> none  [the longest x1 146 us: body(): lax.all_to_all(outgoing, ('group', 'tile'), split_axis=0, concat_axis=0,...]
    pallas_call x0 -> x1, Pallas kernels: none -> 56.2 us  [ocean_step(): pl.pallas_call(step_kernel, out_shape=(field,) * 3, in_specs=[smem, smem]...]
    conv_general_dilated x12 -> x0, local copies, waits for them, and re-layouts: 42.3 us -> none  [convolve(): lax.conv_general_dilated(source, kernel, (1, 1), 'VALID', dimension_numbe...]
    another operation x1 -> x0, loops' own time: 20.6 us -> none  [body(): results = lax.map(closure, arriving[senders])]
    ppermute x6 -> x2, starting transfers between devices: 16.4 us -> 6.5 us  [the longest x1 4.58 us: body(): upper = lax.ppermute(border(slice(rows - edge, rows)), 'tile', forward)]
    scatter x2 -> x0, local copies, waits for them, and re-layouts: 7.36 us -> none  [the longest x1 5.04 us: body(): outgoing = jnp.zeros((devices,) + windows.shape[1:], jnp.bfloat16).at[tar...]
  transfers between devices with their start and end apart: 8 -> 2, of which waited for: 4 -> 0; matrix products, arithmetic and copies ran while one was open for 1% -> 12% of each run, Pallas kernels for 0% -> 0%
where the time goes in v2:
time: 77.5 us; the launch traced here: 77 us
  Pallas kernels  56.2 us (73%)
  local copies, waits for them, and re-layouts  8.98 us (12%)
  starting transfers between devices  6.5 us (8%)
  other arithmetic  4.47 us (6%)
  between operations  0.78 us (1%)
    pallas_call x1, Pallas kernels, ocean_step(): pl.pallas_call(step_kernel, out_shape=(field,) * 3, in_specs=[smem, smem]...  56.2 us
    ppermute x1, starting transfers between devices, body(): upper = lax.ppermute(border(slice(rows - edge, rows)), 'tile', forward)  4.58 us
    ppermute x1, starting transfers between devices, body(): lower = lax.ppermute(border(slice(0, edge)), 'tile', backward)  1.92 us
  transfers between devices with their start and end apart: 2, of which 0 were waited for; matrix products, arithmetic and copies ran while one was open for 12% of the time, Pallas kernels for 0%

profile of v2, /device:TPU:1, one launch (start us, length us, event | category | flops | bytes accessed | tf_op | source)
XLA Modules:
  0.0 77.0 jit_solution(3112710764933484369)
XLA Ops:
  0.6 0.0 copy-start
  0.6 0.8 reshape.22
  1.4 0.0 copy-start.3
  1.4 0.1 broadcast_bitcast_fusion
  1.5 0.8 %fusion.8 = (f32[1,5,1024]{2,1,0:T(8,128)S(1)}, f32[1,5,1024]{2,1,0:T(8,128)S(1)}) fusion(f32[1,128,1024]{2,1,0:T(8,128)} %tracer_ref.1), kind=kLoop, calls=%fused_computation.38 | loop fusion | bytes 81920 | tf_op jit(solution)/shard_map/slice | solution.py:348
  2.3 0.8 %convert_bitcast_fusion = (f32[1,5,1024]{2,1,0:T(8,128)S(1)}, f32[1,5,1024]{2,1,0:T(8,128)S(1)}) fusion(s32[128,1024]{1,0:T(8,128)} %land_ref.1, s32[1024]{0:T(1024)S(1)} %broadcast_bitcast_fusion), kind=kLoop, calls=%fused_computation.14 | loop fusion | flops 30720 | bytes 86016 | tf_op jit(solution)/shard_map/broadcast_in_dim | solution.py:348
  3.1 0.8 %fusion.6 = (f32[1,5,1024]{2,1,0:T(8,128)S(1)}, f32[1,5,1024]{2,1,0:T(8,128)S(1)}, f32[1,5,1024]{2,1,0:T(8,128)S(1)}, f32[1,5,1024]{2,1,0:T(8,128)S(1)}) fusion(f32[1,128,1024]{2,1,0:T(8,128)} %east_ref.1, f32[1,128,1024]{2,1,0:T(8,128)} %north_ref.1), kind=kLoop, calls=%fused_computation.36 | loop fusion | bytes 163840 | tf_op jit(solution)/shard_map/slice | solution.py:348
  3.9 4.6 %collective-permute-start = (f32[4,5,1024]{2,1,0:T(8,128)S(1)}, f32[4,5,1024]{2,1,0:T(8,128)S(1)}, u32[]{:S(2)}, u32[]{:S(2)}) collective-permute-start(f32[4,5,1024]{2,1,0:T(8,128)S(1)} %pad_maximum_fusion), channel_id=1, source_target_pairs={{0,1},{1,2},{2,3},{3,4},{4,5},{5,6},{6,7},{8,9},{9,10},{10,11},{11... | collective-permute-start | bytes 245768 | tf_op jit(solution)/shard_map/ppermute | solution.py:352
  8.5 1.9 %collective-permute-start.1 = (f32[4,5,1024]{2,1,0:T(8,128)S(1)}, f32[4,5,1024]{2,1,0:T(8,128)S(1)}, u32[]{:S(2)}, u32[]{:S(2)}) collective-permute-start(f32[4,5,1024]{2,1,0:T(8,128)S(1)} %pad_maximum_fusion.1), channel_id=1, source_target_pairs={{1,0},{2,1},{3,2},{4,3},{5,4},{6,5},{7,6},{9,8},{10,9},{11,10},{12... | collective-permute-start | bytes 245768 | tf_op jit(solution)/shard_map/ppermute | solution.py:353
  10.5 0.7 broadcast_multiply_fusion.1
  11.1 0.7 broadcast_multiply_fusion
  11.8 0.7 broadcast_in_dim_tile.10.mid_ref
  12.5 0.7 broadcast_in_dim_tile.9.low_ref
  13.1 0.7 pad.64
  13.8 0.7 broadcast_in_dim_tile.12.high_ref
  14.5 0.7 multiply_bitcast_fusion.1
  15.3 0.1 reshape.23
  15.4 0.9 %pad_bitcast_fusion.3 = (bf16[4,4,1,3,64]{4,1,0,3,2:T(4,128)(2,1)S(1)}, bf16[4,4,1,3,64]{4,1,0,3,2:T(4,128)(2,1)S(1)}, bf16[4,4,1,3,64]{4,1,0,3,2:T(4,128)(2,1)S(1)}, bf16[4,4,1,3,64]{4,1,0,3,2:T(4,128)(2,1)S(1)}) fusion(bf16[3,3,3,64]{3,1,0,2:T(4,128)(2,1)} %bitcast.47), kind=kLoop, calls=%fused_computation.25 | loop fusion | bytes 28032 | tf_op jit(solution)/shard_map/stack | solution.py:26
  16.5 0.7 reshape.25.three_ref
  17.2 0.0 copy-done
  17.2 0.1 copy.17
  17.4 0.8 %fusion.2.taps_ref = bf16[3,4,64,128]{3,2,1,0:T(8,128)(2,1)} fusion(bf16[3,3,64,64]{3,2,1,0:T(8,128)(2,1)S(1)} %multiply_bitcast_fusion), kind=kLoop, calls=%fused_computation.4 | loop fusion | flops 786432 | bytes 270336 | tf_op jit(solution)/shard_map/concatenate | solution.py:46
  18.2 0.6 pad.56.one_ref
  18.8 0.7 pad_add_fusion.where_ref
  19.4 0.0 collective-permute-done.upper_ref
  19.4 0.0 copy-start.1
  19.4 0.0 collective-permute-done.1.lower_ref
  19.5 0.0 copy-done.3
  19.5 0.6 copy-done.1
  20.1 0.0 copy-start.2
  20.1 0.7 copy-done.2
  20.7 56.2 %step.1 = (f32[1,128,1024]{2,1,0:T(8,128)}, f32[1,128,1024]{2,1,0:T(8,128)}, f32[1,128,1024]{2,1,0:T(8,128)}) custom-call(s32[8]{0:T(128)} %copy-done.3, s32[3]{0:T(128)} %pad_add_fusion.where_ref, f32[1,128,1024]{2,1,0:T(8,128)} %east_ref.1, f32[1,128,1024]{2,1,0:T(8,128)} %north_ref.1, f32[1,128,1024]{2,1,0:T(8,128)} %tracer_ref.1, s32[128,1024]{1,0:T(8,128)} %land_ref.1, ...), custom_call_target="tpu_custom_call" | custom-call | tf_op jit(solution)/shard_map/step/pallas_call | solution.py:299
  (14 shorter events, 0.3 us)
Async XLA Ops:
  0.6 16.6 %copy-start = (bf16[64,64,3,3]{1,0,3,2:T(8,128)(2,1)S(1)}, bf16[64,64,3,3]{1,0,3,2:T(8,128)(2,1)}, u32[]{:S(2)}) copy-start(bf16[64,64,3,3]{1,0,3,2:T(8,128)(2,1)} %param.20) | copy-start | bytes 221188
  1.4 18.0 %copy-start.3 = (s32[8]{0:T(128)}, s32[8]{0:T(128)S(1)}, u32[]{:S(2)}) copy-start(s32[8]{0:T(128)S(1)} %dynamic-slice_bitcast_fusion.depth_ref) | copy-start | bytes 100
  3.9 15.5 %collective-permute-start = (f32[4,5,1024]{2,1,0:T(8,128)S(1)}, f32[4,5,1024]{2,1,0:T(8,128)S(1)}, u32[]{:S(2)}, u32[]{:S(2)}) collective-permute-start(f32[4,5,1024]{2,1,0:T(8,128)S(1)} %pad_maximum_fusion), channel_id=1, source_target_pairs={{0,1},{1,2},{2,3},{3,4},{4,5},{5,6},{6,7},{8,9},{9,10},{10,11},{11... | collective-permute-start | bytes 245768 | tf_op jit(solution)/shard_map/ppermute | solution.py:352
  8.5 10.9 %collective-permute-start.1 = (f32[4,5,1024]{2,1,0:T(8,128)S(1)}, f32[4,5,1024]{2,1,0:T(8,128)S(1)}, u32[]{:S(2)}, u32[]{:S(2)}) collective-permute-start(f32[4,5,1024]{2,1,0:T(8,128)S(1)} %pad_maximum_fusion.1), channel_id=1, source_target_pairs={{1,0},{2,1},{3,2},{4,3},{5,4},{6,5},{7,6},{9,8},{10,9},{11,10},{12... | collective-permute-start | bytes 245768 | tf_op jit(solution)/shard_map/ppermute | solution.py:353
  19.4 0.6 copy-start.1
  20.1 0.7 copy-start.2

commit v3 on v2

--- a/solution.py
+++ b/solution.py
@@ -18,6 +18,7 @@
 HALO = 4
 PAD = 16
 LEAD = 8
+TURN = 6
 
 
 def taps(kernel):
@@ -41,6 +42,11 @@
     outputs = conv_three.shape[0]
     half = jnp.asarray(0.5, jnp.bfloat16)
     one = taps(conv_one * half).transpose(5, 1, 0, 2, 3, 4).reshape(16 * inputs, 4 * hidden)
+    rest, pieces = jnp.tile(0.5 * bias_one, 4)[None], []
+    for _ in range(3):
+        pieces.append(lax.reduce_precision(rest, 8, 7))
+        rest = rest - pieces[-1]
+    one = jnp.concatenate([one] + [piece.astype(jnp.bfloat16) for piece in pieces], axis=0)
     one = jnp.pad(one, ((0, LANES - one.shape[0]), (0, 0)))
     two = (conv_two * half).transpose(2, 3, 1, 0)
     two = jnp.concatenate(
@@ -49,10 +55,9 @@
     three = jnp.pad(taps(conv_three), ((0, 0),) * 4 + ((0, 4 - outputs), (0, 0)))
     three = three.reshape(2, 2, 2, 2, 2, 2, 4, hidden).transpose(0, 2, 5, 4, 6, 1, 3, 7)
     three = three.reshape(64, 4 * hidden)
-    low = jnp.tile(0.5 * bias_one, 4)[None]
     mid = jnp.tile(0.5 * bias_two, 4)[None]
     high = jnp.tile(jnp.pad(bias_three, (0, 4 - outputs)), 4)[:, None]
-    return one, low, two, mid, three, high
+    return one, two, mid, three, high
 
 
 def tables(cols):
@@ -80,7 +85,6 @@
     upper_ref,
     lower_ref,
     one_ref,
-    low_ref,
     taps_ref,
     mid_ref,
     three_ref,
@@ -111,7 +115,8 @@
     rows_one, rows_two = (groups + 2) * STRIPS, (groups + 1) * STRIPS
     pitch = sheet.shape[0] // 3
     windows = -(-(half + 2) // LANES)
-    turns = (rows + 4) // 4
+    turns = (rows // 2 + 2) // TURN
+    strip = groups + 3
     lane = lax.broadcasted_iota(jnp.int32, (8, cols), 1)
     sub = lax.broadcasted_iota(jnp.int32, (8, LANES), 0)
 
@@ -123,7 +128,8 @@
             at = (slice(k * channels, (k + 1) * channels), slice(p * LANES, (p + 1) * LANES))
             two[at] = taps_ref[tap, 2 * bx + px] if 0 <= tap < 3 else jnp.zeros((channels, LANES), bf16)
     parts[...] = jnp.zeros_like(parts)
-    turned[...] = jnp.zeros_like(turned)
+    columns = lax.broadcasted_iota(jnp.int32, turned.shape, 2)
+    turned[...] = jnp.where((columns >= 48) & (columns < 51), 1.0, 0.0)
     sheet[...] = jnp.zeros_like(sheet)
     sums[...] = jnp.zeros_like(sums)
     top[...] = jnp.zeros_like(top)
@@ -195,6 +201,7 @@
                 parts[s, m, LEAD : LEAD + 3 * pitch, :] = pieces[:, s * LANES : (s + 1) * LANES]
 
     def prepare(slot, base, offset):
+        flipped, twin = [], slot % 2
         for m in range(windows):
             at = lambda s, first: parts[s, m, pl.ds(base + first, 8), :]
             stack = jnp.concatenate(
@@ -209,13 +216,16 @@
                 ],
                 axis=0,
             )
-            turned[slot, m * LANES : (m + 1) * LANES, 0:48] = stack.T
+            flipped.append(stack.T)
+        flipped = jnp.concatenate(flipped, axis=0)
+        for s in range(STRIPS):
+            turned[twin, s * strip : s * strip + groups + 8, 0:48] = flipped[s * groups : (s + 1) * groups + 8]
         for t in range(groups + 2):
-            ready[slot, t * STRIPS : (t + 1) * STRIPS, :] = turned[slot, pl.ds(t, STRIPS, groups), :].astype(bf16)
+            ready[slot, t * STRIPS : (t + 1) * STRIPS, :] = turned[twin, pl.ds(t, STRIPS, strip), :].astype(bf16)
 
     def layer_one(slot, target):
         value = jnp.dot(ready[slot], one_ref[...], preferred_element_type=f32)
-        hidden[target] = gate(value + low_ref[...]).astype(bf16)
+        hidden[target] = gate(value).astype(bf16)
 
     def layer_two(slot):
         gathered = jnp.concatenate(
@@ -230,14 +240,14 @@
             three_ref[...], top[slot], (((1,), (1,)), ((), ())), preferred_element_type=f32
         )
         old = sums[...]
-        wide = pltpu.roll(old[16:32] + new[48:64], new.shape[1] - STRIPS, 1)
-        value = old[0:16, 0:half] + new[32:48, 0:half] + wide[:, 0:half] + high_ref[...]
+        wide = old[16:32, STRIPS : STRIPS + half] + new[48:64, STRIPS : STRIPS + half]
+        value = old[0:16, 0:half] + new[32:48, 0:half] + wide + high_ref[...]
         stress[pl.ds(base + offset, 8), 0:half] = value[0:8]
         stress[pl.ds(base + offset, 8), half:cols] = value[8:16]
         sums[...] = new
 
     def finish(level, number):
-        merged = jnp.dot(stress[24:, :].astype(bf16), merge_ref[...], preferred_element_type=f32)
+        merged = jnp.dot(stress[8 * (TURN + 1) :, :].astype(bf16), merge_ref[...], preferred_element_type=f32)
         for tile in range(cols // LANES):
             natural[tile] = merged[:, tile * LANES : (tile + 1) * LANES]
 
@@ -259,43 +269,46 @@
         number = (where_ref[0] + level).astype(f32)
         advance(level, number)
         split_columns()
-        for slot in range(3):
-            prepare(slot % 2, 0, 2 * slot)
-            layer_one(slot % 2, slot)
-        prepare(0, 0, 6)
-        prepare(1, 0, 8)
+        for slot in range(TURN + 1):
+            prepare(slot % TURN, 0, 2 * slot)
+            layer_one(slot % TURN, slot)
+        for slot in range(TURN):
+            prepare(slot, 0, 2 * (TURN + 1 + slot))
 
         def turn(k, carry):
-            layer_three(0, pl.multiple_of(16 * k, 16), 0)
-            layer_three(1, pl.multiple_of(16 * k, 16), 8)
-            layer_two(0)
-            layer_two(1)
-            hidden[0] = hidden[2]
-            layer_one(0, 1)
-            layer_one(1, 2)
-            prepare(0, 4 * k, 10)
-            prepare(1, 4 * k, 12)
+            at = pl.multiple_of(8 * TURN * k, 16)
+            base = 2 * TURN * k
+            for i in range(TURN):
+                layer_three(i, at, 8 * i)
+                layer_two(i)
+                if i:
+                    layer_one(i - 1, i)
+                    prepare(i - 1, base, 2 * (2 * TURN + i))
+            hidden[0] = hidden[TURN]
+            layer_one(TURN - 1, TURN)
+            prepare(TURN - 1, base, 6 * TURN)
             return carry
 
         lax.fori_loop(0, turns, turn, 0)
-        layer_three(0, 16 * turns, 0)
-        layer_three(1, 16 * turns, 8)
+        for i in range(TURN):
+            layer_three(i, 8 * TURN * turns, 8 * i)
         finish(level, number)
 
 
 def ocean_step(depth, where, fields, land, upper, lower, weights):
     levels_here, rows, cols = fields[0].shape
-    width = weights[1].shape[1]
+    width = weights[0].shape[1]
     half = cols // 2
     groups = half // STRIPS
     windows = -(-(half + 2) // LANES)
-    turns = (rows + 4) // 4
+    turns = (rows // 2 + 2) // TURN
     pitch = rows + 4 * HALO
     vmem = pl.BlockSpec(memory_space=pltpu.VMEM)
     smem = pl.BlockSpec(memory_space=pltpu.SMEM)
     operands = tuple(fields) + (land, upper, lower) + tuple(weights) + tuple(tables(cols))
     field = jax.ShapeDtypeStruct(fields[0].shape, jnp.float32)
-    top_rows = -(-(groups + 1) * STRIPS // LANES) * LANES
+    top_rows = (groups + 1) * STRIPS
+    stress_rows = 8 * TURN * (turns + 1)
     return pl.pallas_call(
         step_kernel,
         out_shape=(field,) * 3,
@@ -305,17 +318,17 @@
             pltpu.VMEM((4, rows + 2 * PAD, cols), jnp.float32),
             pltpu.VMEM((3 * pitch, (2 * windows + 1) * LANES), jnp.float32),
             pltpu.VMEM((8, cols), jnp.float32),
-            pltpu.VMEM((4, windows, LEAD + 3 * pitch + 24, LANES), jnp.float32),
-            pltpu.VMEM((2, windows * LANES, LANES), jnp.float32),
-            pltpu.VMEM((2, (groups + 2) * STRIPS, LANES), jnp.bfloat16),
+            pltpu.VMEM((4, windows, LEAD + 3 * pitch + 8 * TURN, LANES), jnp.float32),
+            pltpu.VMEM((2, STRIPS * (groups + 3) + 8, LANES), jnp.float32),
+            pltpu.VMEM((TURN, (groups + 2) * STRIPS, LANES), jnp.bfloat16),
             pltpu.VMEM((4 * width, width), jnp.bfloat16),
-            pltpu.VMEM((3, (groups + 2) * STRIPS, width), jnp.bfloat16),
-            pltpu.VMEM((2, top_rows, width), jnp.bfloat16),
+            pltpu.VMEM((TURN + 1, (groups + 2) * STRIPS, width), jnp.bfloat16),
+            pltpu.VMEM((TURN, top_rows, width), jnp.bfloat16),
             pltpu.VMEM((64, top_rows), jnp.float32),
-            pltpu.VMEM((16 * (turns + 1), cols), jnp.float32),
-            pltpu.VMEM((cols // LANES, 16 * (turns + 1) - 24, LANES), jnp.float32),
+            pltpu.VMEM((stress_rows, cols), jnp.float32),
+            pltpu.VMEM((cols // LANES, stress_rows - 8 * (TURN + 1), LANES), jnp.float32),
         ],
-        compiler_params=pltpu.CompilerParams(vmem_limit_bytes=60 * 1024 * 1024),
+        compiler_params=pltpu.CompilerParams(vmem_limit_bytes=40 * 1024 * 1024),
         name="step",
     )(depth, where, *operands)
 

time: 77.5 us -> 63 us (0.81)
  Pallas kernels: 56.2 us -> 38.9 us
  other arithmetic: 4.47 us -> 6.7 us
    pallas_call x1, Pallas kernels: 56.2 us -> 38.9 us  [ocean_step(): pl.pallas_call(step_kernel, out_shape=(field,) * 3, in_specs=[smem, smem]...]
    unnamed x9 -> x13, local copies, waits for them, and re-layouts: 1.43 us -> 4.78 us
    concatenate x2, other arithmetic: 0.03 us -> 1.34 us  [border(): jnp.concatenate([velocity_u[:, at], velocity_v[:, at], tracer[:, at], rea...]
    transpose x1, other arithmetic: 0.02 us -> 0.92 us  [arranged_weights(): two = (conv_two * half).transpose(2, 3, 1, 0)]
  transfers between devices with their start and end apart: 2 -> 2, of which waited for: 0 -> 0; matrix products, arithmetic and copies ran while one was open for 12% -> 15% of each run, Pallas kernels for 0% -> 0%
where the time goes in v3:
time: 63 us; the launch traced here: 62.4 us
  Pallas kernels  38.9 us (62%)
  local copies, waits for them, and re-layouts  9.47 us (15%)
  other arithmetic  6.7 us (11%)
  starting transfers between devices  6.48 us (10%)
  between operations  0.79 us (1%)
    pallas_call x1, Pallas kernels, ocean_step(): pl.pallas_call(step_kernel, out_shape=(field,) * 3, in_specs=[smem, smem]...  38.9 us
    unnamed x13, local copies, waits for them, and re-layouts  4.78 us
    ppermute x1, starting transfers between devices, body(): upper = lax.ppermute(border(slice(rows - edge, rows)), 'tile', forward)  4.57 us
    ppermute x1, starting transfers between devices, body(): lower = lax.ppermute(border(slice(0, edge)), 'tile', backward)  1.91 us
    concatenate x2, other arithmetic, border(): jnp.concatenate([velocity_u[:, at], velocity_v[:, at], tracer[:, at], rea...  1.34 us
  transfers between devices with their start and end apart: 2, of which 0 were waited for; matrix products, arithmetic and copies ran while one was open for 15% of the time, Pallas kernels for 0%

profile of v3, /device:TPU:1, one launch (start us, length us, event | category | flops | bytes accessed | tf_op | source)
XLA Modules:
  0.0 62.4 jit_solution(7841004991161221093)
XLA Ops:
  0.6 0.0 copy-start
  0.6 0.0 copy-start.1
  0.7 0.0 copy-start.2
  0.7 0.9 %reshape.82 = s32[8,8]{1,0:T(8,128)S(1)} reshape(s32[64]{0:T(128)} %param.17) | data formatting | bytes 512 | tf_op jit(solution)/shard_map/reshape | solution.py:355
  1.6 0.1 broadcast_bitcast_fusion
  1.6 0.8 %fusion.17 = (f32[1,5,1024]{2,1,0:T(8,128)S(1)}, f32[1,5,1024]{2,1,0:T(8,128)S(1)}) fusion(f32[1,128,1024]{2,1,0:T(8,128)} %tracer_ref.1), kind=kLoop, calls=%fused_computation.52 | loop fusion | bytes 81920 | tf_op jit(solution)/shard_map/slice | solution.py:361
  2.4 0.8 %convert_bitcast_fusion = (f32[1,5,1024]{2,1,0:T(8,128)S(1)}, f32[1,5,1024]{2,1,0:T(8,128)S(1)}) fusion(s32[128,1024]{1,0:T(8,128)} %land_ref.1, s32[1024]{0:T(1024)S(1)} %broadcast_bitcast_fusion), kind=kLoop, calls=%fused_computation.22 | loop fusion | flops 30720 | bytes 86016 | tf_op jit(solution)/shard_map/broadcast_in_dim | solution.py:361
  3.2 0.8 %fusion.15 = (f32[1,5,1024]{2,1,0:T(8,128)S(1)}, f32[1,5,1024]{2,1,0:T(8,128)S(1)}, f32[1,5,1024]{2,1,0:T(8,128)S(1)}, f32[1,5,1024]{2,1,0:T(8,128)S(1)}) fusion(f32[1,128,1024]{2,1,0:T(8,128)} %east_ref.1, f32[1,128,1024]{2,1,0:T(8,128)} %north_ref.1), kind=kLoop, calls=%fused_computation.50 | loop fusion | bytes 163840 | tf_op jit(solution)/shard_map/slice | solution.py:361
  4.0 0.7 %pad_maximum_fusion = f32[4,5,1024]{2,1,0:T(8,128)} fusion(f32[1,5,1024]{2,1,0:T(8,128)S(1)} %get-tuple-element.4, f32[1,5,1024]{2,1,0:T(8,128)S(1)} %get-tuple-element.10, f32[1,5,1024]{2,1,0:T(8,128)S(1)} %get-tuple-element.22, f32[1,5,1024]{2,1,0:T(8,128)S(1)} %get-tuple-element.6), kind=kLoop, calls=%fused_computation.14 | loop fusion | flops 61440 | bytes 163840 | tf_op jit(solution)/shard_map/concatenate | solution.py:361
  4.7 4.6 %collective-permute-start = (f32[4,5,1024]{2,1,0:T(8,128)}, f32[4,5,1024]{2,1,0:T(8,128)S(1)}, u32[]{:S(2)}, u32[]{:S(2)}) collective-permute-start(f32[4,5,1024]{2,1,0:T(8,128)} %pad_maximum_fusion), channel_id=1, source_target_pairs={{0,1},{1,2},{2,3},{3,4},{4,5},{5,6},{6,7},{8,9},{9,10},{10,11},{11... | collective-permute-start | bytes 245768 | tf_op jit(solution)/shard_map/ppermute | solution.py:365
  9.3 0.7 %pad_maximum_fusion.1 = f32[4,5,1024]{2,1,0:T(8,128)} fusion(f32[1,5,1024]{2,1,0:T(8,128)S(1)} %get-tuple-element.3, f32[1,5,1024]{2,1,0:T(8,128)S(1)} %get-tuple-element.9, f32[1,5,1024]{2,1,0:T(8,128)S(1)} %get-tuple-element.23, f32[1,5,1024]{2,1,0:T(8,128)S(1)} %get-tuple-element.5), kind=kLoop, calls=%fused_computation.15 | loop fusion | flops 61440 | bytes 163840 | tf_op jit(solution)/shard_map/concatenate | solution.py:361
  10.0 1.9 %collective-permute-start.1 = (f32[4,5,1024]{2,1,0:T(8,128)}, f32[4,5,1024]{2,1,0:T(8,128)S(1)}, u32[]{:S(2)}, u32[]{:S(2)}) collective-permute-start(f32[4,5,1024]{2,1,0:T(8,128)} %pad_maximum_fusion.1), channel_id=1, source_target_pairs={{1,0},{2,1},{3,2},{4,3},{5,4},{6,5},{7,6},{9,8},{10,9},{11,10},{12... | collective-permute-start | bytes 245768 | tf_op jit(solution)/shard_map/ppermute | solution.py:366
  11.9 0.7 %broadcast_multiply_fusion.1 = f32[64]{0:T(128)S(1)} fusion(f32[64]{0:T(128)} %param.19), kind=kLoop, calls=%fused_computation.49 | loop fusion | flops 64 | bytes 512 | tf_op jit(solution)/shard_map/mul | solution.py:45
  12.5 0.7 %broadcast_multiply_fusion = f32[64]{0:T(128)S(1)} fusion(f32[64]{0:T(128)} %param.21), kind=kLoop, calls=%fused_computation.48 | loop fusion | flops 64 | bytes 512 | tf_op jit(solution)/shard_map/mul | solution.py:58
  13.2 0.1 broadcast_in_dim_tile.10.mid_ref
  13.3 0.1 broadcast_in_dim_tile.9
  13.4 0.6 reduce-precision_convert_fusion.1
  14.0 0.7 %pad.64 = f32[4]{0:T(128)S(1)} pad(f32[3]{0:T(128)} %param.23, f32[]{:T(128)} %constant.33.clone.1), padding=0_1 | pad | bytes 32 | tf_op jit(solution)/shard_map/jit(_pad)/pad | solution.py:59
  14.6 0.1 broadcast_in_dim_tile.12.high_ref
  14.7 0.7 %multiply_bitcast_fusion.1 = bf16[3,3,64,3]{2,1,0,3:T(4,128)(2,1)S(1)} fusion(bf16[64,3,3,3]{0,3,2,1:T(4,128)(2,1)} %param.18), kind=kLoop, calls=%fused_computation.38 | loop fusion | flops 1728 | bytes 6912 | tf_op jit(solution)/shard_map/transpose | solution.py:29
  15.6 0.1 reshape.83
  15.7 0.9 %pad_bitcast_fusion.3 = (bf16[4,4,1,3,64]{4,1,0,3,2:T(4,128)(2,1)S(1)}, bf16[4,4,1,3,64]{4,1,0,3,2:T(4,128)(2,1)S(1)}, bf16[4,4,1,3,64]{4,1,0,3,2:T(4,128)(2,1)S(1)}, bf16[4,4,1,3,64]{4,1,0,3,2:T(4,128)(2,1)S(1)}) fusion(bf16[3,3,3,64]{3,1,0,2:T(4,128)(2,1)} %bitcast.47), kind=kLoop, calls=%fused_computation.33 | loop fusion | bytes 28032 | tf_op jit(solution)/shard_map/stack | solution.py:27
  16.7 0.1 reshape.85.three_ref
  16.8 1.7 %copy.17 = bf16[64,64,3,3]{0,1,3,2:T(8,128)(2,1)} copy(bf16[64,64,3,3]{1,0,3,2:T(8,128)(2,1)} %param.20) | data formatting | bytes 147456 | tf_op args[7]
  18.5 0.9 %multiply_bitcast_fusion = bf16[3,3,64,64]{3,2,1,0:T(8,128)(2,1)S(1)} fusion(bf16[64,64,3,3]{0,1,3,2:T(8,128)(2,1)} %copy.17), kind=kLoop, calls=%fused_computation.5 | loop fusion | flops 36864 | bytes 147456 | tf_op jit(solution)/shard_map/transpose | solution.py:51
  19.4 0.1 fusion.2.taps_ref
  19.6 0.7 %fusion.11.one_ref = bf16[128,256]{1,0:T(8,128)(2,1)S(1)} fusion(bf16[1,256]{1,0:T(2,128)(2,1)S(1)} %get-tuple-element.20, bf16[1,256]{1,0:T(2,128)(2,1)} %get-tuple-element.21, bf16[1,256]{1,0:T(2,128)(2,1)S(1)} %get-tuple-element.19, bf16[48,256]{1,0:T(8,128)(2,1)S(1)} %reshape.83), kind=kLoop, calls=%fused_computation.18 | loop fusion | flops 425984 | bytes 91648 | tf_op jit(solution)/shard_map/concatenate | solution.py:49
  20.2 0.1 pad_add_fusion.where_ref
  20.4 1.0 %copy-done.3 = f32[1,128,1024]{2,1,0:T(8,128)S(1)} copy-done((f32[1,128,1024]{2,1,0:T(8,128)S(1)}, f32[1,128,1024]{2,1,0:T(8,128)}, u32[]{:S(2)}) %copy-start.3) | copy-done | bytes 524312
  21.4 1.0 %copy-done.4 = f32[1,128,1024]{2,1,0:T(8,128)S(1)} copy-done((f32[1,128,1024]{2,1,0:T(8,128)S(1)}, f32[1,128,1024]{2,1,0:T(8,128)}, u32[]{:S(2)}) %copy-start.4) | copy-done | bytes 524312
  22.4 1.0 %copy-done.5 = bf16[384,512]{1,0:T(8,128)(2,1)S(1)} copy-done((bf16[384,512]{1,0:T(8,128)(2,1)S(1)}, bf16[384,512]{1,0:T(8,128)(2,1)}, u32[]{:S(2)}) %copy-start.5) | copy-done | bytes 393240
  23.4 38.9 %step.1 = (f32[1,128,1024]{2,1,0:T(8,128)}, f32[1,128,1024]{2,1,0:T(8,128)}, f32[1,128,1024]{2,1,0:T(8,128)}) custom-call(s32[8]{0:T(128)S(1)} %dynamic-slice_bitcast_fusion.depth_ref, s32[3]{0:T(128)S(1)} %pad_add_fusion.where_ref, f32[1,128,1024]{2,1,0:T(8,128)S(1)} %copy-done.3, f32[1,128,1024]{2,1,0:T(8,128)S(1)} %copy-done.4, ...), custom_call_target="tpu_custom_call" | custom-call | tf_op jit(solution)/shard_map/step/pallas_call | solution.py:312
  (19 shorter events, 0.3 us)
Async XLA Ops:
  0.6 19.7 %copy-start = (bf16[1024,1024]{1,0:T(8,128)(2,1)S(1)}, bf16[1024,1024]{1,0:T(8,128)(2,1)}, u32[]{:S(2)}) copy-start(bf16[1024,1024]{1,0:T(8,128)(2,1)} %constant.35.clone.merge_ref) | copy-start | bytes 6291460
  0.6 19.7 %copy-start.1 = (f32[1,128,1024]{2,1,0:T(8,128)S(1)}, f32[1,128,1024]{2,1,0:T(8,128)}, u32[]{:S(2)}) copy-start(f32[1,128,1024]{2,1,0:T(8,128)} %tracer_ref.1) | copy-start | bytes 1572868
  0.7 19.7 %copy-start.2 = (s32[128,1024]{1,0:T(8,128)S(1)}, s32[128,1024]{1,0:T(8,128)}, u32[]{:S(2)}) copy-start(s32[128,1024]{1,0:T(8,128)} %land_ref.1) | copy-start | bytes 1572868
  4.7 15.6 %collective-permute-start = (f32[4,5,1024]{2,1,0:T(8,128)}, f32[4,5,1024]{2,1,0:T(8,128)S(1)}, u32[]{:S(2)}, u32[]{:S(2)}) collective-permute-start(f32[4,5,1024]{2,1,0:T(8,128)} %pad_maximum_fusion), channel_id=1, source_target_pairs={{0,1},{1,2},{2,3},{3,4},{4,5},{5,6},{6,7},{8,9},{9,10},{10,11},{11... | collective-permute-start | bytes 245768 | tf_op jit(solution)/shard_map/ppermute | solution.py:365
  10.0 10.4 %collective-permute-start.1 = (f32[4,5,1024]{2,1,0:T(8,128)}, f32[4,5,1024]{2,1,0:T(8,128)S(1)}, u32[]{:S(2)}, u32[]{:S(2)}) collective-permute-start(f32[4,5,1024]{2,1,0:T(8,128)} %pad_maximum_fusion.1), channel_id=1, source_target_pairs={{1,0},{2,1},{3,2},{4,3},{5,4},{6,5},{7,6},{9,8},{10,9},{11,10},{12... | collective-permute-start | bytes 245768 | tf_op jit(solution)/shard_map/ppermute | solution.py:366
  20.4 1.0 %copy-start.3 = (f32[1,128,1024]{2,1,0:T(8,128)S(1)}, f32[1,128,1024]{2,1,0:T(8,128)}, u32[]{:S(2)}) copy-start(f32[1,128,1024]{2,1,0:T(8,128)} %east_ref.1) | copy-start | bytes 1572868
  21.4 1.0 %copy-start.4 = (f32[1,128,1024]{2,1,0:T(8,128)S(1)}, f32[1,128,1024]{2,1,0:T(8,128)}, u32[]{:S(2)}) copy-start(f32[1,128,1024]{2,1,0:T(8,128)} %north_ref.1) | copy-start | bytes 1572868
  22.4 1.0 %copy-start.5 = (bf16[384,512]{1,0:T(8,128)(2,1)S(1)}, bf16[384,512]{1,0:T(8,128)(2,1)}, u32[]{:S(2)}) copy-start(bf16[384,512]{1,0:T(8,128)(2,1)} %constant.34.clone.split_ref) | copy-start | bytes 1179652

commit v4 on v3

v4 whole, which is shorter than its diff:
```python
import jax
import jax.numpy as jnp
from jax import lax
from jax.experimental import pallas as pl
from jax.experimental.pallas import tpu as pltpu
from jax.sharding import PartitionSpec as P

time_step = 0.1
viscosity = 0.5
diffusivity = 0.5
eddy_gain = 0.5
coriolis_base = 0.2
coriolis_slope = 0.6

LANES = 128
STRIPS = 16
HALO = 4
PAD = 16
LEAD = 8
EDGE = 8
TURN = 6


def gate(value):
    return value + value * jnp.tanh(value)


def border_kernel(depth_ref, east_ref, north_ref, tracer_ref, land_ref, first_ref, last_ref, shore, sems):
    levels_here, rows, cols = east_ref.shape
    depth = first_ref.shape[1]
    across = cols // rows
    tile_index = lax.axis_index("tile")
    copies = []
    for side, (target, start) in enumerate(((first_ref, 0), (last_ref, rows - depth))):
        at = pl.ds(start, depth)
        for f, ref in enumerate((east_ref, north_ref, tracer_ref)):
            for level in range(levels_here):
                slot = f * levels_here + level
                copies.append(pltpu.make_async_copy(ref.at[level, at], target.at[slot], sems.at[side, slot]))
        copies.append(pltpu.make_async_copy(land_ref.at[at], shore.at[side], sems.at[side, 3 * levels_here]))
    for copy in copies:
        copy.start()
    for copy in copies:
        copy.wait()
    for side, target in enumerate((first_ref, last_ref)):
        for tile in range(across):
            at = slice(tile * rows, (tile + 1) * rows)
            value = jnp.full((depth, rows), depth_ref[tile_index * across + tile], jnp.int32)
            target[3 * levels_here, :, at] = jnp.where(shore[side, :, at] == 1, value, 0).astype(jnp.float32)


def borders(tile_depth, fields, land, depth):
    levels_here, _, cols = fields[0].shape
    count = 3 * levels_here + 1
    edge = jax.ShapeDtypeStruct((count, depth, cols), jnp.float32)
    far = pl.BlockSpec(memory_space=pltpu.HBM)
    vmem = pl.BlockSpec(memory_space=pltpu.VMEM)
    return pl.pallas_call(
        border_kernel,
        out_shape=(edge, edge),
        in_specs=[pl.BlockSpec(memory_space=pltpu.SMEM)] + [far] * 4,
        out_specs=(vmem, vmem),
        scratch_shapes=[pltpu.VMEM((2, depth, cols), jnp.int32), pltpu.SemaphoreType.DMA((2, count))],
        compiler_params=pltpu.CompilerParams(vmem_limit_bytes=62 * 1024 * 1024),
        name="borders",
    )(tile_depth, *fields, land)


def step_kernel(
    depth_ref,
    high_ref,
    east_ref,
    north_ref,
    tracer_ref,
    land_ref,
    upper_ref,
    lower_ref,
    one_ref,
    low_ref,
    two_ref,
    mid_ref,
    three_ref,
    out_east,
    out_north,
    out_tracer,
    fields,
    shore,
    merge,
    split,
    one,
    three,
    rough,
    high,
    mid,
    sheet,
    parts,
    turned,
    ready,
    two,
    hidden,
    top,
    sums,
    stress,
    natural,
    sems,
):
    levels_here, rows, cols = east_ref.shape
    edge = upper_ref.shape[1]
    across = cols // rows
    f32, bf16 = jnp.float32, jnp.bfloat16
    groups = cols // 2 // STRIPS
    half = cols // 2
    rows_two = (groups + 1) * STRIPS
    pitch = sheet.shape[0] // 3
    windows = -(-(half + 2) // LANES)
    turns = (rows // 2 + 2) // TURN
    strip = groups + 3
    lane = lax.broadcasted_iota(jnp.int32, (8, cols), 1)
    sub = lax.broadcasted_iota(jnp.int32, (8, LANES), 0)
    tile_index = lax.axis_index("tile")
    first_row = tile_index * rows
    total_rows = lax.axis_size("tile") * rows
    first_level = lax.axis_index("group") * levels_here

    def bring(level):
        return [
            pltpu.make_async_copy(ref.at[level], fields.at[f, pl.ds(PAD, rows)], sems.at[f])
            for f, ref in enumerate((east_ref, north_ref, tracer_ref))
        ]

    shore_copy = pltpu.make_async_copy(land_ref, shore, sems.at[3])
    shore_copy.start()
    for copy in bring(0):
        copy.start()

    channels = two_ref.shape[2]
    blank = jnp.zeros((channels, channels), bf16)
    for k in range(16):
        by, bx, py, px = k // 8, k // 4 % 2, k // 2 % 2, k % 2
        for p in range(2):
            row, column = 2 * by + py - p, 2 * bx + px
            pair = [
                two_ref[row, column - par] if 0 <= row < 3 and 0 <= column - par < 3 else blank
                for par in range(2)
            ]
            two[k * channels : (k + 1) * channels, p * LANES : (p + 1) * LANES] = jnp.concatenate(pair, axis=1)
    rough[...] = jnp.zeros_like(rough)
    inputs = one_ref.shape[0]
    none = jnp.zeros((3, channels), f32)
    for c in range(inputs):
        for source in range(4):
            pair = [one_ref[c, source - par] if 0 <= source - par < 3 else none for par in range(2)]
            pair = jnp.concatenate(pair, axis=1)
            for p in range(2):
                start = c * 16 + source * 4 + p
                rough[start : start + 3, p * LANES : (p + 1) * LANES] = pair
    rest = jnp.concatenate([0.5 * low_ref[...]] * 4, axis=1)
    for k in range(3):
        piece = rest.astype(bf16).astype(f32)
        rough[16 * inputs + k : 16 * inputs + k + 1, :] = piece
        rest = rest - piece
    one[...] = rough[...].astype(bf16)
    none = jnp.zeros((4, channels), f32)
    for k in range(32):
        by, bx, par, p, py = k // 16, k // 8 % 2, k // 4 % 2, k // 2 % 2, k % 2
        row = 2 * by + py - p
        pair = [
            three_ref[row, 2 * bx + px - par] if 0 <= row < 3 and 0 <= 2 * bx + px - par < 3 else none
            for px in range(2)
        ]
        start = 32 * by + 16 * bx + 8 * par + 4 * p
        rough[start : start + 4, py * LANES : (py + 1) * LANES] = jnp.concatenate(pair, axis=1)
    three[...] = rough[0:64, :].astype(bf16)
    mid[...] = jnp.concatenate([0.5 * mid_ref[...]] * 4, axis=1)
    comp = lax.broadcasted_iota(jnp.int32, high.shape, 0) & 3
    value = jnp.zeros(high.shape, f32)
    for c in range(high_ref.shape[0]):
        value = jnp.where(comp == c, high_ref[c], value)
    high[...] = value
    w = lax.broadcasted_iota(jnp.int32, (3 * LANES, LANES), 0)
    x = lax.broadcasted_iota(jnp.int32, (3 * LANES, LANES), 1)
    for s in range(4):
        split[:, s * LANES : (s + 1) * LANES] = jnp.where(w == 2 * x - 3 + s + LANES, 1.0, 0.0).astype(bf16)

    at_strip = lax.broadcasted_iota(jnp.int32, (STRIPS, LANES), 0)
    at_lane = lax.broadcasted_iota(jnp.int32, (STRIPS, LANES), 1)
    for tile in range(cols // LANES):
        inside = at_lane + tile * LANES - 2 * groups * at_strip
        for par in range(2):
            for t in range(groups):
                start = par * half + t * STRIPS
                merge[start : start + STRIPS, tile * LANES : (tile + 1) * LANES] = jnp.where(
                    inside == 2 * t + par, 1.0, 0.0
                ).astype(bf16)
    columns = lax.broadcasted_iota(jnp.int32, turned.shape, 2)
    turned[...] = jnp.where((columns >= 48) & (columns < 51), 1.0, 0.0)
    for s in range(4):
        for m in range(windows):
            parts[s, m, 0:LEAD, :] = jnp.zeros((LEAD, LANES), f32)
            parts[s, m, LEAD + 3 * pitch :, :] = jnp.zeros((parts.shape[2] - LEAD - 3 * pitch, LANES), f32)
    sheet[:, 0:LANES] = jnp.zeros((3 * pitch, LANES), f32)
    sheet[:, LANES + cols :] = jnp.zeros((3 * pitch, sheet.shape[1] - LANES - cols), f32)
    for f in range(3):
        low_pad = f * pitch + rows + 2 * HALO
        sheet[low_pad : (f + 1) * pitch, :] = jnp.zeros((pitch - rows - 2 * HALO, sheet.shape[1]), f32)

    shore_copy.wait()
    depths = jnp.concatenate(
        [
            jnp.full((8, rows), depth_ref[tile_index * across + tile], jnp.int32).astype(f32)
            for tile in range(across)
        ],
        axis=1,
    )
    fields[3, PAD - edge : PAD, :] = upper_ref[3 * levels_here]
    fields[3, PAD + rows : PAD + rows + edge, :] = lower_ref[3 * levels_here]
    for r in range(0, rows, 8):
        fields[3, PAD + r : PAD + r + 8, :] = jnp.where(shore[r : r + 8, :] == 1, depths, 0.0)

    def sideways(value):
        left = jnp.where(lane > 0, pltpu.roll(value, 1, 1), 0.0)
        right = jnp.where(lane < cols - 1, pltpu.roll(value, cols - 1, 1), 0.0)
        return left, right

    def wet(number, at):
        return jnp.where(number < fields[3, at : at + 8, :], 1.0, 0.0)

    def advance(level, number):
        copies = bring(level)
        for f, copy in enumerate(copies):
            if level:
                copy.start()
            fields[f, PAD - edge : PAD, :] = upper_ref[f * levels_here + level]
            fields[f, PAD + rows : PAD + rows + edge, :] = lower_ref[f * levels_here + level]
        for copy in copies:
            copy.wait()
        for start in range(-8, rows + 8, 8):
            at = start + PAD

            def around(slot):
                here = fields[slot, at : at + 8, :]
                return (here, fields[slot, at - 1 : at + 7, :], fields[slot, at + 1 : at + 9, :]) + sideways(here)

            def curvature(a):
                return a[2] + a[1] + a[4] + a[3] - 4.0 * a[0]

            east, north, tracer = around(0), around(1), around(2)
            active = wet(number, at)
            row = first_row + start + lax.broadcasted_iota(jnp.int32, (8, cols), 0)
            coriolis = coriolis_base + coriolis_slope * (row.astype(f32) + 0.5) / total_rows
            grad_east = 0.5 * (tracer[2] - tracer[1])
            grad_north = 0.5 * (tracer[4] - tracer[3])
            rate = time_step * active
            news = (
                east[0] + rate * (coriolis * north[0] - grad_east + viscosity * curvature(east)),
                north[0] + rate * (-coriolis * east[0] - grad_north + viscosity * curvature(north)),
                tracer[0]
                + rate * (-(east[0] * grad_east + north[0] * grad_north) + diffusivity * curvature(tracer)),
            )
            for f, (new, out) in enumerate(zip(news, (out_east, out_north, out_tracer), strict=True)):
                if 0 <= start < rows:
                    out[level, start : start + 8, :] = new
                new = new * active
                first, last = max(start, -HALO), min(start + 8, rows + HALO)
                sheet[f * pitch + first + HALO : f * pitch + last + HALO, LANES : LANES + cols] = new[
                    first - start : last - start
                ]

    def split_columns():
        for m in range(windows):
            source = sheet[:, 2 * m * LANES : (2 * m + 3) * LANES].astype(bf16)
            pieces = jnp.dot(source, split[...], preferred_element_type=f32)
            for s in range(4):
                parts[s, m, LEAD : LEAD + 3 * pitch, :] = pieces[:, s * LANES : (s + 1) * LANES]

    def prepare(slot, base, offset):
        flipped, twin = [], slot % 2
        for m in range(windows):
            at = lambda s, first: parts[s, m, pl.ds(base + first, 8), :]
            stack = jnp.concatenate(
                [
                    jnp.where(
                        sub < 4,
                        at(s, LEAD + c * pitch + offset),
                        at(s + 1, LEAD + c * pitch + offset - 4),
                    )
                    for c in range(3)
                    for s in (0, 2)
                ],
                axis=0,
            )
            flipped.append(stack.T)
        flipped = jnp.concatenate(flipped, axis=0)
        for s in range(STRIPS):
            turned[twin, s * strip : s * strip + groups + 8, 0:48] = flipped[s * groups : (s + 1) * groups + 8]
        for t in range(groups + 2):
            ready[slot, t * STRIPS : (t + 1) * STRIPS, :] = turned[twin, pl.ds(t, STRIPS, strip), :].astype(bf16)

    def layer_one(slot, target):
        value = jnp.dot(ready[slot], one[...], preferred_element_type=f32)
        hidden[target] = gate(value).astype(bf16)

    def layer_two(slot):
        gathered = jnp.concatenate(
            [hidden[slot + by, bx * STRIPS : bx * STRIPS + rows_two, :] for by in range(2) for bx in range(2)],
            axis=1,
        )
        value = jnp.dot(gathered, two[...], preferred_element_type=f32)
        top[slot, 0:rows_two, :] = gate(value + mid[...]).astype(bf16)

    def layer_three(slot, base, offset):
        new = lax.dot_general(
            three[...], top[slot], (((1,), (1,)), ((), ())), preferred_element_type=f32
        )
        old = sums[...]
        wide = old[16:32, STRIPS : STRIPS + half] + new[48:64, STRIPS : STRIPS + half]
        value = old[0:16, 0:half] + new[32:48, 0:half] + wide + high[...]
        stress[pl.ds(base + offset, 8), 0:half] = value[0:8]
        stress[pl.ds(base + offset, 8), half:cols] = value[8:16]
        sums[...] = new

    def finish(level, number):
        merged = jnp.dot(stress[8 * (TURN + 1) :, :].astype(bf16), merge[...], preferred_element_type=f32)
        for tile in range(cols // LANES):
            natural[tile] = merged[:, tile * LANES : (tile + 1) * LANES]

        def field(start, shift, comp):
            at = pl.ds(4 * (start + 1 + shift) + comp, 8, 4)
            value = jnp.concatenate([natural[tile, at, :] for tile in range(cols // LANES)], axis=1)
            return value * wet(number, start + PAD + shift)

        for start in range(0, rows, 8):
            rate = eddy_gain * wet(number, start + PAD)
            east_left, east_right = sideways(field(start, 0, 1))
            north_left, north_right = sideways(field(start, 0, 2))
            push_east = 0.5 * (field(start, 1, 0) - field(start, -1, 0)) + 0.5 * (east_right - east_left)
            push_north = 0.5 * (field(start, 1, 1) - field(start, -1, 1)) + 0.5 * (north_right - north_left)
            out_east[level, start : start + 8, :] += rate * push_east
            out_north[level, start : start + 8, :] += rate * push_north

    for level in range(levels_here):
        number = (first_level + level).astype(f32)
        advance(level, number)
        split_columns()
        for slot in range(TURN + 1):
            prepare(slot % TURN, 0, 2 * slot)
            layer_one(slot % TURN, slot)
        for slot in range(TURN):
            prepare(slot, 0, 2 * (TURN + 1 + slot))

        def turn(k, carry):
            at = pl.multiple_of(8 * TURN * k, 16)
            base = 2 * TURN * k
            for i in range(TURN):
                layer_three(i, at, 8 * i)
                layer_two(i)
                if i:
                    layer_one(i - 1, i)
                    prepare(i - 1, base, 2 * (2 * TURN + i))
            hidden[0] = hidden[TURN]
            layer_one(TURN - 1, TURN)
            prepare(TURN - 1, base, 6 * TURN)
            return carry

        lax.fori_loop(0, turns, turn, 0)
        for i in range(TURN):
            layer_three(i, 8 * TURN * turns, 8 * i)
        finish(level, number)


def ocean_step(tile_depth, fields, land, upper, lower, weights):
    conv_one, bias_one, conv_two, bias_two, conv_three, bias_three = weights
    levels_here, rows, cols = fields[0].shape
    hidden = conv_two.shape[0]
    width = 4 * hidden
    half = cols // 2
    groups = half // STRIPS
    windows = -(-(half + 2) // LANES)
    turns = (rows // 2 + 2) // TURN
    pitch = rows + 4 * HALO
    f32, bf16 = jnp.float32, jnp.bfloat16
    one = conv_one.transpose(1, 3, 2, 0).astype(f32) * 0.5
    two = conv_two.transpose(2, 3, 1, 0) * jnp.asarray(0.5, bf16)
    three = jnp.pad(conv_three.transpose(2, 3, 0, 1).astype(f32), ((0, 0), (0, 0), (0, 4 - conv_three.shape[0]), (0, 0)))
    vmem = pl.BlockSpec(memory_space=pltpu.VMEM)
    smem = pl.BlockSpec(memory_space=pltpu.SMEM)
    far = pl.BlockSpec(memory_space=pltpu.HBM)
    field = jax.ShapeDtypeStruct(fields[0].shape, f32)
    top_rows = (groups + 1) * STRIPS
    stress_rows = 8 * TURN * (turns + 1)
    return pl.pallas_call(
        step_kernel,
        out_shape=(field,) * 3,
        in_specs=[smem, smem] + [far] * 4 + [vmem] * 7,
        out_specs=(vmem,) * 3,
        scratch_shapes=[
            pltpu.VMEM((4, rows + 2 * PAD, cols), f32),
            pltpu.VMEM((rows, cols), jnp.int32),
            pltpu.VMEM((cols, cols), bf16),
            pltpu.VMEM((3 * LANES, 4 * LANES), bf16),
            pltpu.VMEM((LANES, width), bf16),
            pltpu.VMEM((64, width), bf16),
            pltpu.VMEM((LANES, width), f32),
            pltpu.VMEM((16, half), f32),
            pltpu.VMEM((1, width), f32),
            pltpu.VMEM((3 * pitch, (2 * windows + 1) * LANES), f32),
            pltpu.VMEM((4, windows, LEAD + 3 * pitch + 8 * TURN, LANES), f32),
            pltpu.VMEM((2, STRIPS * (groups + 3) + 8, LANES), f32),
            pltpu.VMEM((TURN, (groups + 2) * STRIPS, LANES), bf16),
            pltpu.VMEM((4 * width, width), bf16),
            pltpu.VMEM((TURN + 1, (groups + 2) * STRIPS, width), bf16),
            pltpu.VMEM((TURN, top_rows, width), bf16),
            pltpu.VMEM((64, top_rows), f32),
            pltpu.VMEM((stress_rows, cols), f32),
            pltpu.VMEM((cols // LANES, stress_rows - 8 * (TURN + 1), LANES), f32),
            pltpu.SemaphoreType.DMA((4,)),
        ],
        compiler_params=pltpu.CompilerParams(vmem_limit_bytes=44 * 1024 * 1024),
        name="step",
    )(
        tile_depth,
        bias_three,
        *fields,
        land,
        upper,
        lower,
        one,
        bias_one[None],
        two,
        bias_two[None],
        three,
    )


def body(
    velocity_u,
    velocity_v,
    tracer,
    land,
    tile_depth,
    conv_one,
    bias_one,
    conv_two,
    bias_two,
    conv_three,
    bias_three,
):
    fields = (velocity_u, velocity_v, tracer)
    tile_count = lax.axis_size("tile")
    forward = [(i, i + 1) for i in range(tile_count - 1)]
    backward = [(target, source) for source, target in forward]
    first, last = borders(tile_depth, fields, land, EDGE)
    upper = lax.ppermute(last, "tile", forward)
    lower = lax.ppermute(first, "tile", backward)
    weights = (conv_one, bias_one, conv_two, bias_two, conv_three, bias_three)
    return ocean_step(tile_depth, fields, land, upper, lower, weights)


def solution(mesh):
    field = P("group", "tile", None)
    in_specs = (field, field, field, P("tile", None)) + (P(),) * 7
    return jax.shard_map(
        body, mesh=mesh, in_specs=in_specs, out_specs=(field,) * 3, check_vma=False
    )
```

time: 63 us -> 54.5 us (0.87)
  local copies, waits for them, and re-layouts: 9.47 us -> 2.19 us
  other arithmetic: 6.7 us -> 0.03 us
  waiting for transfers between devices: 0.01 us -> 2.98 us
  Pallas kernels: 38.9 us -> 41.6 us
    ppermute x2, waiting for transfers between devices: 0.01 us -> 2.98 us  [the longest x1 2.97 us: body(): lower = lax.ppermute(first, 'tile', backward)]
    unnamed x13 -> x24, local copies, waits for them, and re-layouts: 4.78 us -> 2.19 us
    pallas_call x0 -> x1, Pallas kernels: none -> 2.45 us  [borders(): pl.pallas_call(border_kernel, out_shape=(edge, edge), in_specs=[pl.BlockS...]
    concatenate x4 -> x0, other arithmetic: 2.13 us -> none  [the longest x2 1.34 us: border(): jnp.concatenate([velocity_u[:, at], velocity_v[:, at], tracer[:, at], rea...]
    transpose x3 -> x0, other arithmetic: 1.68 us -> none  [the longest x1 0.92 us: arranged_weights(): two = (conv_two * half).transpose(2, 3, 1, 0)]
    slice x2 -> x0, local copies, waits for them, and re-layouts: 1.61 us -> none  [the longest x1 0.82 us: border(): velocity_u[:, at]]
    mul x2, other arithmetic: 1.32 us -> 0.02 us  [the longest x1 0.02 us: ocean_step(): two = conv_two.transpose(2, 3, 1, 0) * jnp.asarray(0.5, bf16)]
    another operation x8 -> x0, local copies, waits for them, and re-layouts: 1.15 us -> none  [the longest x2 0.9 us: taps(): jnp.stack([jnp.pad(kernel.transpose(2, 3, 0, 1), ((p, 1 - p), (par, 1 - p...]
  transfers between devices with their start and end apart: 2 -> 2, of which waited for: 0 -> 1; matrix products, arithmetic and copies ran while one was open for 15% -> 0% of each run, Pallas kernels for 0% -> 0%
where the time goes in v4:
time: 54.5 us; the launch traced here: 54.2 us
  Pallas kernels  41.6 us (76%)
  starting transfers between devices  6.63 us (12%)
  waiting for transfers between devices  2.98 us (5%)
  local copies, waits for them, and re-layouts  2.19 us (4%)
  between operations  0.78 us (1%)
    pallas_call x1, Pallas kernels, ocean_step(): pl.pallas_call(step_kernel, out_shape=(field,) * 3, in_specs=[smem, smem]...  39.1 us
    ppermute x1, starting transfers between devices, body(): upper = lax.ppermute(last, 'tile', forward)  4.71 us
    ppermute x1, waiting for transfers between devices, body(): lower = lax.ppermute(first, 'tile', backward)  2.97 us
    pallas_call x1, Pallas kernels, borders(): pl.pallas_call(border_kernel, out_shape=(edge, edge), in_specs=[pl.BlockS...  2.45 us
    unnamed x24, local copies, waits for them, and re-layouts  2.19 us
    ppermute x1, starting transfers between devices, body(): lower = lax.ppermute(first, 'tile', backward)  1.92 us
  transfers between devices with their start and end apart: 2, of which 1 were waited for; matrix products, arithmetic and copies ran while one was open for 0% of the time, Pallas kernels for 0%

profile of v4, /device:TPU:1, one launch (start us, length us, event | category | flops | bytes accessed | tf_op | source)
XLA Modules:
  0.0 54.2 jit_solution(4767493862821019258)
XLA Ops:
  0.6 0.0 copy-start.8
  0.6 0.0 copy-start.1
  0.7 0.0 copy-start.2
  0.7 0.0 copy-start.3
  0.7 2.4 %borders.1 = (f32[4,8,1024]{2,1,0:T(8,128)}, f32[4,8,1024]{2,1,0:T(8,128)}) custom-call(s32[64]{0:T(128)} %depth_ref.3, f32[1,128,1024]{2,1,0:T(8,128)} %east_ref.3, f32[1,128,1024]{2,1,0:T(8,128)} %north_ref.3, f32[1,128,1024]{2,1,0:T(8,128)} %tracer_ref.3, s32[128,1024]{1,0:T(8,128)} %land_ref.3), custom_call_target="tpu_custom_call" | custom-call | tf_op jit(solution)/shard_map/borders/pallas_call | solution.py:58
  3.1 0.0 copy-start
  3.1 4.7 %collective-permute-start = (f32[4,8,1024]{2,1,0:T(8,128)}, f32[4,8,1024]{2,1,0:T(8,128)S(1)}, u32[]{:S(2)}, u32[]{:S(2)}) collective-permute-start(f32[4,8,1024]{2,1,0:T(8,128)} %get-tuple-element.5), channel_id=1, source_target_pairs={{0,1},{1,2},{2,3},{3,4},{4,5},{5,6},{6,7},{8,9},{9,10},{10,11},{11... | collective-permute-start | bytes 393224 | tf_op jit(solution)/shard_map/ppermute | solution.py:453
  7.9 1.9 %collective-permute-start.1 = (f32[4,8,1024]{2,1,0:T(8,128)}, f32[4,8,1024]{2,1,0:T(8,128)S(1)}, u32[]{:S(2)}, u32[]{:S(2)}) collective-permute-start(f32[4,8,1024]{2,1,0:T(8,128)} %get-tuple-element.6), channel_id=1, source_target_pairs={{1,0},{2,1},{3,2},{4,3},{5,4},{6,5},{7,6},{9,8},{10,9},{11,10},{12... | collective-permute-start | bytes 393224 | tf_op jit(solution)/shard_map/ppermute | solution.py:454
  9.8 0.0 copy-done.8
  9.8 0.1 copy.15
  9.9 0.0 copy-start.9
  10.0 0.7 %copy-done.9 = bf16[64,3,3,3]{0,3,2,1:T(4,128)(2,1)S(1)} copy-done((bf16[64,3,3,3]{0,3,2,1:T(4,128)(2,1)S(1)}, bf16[64,3,3,3]{0,3,2,1:T(4,128)(2,1)}, u32[]{:S(2)}) %copy-start.9) | copy-done | bytes 3480
  10.7 0.0 copy-start.10
  10.7 0.7 %copy-done.10 = bf16[3,64,3,3]{1,3,2,0:T(4,128)(2,1)S(1)} copy-done((bf16[3,64,3,3]{1,3,2,0:T(4,128)(2,1)S(1)}, bf16[3,64,3,3]{1,3,2,0:T(4,128)(2,1)}, u32[]{:S(2)}) %copy-start.10) | copy-done | bytes 3480
  11.4 0.0 copy-start.7
  11.4 0.0 collective-permute-done.upper_ref
  11.4 3.0 %collective-permute-done.1.lower_ref = f32[4,8,1024]{2,1,0:T(8,128)S(1)} collective-permute-done((f32[4,8,1024]{2,1,0:T(8,128)}, f32[4,8,1024]{2,1,0:T(8,128)S(1)}, u32[]{:S(2)}, u32[]{:S(2)}) %collective-permute-start.1) | collective-permute-done | bytes 131104 | tf_op jit(solution)/shard_map/ppermute | solution.py:454
  14.4 0.0 copy-start.4
  14.4 0.0 copy-start.5
  14.4 0.0 copy-start.6
  14.4 0.0 copy-done.1
  14.4 0.0 copy-done.2
  14.4 0.0 copy-done.3
  14.4 0.0 copy-done
  14.4 0.0 copy-done.7
  14.4 0.6 %copy-done.4 = s32[64]{0:T(128)S(1)} copy-done((s32[64]{0:T(128)S(1)}, s32[64]{0:T(128)}, u32[]{:S(2)}) %copy-start.4) | copy-done | bytes 280
  15.0 0.0 copy-done.5
  15.0 0.0 copy-done.6
  15.0 39.1 %step.1 = (f32[1,128,1024]{2,1,0:T(8,128)}, f32[1,128,1024]{2,1,0:T(8,128)}, f32[1,128,1024]{2,1,0:T(8,128)}) custom-call(s32[64]{0:T(128)S(1)} %copy-done.4, f32[3]{0:T(128)S(1)} %copy-done.5, f32[1,128,1024]{2,1,0:T(8,128)S(1)} %copy-done, f32[1,128,1024]{2,1,0:T(8,128)S(1)} %copy-done.1, f32[1,128,1024]{2,1,0:T(8,128)S(1)} %copy-done.2, ...), custom_call_target="tpu_custom_call" | custom-call | tf_op jit(solution)/shard_map/step/pallas_call | solution.py:391
  (4 shorter events, 0.0 us)
Async XLA Ops:
  0.6 9.2 %copy-start.8 = (bf16[64,64,3,3]{1,0,3,2:T(8,128)(2,1)S(1)}, bf16[64,64,3,3]{1,0,3,2:T(8,128)(2,1)}, u32[]{:S(2)}) copy-start(bf16[64,64,3,3]{1,0,3,2:T(8,128)(2,1)} %param.18) | copy-start | bytes 221188
  0.6 13.7 %copy-start.1 = (f32[1,128,1024]{2,1,0:T(8,128)S(1)}, f32[1,128,1024]{2,1,0:T(8,128)}, u32[]{:S(2)}) copy-start(f32[1,128,1024]{2,1,0:T(8,128)} %north_ref.3) | copy-start | bytes 1572868
  0.7 13.7 %copy-start.2 = (f32[1,128,1024]{2,1,0:T(8,128)S(1)}, f32[1,128,1024]{2,1,0:T(8,128)}, u32[]{:S(2)}) copy-start(f32[1,128,1024]{2,1,0:T(8,128)} %tracer_ref.3) | copy-start | bytes 1572868
  0.7 13.7 %copy-start.3 = (s32[128,1024]{1,0:T(8,128)S(1)}, s32[128,1024]{1,0:T(8,128)}, u32[]{:S(2)}) copy-start(s32[128,1024]{1,0:T(8,128)} %land_ref.3) | copy-start | bytes 1572868
  3.1 11.3 %copy-start = (f32[1,128,1024]{2,1,0:T(8,128)S(1)}, f32[1,128,1024]{2,1,0:T(8,128)}, u32[]{:S(2)}) copy-start(f32[1,128,1024]{2,1,0:T(8,128)} %east_ref.3) | copy-start | bytes 1572868
  3.1 8.2 %collective-permute-start = (f32[4,8,1024]{2,1,0:T(8,128)}, f32[4,8,1024]{2,1,0:T(8,128)S(1)}, u32[]{:S(2)}, u32[]{:S(2)}) collective-permute-start(f32[4,8,1024]{2,1,0:T(8,128)} %get-tuple-element.5), channel_id=1, source_target_pairs={{0,1},{1,2},{2,3},{3,4},{4,5},{5,6},{6,7},{8,9},{9,10},{10,11},{11... | collective-permute-start | bytes 393224 | tf_op jit(solution)/shard_map/ppermute | solution.py:453
  7.9 6.5 %collective-permute-start.1 = (f32[4,8,1024]{2,1,0:T(8,128)}, f32[4,8,1024]{2,1,0:T(8,128)S(1)}, u32[]{:S(2)}, u32[]{:S(2)}) collective-permute-start(f32[4,8,1024]{2,1,0:T(8,128)} %get-tuple-element.6), channel_id=1, source_target_pairs={{1,0},{2,1},{3,2},{4,3},{5,4},{6,5},{7,6},{9,8},{10,9},{11,10},{12... | collective-permute-start | bytes 393224 | tf_op jit(solution)/shard_map/ppermute | solution.py:454
  9.9 0.7 %copy-start.9 = (bf16[64,3,3,3]{0,3,2,1:T(4,128)(2,1)S(1)}, bf16[64,3,3,3]{0,3,2,1:T(4,128)(2,1)}, u32[]{:S(2)}) copy-start(bf16[64,3,3,3]{0,3,2,1:T(4,128)(2,1)} %param.16) | copy-start | bytes 10372
  10.7 0.7 %copy-start.10 = (bf16[3,64,3,3]{1,3,2,0:T(4,128)(2,1)S(1)}, bf16[3,64,3,3]{1,3,2,0:T(4,128)(2,1)}, u32[]{:S(2)}) copy-start(bf16[3,64,3,3]{1,3,2,0:T(4,128)(2,1)} %param.20) | copy-start | bytes 10372
  11.4 3.0 %copy-start.7 = (f32[64]{0:T(128)S(1)}, f32[64]{0:T(128)}, u32[]{:S(2)}) copy-start(f32[64]{0:T(128)} %param.19) | copy-start | bytes 772
  14.4 0.7 %copy-start.4 = (s32[64]{0:T(128)S(1)}, s32[64]{0:T(128)}, u32[]{:S(2)}) copy-start(s32[64]{0:T(128)} %depth_ref.3) | copy-start | bytes 772
  14.4 0.7 %copy-start.5 = (f32[3]{0:T(128)S(1)}, f32[3]{0:T(128)}, u32[]{:S(2)}) copy-start(f32[3]{0:T(128)} %high_ref.1) | copy-start | bytes 40
  14.4 0.7 %copy-start.6 = (f32[64]{0:T(128)S(1)}, f32[64]{0:T(128)}, u32[]{:S(2)}) copy-start(f32[64]{0:T(128)} %param.17) | copy-start | bytes 772

commit v5 on v4

--- a/solution.py
+++ b/solution.py
@@ -66,15 +66,47 @@
     )(tile_depth, *fields, land)
 
 
-def step_kernel(
+def sideways(value, lane):
+    cols = value.shape[1]
+    left = jnp.where(lane > 0, pltpu.roll(value, 1, 1), 0.0)
+    right = jnp.where(lane < cols - 1, pltpu.roll(value, cols - 1, 1), 0.0)
+    return left, right
+
+
+def evolve(fields, at, active, row, rows):
+    cols = fields.shape[-1]
+    f32 = jnp.float32
+    lane = lax.broadcasted_iota(jnp.int32, (8, cols), 1)
+    places = (row + lax.broadcasted_iota(jnp.int32, (8, LANES), 0)).astype(f32)
+    total_rows = lax.axis_size("tile") * rows
+    coriolis = coriolis_base + coriolis_slope * (places + 0.5) / total_rows
+    coriolis = jnp.concatenate([coriolis] * (cols // LANES), axis=1)
+
+    def around(f):
+        here = fields[f, at : at + 8, :]
+        return (here, fields[f, at - 1 : at + 7, :], fields[f, at + 1 : at + 9, :]) + sideways(here, lane)
+
+    def curvature(a):
+        return a[2] + a[1] + a[4] + a[3] - 4.0 * a[0]
+
+    east, north, tracer = around(0), around(1), around(2)
+    grad_east = 0.5 * (tracer[2] - tracer[1])
+    grad_north = 0.5 * (tracer[4] - tracer[3])
+    rate = time_step * active
+    return (
+        east[0] + rate * (coriolis * north[0] - grad_east + viscosity * curvature(east)),
+        north[0] + rate * (-coriolis * east[0] - grad_north + viscosity * curvature(north)),
+        tracer[0] + rate * (-(east[0] * grad_east + north[0] * grad_north) + diffusivity * curvature(tracer)),
+    )
+
+
+def interior_kernel(
     depth_ref,
     high_ref,
     east_ref,
     north_ref,
     tracer_ref,
     land_ref,
-    upper_ref,
-    lower_ref,
     one_ref,
     low_ref,
     two_ref,
@@ -83,43 +115,27 @@
     out_east,
     out_north,
     out_tracer,
+    reach,
+    sheet,
+    one,
+    two,
+    three,
+    mid,
+    high,
+    split,
+    merge,
     fields,
     shore,
-    merge,
-    split,
-    one,
-    three,
     rough,
-    high,
-    mid,
-    sheet,
-    parts,
-    turned,
-    ready,
-    two,
-    hidden,
-    top,
-    sums,
-    stress,
-    natural,
     sems,
 ):
     levels_here, rows, cols = east_ref.shape
-    edge = upper_ref.shape[1]
     across = cols // rows
     f32, bf16 = jnp.float32, jnp.bfloat16
     groups = cols // 2 // STRIPS
     half = cols // 2
-    rows_two = (groups + 1) * STRIPS
-    pitch = sheet.shape[0] // 3
-    windows = -(-(half + 2) // LANES)
-    turns = (rows // 2 + 2) // TURN
-    strip = groups + 3
-    lane = lax.broadcasted_iota(jnp.int32, (8, cols), 1)
-    sub = lax.broadcasted_iota(jnp.int32, (8, LANES), 0)
+    pitch = sheet.shape[1] // 3
     tile_index = lax.axis_index("tile")
-    first_row = tile_index * rows
-    total_rows = lax.axis_size("tile") * rows
     first_level = lax.axis_index("group") * levels_here
 
     def bring(level):
@@ -192,17 +208,18 @@
                 merge[start : start + STRIPS, tile * LANES : (tile + 1) * LANES] = jnp.where(
                     inside == 2 * t + par, 1.0, 0.0
                 ).astype(bf16)
-    columns = lax.broadcasted_iota(jnp.int32, turned.shape, 2)
-    turned[...] = jnp.where((columns >= 48) & (columns < 51), 1.0, 0.0)
-    for s in range(4):
-        for m in range(windows):
-            parts[s, m, 0:LEAD, :] = jnp.zeros((LEAD, LANES), f32)
-            parts[s, m, LEAD + 3 * pitch :, :] = jnp.zeros((parts.shape[2] - LEAD - 3 * pitch, LANES), f32)
-    sheet[:, 0:LANES] = jnp.zeros((3 * pitch, LANES), f32)
-    sheet[:, LANES + cols :] = jnp.zeros((3 * pitch, sheet.shape[1] - LANES - cols), f32)
+    for level in range(levels_here):
+        sheet[level, :, 0:LANES] = jnp.zeros((3 * pitch, LANES), f32)
+        sheet[level, :, LANES + cols :] = jnp.zeros((3 * pitch, sheet.shape[2] - LANES - cols), f32)
+        for f in range(3):
+            low_pad = f * pitch + rows + 2 * HALO
+            sheet[level, low_pad : (f + 1) * pitch, :] = jnp.zeros((pitch - rows - 2 * HALO, sheet.shape[2]), f32)
+            sheet[level, f * pitch : f * pitch + HALO, :] = jnp.zeros((HALO, sheet.shape[2]), f32)
+            low_pad = f * pitch + rows + HALO
+            sheet[level, low_pad : low_pad + HALO, :] = jnp.zeros((HALO, sheet.shape[2]), f32)
     for f in range(3):
-        low_pad = f * pitch + rows + 2 * HALO
-        sheet[low_pad : (f + 1) * pitch, :] = jnp.zeros((pitch - rows - 2 * HALO, sheet.shape[1]), f32)
+        fields[f, PAD - 8 : PAD, :] = jnp.zeros((8, cols), f32)
+        fields[f, PAD + rows : PAD + rows + 8, :] = jnp.zeros((8, cols), f32)
 
     shore_copy.wait()
     depths = jnp.concatenate(
@@ -212,66 +229,131 @@
         ],
         axis=1,
     )
-    fields[3, PAD - edge : PAD, :] = upper_ref[3 * levels_here]
-    fields[3, PAD + rows : PAD + rows + edge, :] = lower_ref[3 * levels_here]
     for r in range(0, rows, 8):
-        fields[3, PAD + r : PAD + r + 8, :] = jnp.where(shore[r : r + 8, :] == 1, depths, 0.0)
-
-    def sideways(value):
-        left = jnp.where(lane > 0, pltpu.roll(value, 1, 1), 0.0)
-        right = jnp.where(lane < cols - 1, pltpu.roll(value, cols - 1, 1), 0.0)
-        return left, right
-
-    def wet(number, at):
-        return jnp.where(number < fields[3, at : at + 8, :], 1.0, 0.0)
-
-    def advance(level, number):
+        reach[r : r + 8, :] = jnp.where(shore[r : r + 8, :] == 1, depths, 0.0)
+
+    for level in range(levels_here):
         copies = bring(level)
-        for f, copy in enumerate(copies):
+        for copy in copies:
             if level:
                 copy.start()
-            fields[f, PAD - edge : PAD, :] = upper_ref[f * levels_here + level]
-            fields[f, PAD + rows : PAD + rows + edge, :] = lower_ref[f * levels_here + level]
         for copy in copies:
             copy.wait()
-        for start in range(-8, rows + 8, 8):
-            at = start + PAD
-
-            def around(slot):
-                here = fields[slot, at : at + 8, :]
-                return (here, fields[slot, at - 1 : at + 7, :], fields[slot, at + 1 : at + 9, :]) + sideways(here)
-
-            def curvature(a):
-                return a[2] + a[1] + a[4] + a[3] - 4.0 * a[0]
-
-            east, north, tracer = around(0), around(1), around(2)
-            active = wet(number, at)
-            row = first_row + start + lax.broadcasted_iota(jnp.int32, (8, cols), 0)
-            coriolis = coriolis_base + coriolis_slope * (row.astype(f32) + 0.5) / total_rows
-            grad_east = 0.5 * (tracer[2] - tracer[1])
-            grad_north = 0.5 * (tracer[4] - tracer[3])
-            rate = time_step * active
-            news = (
-                east[0] + rate * (coriolis * north[0] - grad_east + viscosity * curvature(east)),
-                north[0] + rate * (-coriolis * east[0] - grad_north + viscosity * curvature(north)),
-                tracer[0]
-                + rate * (-(east[0] * grad_east + north[0] * grad_north) + diffusivity * curvature(tracer)),
-            )
+        number = (first_level + level).astype(f32)
+        for start in range(0, rows, 8):
+            active = jnp.where(number < reach[start : start + 8, :], 1.0, 0.0)
+            news = evolve(fields, start + PAD, active, tile_index * rows + start, rows)
             for f, (new, out) in enumerate(zip(news, (out_east, out_north, out_tracer), strict=True)):
-                if 0 <= start < rows:
-                    out[level, start : start + 8, :] = new
-                new = new * active
-                first, last = max(start, -HALO), min(start + 8, rows + HALO)
-                sheet[f * pitch + first + HALO : f * pitch + last + HALO, LANES : LANES + cols] = new[
-                    first - start : last - start
-                ]
-
-    def split_columns():
+                out[level, start : start + 8, :] = new
+                at = f * pitch + start + HALO
+                sheet[level, at : at + 8, LANES : LANES + cols] = new * active
+
+
+def step_kernel(
+    east_ref,
+    north_ref,
+    tracer_ref,
+    reach_ref,
+    sheet,
+    one,
+    two,
+    three,
+    mid,
+    high,
+    split,
+    merge,
+    upper_ref,
+    first_ref,
+    last_ref,
+    lower_ref,
+    out_east,
+    out_north,
+    out_tracer,
+    edges,
+    rim,
+    reach,
+    parts,
+    turned,
+    ready,
+    hidden,
+    top,
+    sums,
+    stress,
+    natural,
+):
+    levels_here, rows, cols = east_ref.shape
+    depth = upper_ref.shape[1]
+    f32, bf16 = jnp.float32, jnp.bfloat16
+    groups = cols // 2 // STRIPS
+    half = cols // 2
+    rows_two = (groups + 1) * STRIPS
+    pitch = sheet.shape[1] // 3
+    windows = -(-(half + 2) // LANES)
+    turns = (rows // 2 + 2) // TURN
+    strip = groups + 3
+    lane = lax.broadcasted_iota(jnp.int32, (8, cols), 1)
+    sub = lax.broadcasted_iota(jnp.int32, (8, LANES), 0)
+    line = lax.broadcasted_iota(jnp.int32, (8, cols), 0)
+    first_row = lax.axis_index("tile") * rows
+    first_level = lax.axis_index("group") * levels_here
+
+    columns = lax.broadcasted_iota(jnp.int32, turned.shape, 2)
+    turned[...] = jnp.where((columns >= 48) & (columns < 51), 1.0, 0.0)
+    for s in range(4):
         for m in range(windows):
-            source = sheet[:, 2 * m * LANES : (2 * m + 3) * LANES].astype(bf16)
-            pieces = jnp.dot(source, split[...], preferred_element_type=f32)
+            parts[s, m, 0:LEAD, :] = jnp.zeros((LEAD, LANES), f32)
+            parts[s, m, LEAD + 3 * pitch :, :] = jnp.zeros((parts.shape[2] - LEAD - 3 * pitch, LANES), f32)
+    reach[PAD - 8 : PAD, :] = upper_ref[3 * levels_here]
+    reach[PAD + rows : PAD + rows + 8, :] = lower_ref[3 * levels_here]
+    for r in range(0, rows, 8):
+        reach[PAD + r : PAD + r + 8, :] = reach_ref[r : r + 8, :]
+
+    def wet(number, at):
+        return jnp.where(number < reach[at : at + 8, :], 1.0, 0.0)
+
+    def rims(level, number):
+        fixed = {}
+        zero = jnp.zeros((8, cols), f32)
+        rim[:, 0:LANES] = jnp.zeros((rim.shape[0], LANES), f32)
+        rim[:, LANES + cols :] = jnp.zeros((rim.shape[0], rim.shape[1] - LANES - cols), f32)
+        for side, (outer, inner, start) in enumerate(((upper_ref, first_ref, -8), (last_ref, lower_ref, rows - 8))):
+            for f in range(3):
+                edges[f, 0:8, :] = zero
+                edges[f, 8:16, :] = outer[f * levels_here + level]
+                edges[f, 16:24, :] = inner[f * levels_here + level]
+                edges[f, 24:32, :] = zero
+            active = [wet(number, start + PAD + r) for r in (0, 8)]
+            news = [evolve(edges, 8 + r, active[r // 8], first_row + start + r, rows) for r in (0, 8)]
+            for f, ref in enumerate((east_ref, north_ref, tracer_ref)):
+                if side == 0:
+                    kept = jnp.where(line == 0, news[1][f], ref[level, 0:8, :])
+                    features = jnp.concatenate([(news[0][f] * active[0])[8 - HALO :], (kept * active[1])[:HALO]])
+                else:
+                    kept = jnp.where(line == 7, news[0][f], ref[level, rows - 8 : rows, :])
+                    features = jnp.concatenate([(kept * active[0])[8 - HALO :], (news[1][f] * active[1])[:HALO]])
+                fixed[f, side] = kept
+                at = (3 * side + f) * 8
+                rim[at : at + 8, LANES : LANES + cols] = features
+        for f, out in enumerate((out_east, out_north, out_tracer)):
+            out[level, 0:8, :] = fixed[f, 0]
+            out[level, rows - 8 : rows, :] = fixed[f, 1]
+        for start in range(8, rows - 8, 8):
+            out_tracer[level, start : start + 8, :] = tracer_ref[level, start : start + 8, :]
+
+    def split_columns(level):
+        for m in range(windows):
+            at = slice(2 * m * LANES, (2 * m + 3) * LANES)
+            pieces = jnp.dot(sheet[level, :, at].astype(bf16), split[...], preferred_element_type=f32)
             for s in range(4):
                 parts[s, m, LEAD : LEAD + 3 * pitch, :] = pieces[:, s * LANES : (s + 1) * LANES]
+        for m in range(windows):
+            at = slice(2 * m * LANES, (2 * m + 3) * LANES)
+            pieces = jnp.dot(rim[:, at].astype(bf16), split[...], preferred_element_type=f32)
+            for s in range(4):
+                for side in range(2):
+                    for f in range(3):
+                        start, from_ = LEAD + f * pitch + side * rows, (3 * side + f) * 8
+                        parts[s, m, start : start + 8, :] = pieces[from_ : from_ + 8, s * LANES : (s + 1) * LANES]
 
     def prepare(slot, base, offset):
         flipped, twin = [], slot % 2
@@ -331,17 +413,19 @@
 
         for start in range(0, rows, 8):
             rate = eddy_gain * wet(number, start + PAD)
-            east_left, east_right = sideways(field(start, 0, 1))
-            north_left, north_right = sideways(field(start, 0, 2))
+            east_left, east_right = sideways(field(start, 0, 1), lane)
+            north_left, north_right = sideways(field(start, 0, 2), lane)
             push_east = 0.5 * (field(start, 1, 0) - field(start, -1, 0)) + 0.5 * (east_right - east_left)
             push_north = 0.5 * (field(start, 1, 1) - field(start, -1, 1)) + 0.5 * (north_right - north_left)
-            out_east[level, start : start + 8, :] += rate * push_east
-            out_north[level, start : start + 8, :] += rate * push_north
+            inside = 0 < start < rows - 8
+            for out, ref, push in ((out_east, east_ref, push_east), (out_north, north_ref, push_north)):
+                base = (ref if inside else out)[level, start : start + 8, :]
+                out[level, start : start + 8, :] = base + rate * push
 
     for level in range(levels_here):
         number = (first_level + level).astype(f32)
-        advance(level, number)
-        split_columns()
+        rims(level, number)
+        split_columns(level)
         for slot in range(TURN + 1):
             prepare(slot % TURN, 0, 2 * slot)
             layer_one(slot % TURN, slot)
@@ -368,7 +452,7 @@
         finish(level, number)
 
 
-def ocean_step(tile_depth, fields, land, upper, lower, weights):
+def ocean_step(tile_depth, fields, land, upper, first, last, lower, weights):
     conv_one, bias_one, conv_two, bias_two, conv_three, bias_three = weights
     levels_here, rows, cols = fields[0].shape
     hidden = conv_two.shape[0]
@@ -385,51 +469,59 @@
     vmem = pl.BlockSpec(memory_space=pltpu.VMEM)
     smem = pl.BlockSpec(memory_space=pltpu.SMEM)
     far = pl.BlockSpec(memory_space=pltpu.HBM)
-    field = jax.ShapeDtypeStruct(fields[0].shape, f32)
+    shape = jax.ShapeDtypeStruct
+    field = shape(fields[0].shape, f32)
     top_rows = (groups + 1) * STRIPS
     stress_rows = 8 * TURN * (turns + 1)
+    inside = pl.pallas_call(
+        interior_kernel,
+        out_shape=(
+            field,
+            field,
+            field,
+            shape((rows, cols), f32),
+            shape((levels_here, 3 * pitch, (2 * windows + 1) * LANES), f32),
+            shape((LANES, width), bf16),
+            shape((4 * width, width), bf16),
+            shape((64, width), bf16),
+            shape((1, width), f32),
+            shape((16, half), f32),
+            shape((3 * LANES, 4 * LANES), bf16),
+            shape((cols, cols), bf16),
+        ),
+        in_specs=[smem, smem] + [far] * 4 + [vmem] * 5,
+        out_specs=(vmem,) * 12,
+        scratch_shapes=[
+            pltpu.VMEM((3, rows + 2 * PAD, cols), f32),
+            pltpu.VMEM((rows, cols), jnp.int32),
+            pltpu.VMEM((LANES, width), f32),
+            pltpu.SemaphoreType.DMA((4,)),
+        ],
+        cost_estimate=pl.CostEstimate(flops=20_000_000, bytes_accessed=12_000_000, transcendentals=0),
+        compiler_params=pltpu.CompilerParams(vmem_limit_bytes=16 * 1024 * 1024),
+        name="inside",
+    )(tile_depth, bias_three, *fields, land, one, bias_one[None], two, bias_two[None], three)
     return pl.pallas_call(
         step_kernel,
         out_shape=(field,) * 3,
-        in_specs=[smem, smem] + [far] * 4 + [vmem] * 7,
+        in_specs=[vmem] * 16,
         out_specs=(vmem,) * 3,
         scratch_shapes=[
-            pltpu.VMEM((4, rows + 2 * PAD, cols), f32),
-            pltpu.VMEM((rows, cols), jnp.int32),
-            pltpu.VMEM((cols, cols), bf16),
-            pltpu.VMEM((3 * LANES, 4 * LANES), bf16),
-            pltpu.VMEM((LANES, width), bf16),
-            pltpu.VMEM((64, width), bf16),
-            pltpu.VMEM((LANES, width), f32),
-            pltpu.VMEM((16, half), f32),
-            pltpu.VMEM((1, width), f32),
-            pltpu.VMEM((3 * pitch, (2 * windows + 1) * LANES), f32),
+            pltpu.VMEM((3, 32, cols), f32),
+            pltpu.VMEM((48, (2 * windows + 1) * LANES), f32),
+            pltpu.VMEM((rows + 2 * PAD, cols), f32),
             pltpu.VMEM((4, windows, LEAD + 3 * pitch + 8 * TURN, LANES), f32),
             pltpu.VMEM((2, STRIPS * (groups + 3) + 8, LANES), f32),
             pltpu.VMEM((TURN, (groups + 2) * STRIPS, LANES), bf16),
-            pltpu.VMEM((4 * width, width), bf16),
             pltpu.VMEM((TURN + 1, (groups + 2) * STRIPS, width), bf16),
             pltpu.VMEM((TURN, top_rows, width), bf16),
             pltpu.VMEM((64, top_rows), f32),
             pltpu.VMEM((stress_rows, cols), f32),
             pltpu.VMEM((cols // LANES, stress_rows - 8 * (TURN + 1), LANES), f32),
-            pltpu.SemaphoreType.DMA((4,)),
         ],
-        compiler_params=pltpu.CompilerParams(vmem_limit_bytes=44 * 1024 * 1024),
+        compiler_params=pltpu.CompilerParams(vmem_limit_bytes=40 * 1024 * 1024),
         name="step",
-    )(
-        tile_depth,
-        bias_three,
-        *fields,
-        land,
-        upper,
-        lower,
-        one,
-        bias_one[None],
-        two,
-        bias_two[None],
-        three,
-    )
+    )(*inside, upper, first, last, lower)
 
 
 def body(
@@ -453,7 +545,7 @@
     upper = lax.ppermute(last, "tile", forward)
     lower = lax.ppermute(first, "tile", backward)
     weights = (conv_one, bias_one, conv_two, bias_two, conv_three, bias_three)
-    return ocean_step(tile_depth, fields, land, upper, lower, weights)
+    return ocean_step(tile_depth, fields, land, upper, first, last, lower, weights)
 
 
 def solution(mesh):

time: 54.5 us -> 53 us (0.972)
  waiting for transfers between devices: 2.98 us -> 0.01 us
  Pallas kernels: 41.6 us -> 43 us
    ppermute x1, waiting for transfers between devices: 2.97 us -> 0.01 us  [body(): lower = lax.ppermute(first, 'tile', backward)]
    pallas_call x1 -> x2, Pallas kernels: 39.1 us -> 40.6 us  [the longest x1 36.9 us: ocean_step(): pl.pallas_call(step_kernel, out_shape=(field,) * 3, in_specs=[vmem] * 16,...]
    unnamed x24 -> x26, local copies, waits for them, and re-layouts: 2.19 us -> 2.14 us
  transfers between devices with their start and end apart: 2 -> 2, of which waited for: 1 -> 0; matrix products, arithmetic and copies ran while one was open for 0% -> 2% of each run, Pallas kernels for 0% -> 7%
where the time goes in v5:
time: 53 us; the launch traced here: 52.7 us
  Pallas kernels  43 us (81%)
  starting transfers between devices  6.63 us (13%)
  local copies, waits for them, and re-layouts  2.14 us (4%)
  between operations  0.9 us (2%)
    pallas_call x1, Pallas kernels, ocean_step(): pl.pallas_call(step_kernel, out_shape=(field,) * 3, in_specs=[vmem] * 16,...  36.9 us
    ppermute x1, starting transfers between devices, body(): upper = lax.ppermute(last, 'tile', forward)  4.71 us
    pallas_call x1, Pallas kernels, ocean_step(): pl.pallas_call(interior_kernel, out_shape=(field, field, field, shape((ro...  3.65 us
    pallas_call x1, Pallas kernels, borders(): pl.pallas_call(border_kernel, out_shape=(edge, edge), in_specs=[pl.BlockS...  2.44 us
    unnamed x26, local copies, waits for them, and re-layouts  2.14 us
    ppermute x1, starting transfers between devices, body(): lower = lax.ppermute(first, 'tile', backward)  1.92 us
  transfers between devices with their start and end apart: 2, of which 0 were waited for; matrix products, arithmetic and copies ran while one was open for 2% of the time, Pallas kernels for 7%

profile of v5, /device:TPU:1, one launch (start us, length us, event | category | flops | bytes accessed | tf_op | source)
XLA Modules:
  0.0 52.7 jit_solution(5150101525179212128)
XLA Ops:
  0.6 0.0 copy-start.6
  0.6 0.0 copy-start.2
  0.7 0.0 copy-start.1
  0.7 0.0 copy-start
  0.7 0.0 copy-start.10
  0.7 0.0 copy-start.11
  0.7 0.0 copy-start.7
  0.7 0.0 copy-start.9
  0.7 0.0 copy-start.8
  0.7 2.4 %borders.1 = (f32[4,8,1024]{2,1,0:T(8,128)}, f32[4,8,1024]{2,1,0:T(8,128)}) custom-call(s32[64]{0:T(128)} %depth_ref.3, f32[1,128,1024]{2,1,0:T(8,128)} %east_ref.3, f32[1,128,1024]{2,1,0:T(8,128)} %north_ref.3, f32[1,128,1024]{2,1,0:T(8,128)} %tracer_ref.3, s32[128,1024]{1,0:T(8,128)} %land_ref.3), custom_call_target="tpu_custom_call" | custom-call | tf_op jit(solution)/shard_map/borders/pallas_call | solution.py:58
  3.2 0.0 copy-start.4
  3.2 0.0 copy-start.5
  3.2 4.7 %collective-permute-start = (f32[4,8,1024]{2,1,0:T(8,128)}, f32[4,8,1024]{2,1,0:T(8,128)S(1)}, u32[]{:S(2)}, u32[]{:S(2)}) collective-permute-start(f32[4,8,1024]{2,1,0:T(8,128)} %get-tuple-element.29.last_ref), channel_id=1, source_target_pairs={{0,1},{1,2},{2,3},{3,4},{4,5},{5,6},{6,7},{8,9},{9,10},{10,11},{11... | collective-permute-start | bytes 393224 | tf_op jit(solution)/shard_map/ppermute | solution.py:545
  7.9 1.9 %collective-permute-start.1 = (f32[4,8,1024]{2,1,0:T(8,128)}, f32[4,8,1024]{2,1,0:T(8,128)S(1)}, u32[]{:S(2)}, u32[]{:S(2)}) collective-permute-start(f32[4,8,1024]{2,1,0:T(8,128)} %get-tuple-element.30.first_ref), channel_id=1, source_target_pairs={{1,0},{2,1},{3,2},{4,3},{5,4},{6,5},{7,6},{9,8},{10,9},{11,10},{12... | collective-permute-start | bytes 393224 | tf_op jit(solution)/shard_map/ppermute | solution.py:546
  9.8 1.0 %copy.15 = bf16[64,64,3,3]{0,1,3,2:T(8,128)(2,1)S(1)} copy(bf16[64,64,3,3]{1,0,3,2:T(8,128)(2,1)} %param.18) | data formatting | bytes 147456 | tf_op args[7]
  10.9 0.0 copy-done.10
  10.9 0.0 copy-done.11
  11.0 0.0 copy-done.6
  11.0 0.0 copy-done.2
  11.0 0.0 copy-done.1
  11.0 0.0 copy-done
  11.0 0.0 copy-done.7
  11.0 0.0 copy-done.9
  11.0 0.0 copy-done.8
  11.1 0.0 copy-start.3
  11.1 1.0 %copy-done.3 = s32[128,1024]{1,0:T(8,128)S(1)} copy-done((s32[128,1024]{1,0:T(8,128)S(1)}, s32[128,1024]{1,0:T(8,128)}, u32[]{:S(2)}) %copy-start.3) | copy-done | bytes 524312
  12.1 3.7 %inside.1 = (f32[1,128,1024]{2,1,0:T(8,128)S(1)}, f32[1,128,1024]{2,1,0:T(8,128)S(1)}, f32[1,128,1024]{2,1,0:T(8,128)S(1)}, f32[128,1024]{1,0:T(8,128)S(1)}, f32...) custom-call(s32[64]{0:T(128)S(1)} %copy-done.6, ...), custom_call_target="tpu_custom_call" | custom-call | flops 20000000 | bytes 12000000 | tf_op jit(solution)/shard_map/inside/pallas_call | solution.py:476
  15.8 0.0 collective-permute-done.upper_ref
  15.8 0.0 collective-permute-done.1.lower_ref
  15.8 0.0 copy-done.4
  15.8 0.0 copy-done.5
  15.8 36.9 %step.1 = (f32[1,128,1024]{2,1,0:T(8,128)}, f32[1,128,1024]{2,1,0:T(8,128)}, f32[1,128,1024]{2,1,0:T(8,128)}) custom-call(f32[1,128,1024]{2,1,0:T(8,128)S(1)} %get-tuple-element.17.east_ref, f32[1,128,1024]{2,1,0:T(8,128)S(1)} %get-tuple-element.18.north_ref, f32[1,128,1024]{2,1,0:T(8,128)S(1)} %get-tuple-element.19.tracer_ref, ...), custom_call_target="tpu_custom_call" | custom-call | tf_op jit(solution)/shard_map/step/pallas_call | solution.py:504
  (4 shorter events, 0.0 us)
Async XLA Ops:
  0.6 10.4 %copy-start.6 = (s32[64]{0:T(128)S(1)}, s32[64]{0:T(128)}, u32[]{:S(2)}) copy-start(s32[64]{0:T(128)} %depth_ref.3) | copy-start | bytes 772
  0.6 10.4 %copy-start.2 = (f32[1,128,1024]{2,1,0:T(8,128)S(1)}, f32[1,128,1024]{2,1,0:T(8,128)}, u32[]{:S(2)}) copy-start(f32[1,128,1024]{2,1,0:T(8,128)} %tracer_ref.3) | copy-start | bytes 1572868
  0.7 10.4 %copy-start.1 = (f32[1,128,1024]{2,1,0:T(8,128)S(1)}, f32[1,128,1024]{2,1,0:T(8,128)}, u32[]{:S(2)}) copy-start(f32[1,128,1024]{2,1,0:T(8,128)} %north_ref.3) | copy-start | bytes 1572868
  0.7 10.4 %copy-start = (f32[1,128,1024]{2,1,0:T(8,128)S(1)}, f32[1,128,1024]{2,1,0:T(8,128)}, u32[]{:S(2)}) copy-start(f32[1,128,1024]{2,1,0:T(8,128)} %east_ref.3) | copy-start | bytes 1572868
  0.7 10.3 %copy-start.10 = (bf16[64,3,3,3]{0,3,2,1:T(4,128)(2,1)S(1)}, bf16[64,3,3,3]{0,3,2,1:T(4,128)(2,1)}, u32[]{:S(2)}) copy-start(bf16[64,3,3,3]{0,3,2,1:T(4,128)(2,1)} %param.16) | copy-start | bytes 10372
  0.7 10.3 %copy-start.11 = (bf16[3,64,3,3]{1,3,2,0:T(4,128)(2,1)S(1)}, bf16[3,64,3,3]{1,3,2,0:T(4,128)(2,1)}, u32[]{:S(2)}) copy-start(bf16[3,64,3,3]{1,3,2,0:T(4,128)(2,1)} %param.20) | copy-start | bytes 10372
  0.7 10.3 %copy-start.7 = (f32[3]{0:T(128)S(1)}, f32[3]{0:T(128)}, u32[]{:S(2)}) copy-start(f32[3]{0:T(128)} %high_ref.1) | copy-start | bytes 40
  0.7 10.3 %copy-start.9 = (f32[64]{0:T(128)S(1)}, f32[64]{0:T(128)}, u32[]{:S(2)}) copy-start(f32[64]{0:T(128)} %param.19) | copy-start | bytes 772
  0.7 10.3 %copy-start.8 = (f32[64]{0:T(128)S(1)}, f32[64]{0:T(128)}, u32[]{:S(2)}) copy-start(f32[64]{0:T(128)} %param.17) | copy-start | bytes 772
  3.2 12.6 %copy-start.4 = (f32[4,8,1024]{2,1,0:T(8,128)S(1)}, f32[4,8,1024]{2,1,0:T(8,128)}, u32[]{:S(2)}) copy-start(f32[4,8,1024]{2,1,0:T(8,128)} %get-tuple-element.30.first_ref) | copy-start | bytes 393220
  3.2 12.6 %copy-start.5 = (f32[4,8,1024]{2,1,0:T(8,128)S(1)}, f32[4,8,1024]{2,1,0:T(8,128)}, u32[]{:S(2)}) copy-start(f32[4,8,1024]{2,1,0:T(8,128)} %get-tuple-element.29.last_ref) | copy-start | bytes 393220
  3.2 12.6 %collective-permute-start = (f32[4,8,1024]{2,1,0:T(8,128)}, f32[4,8,1024]{2,1,0:T(8,128)S(1)}, u32[]{:S(2)}, u32[]{:S(2)}) collective-permute-start(f32[4,8,1024]{2,1,0:T(8,128)} %get-tuple-element.29.last_ref), channel_id=1, source_target_pairs={{0,1},{1,2},{2,3},{3,4},{4,5},{5,6},{6,7},{8,9},{9,10},{10,11},{11... | collective-permute-start | bytes 393224 | tf_op jit(solution)/shard_map/ppermute | solution.py:545
  7.9 7.9 %collective-permute-start.1 = (f32[4,8,1024]{2,1,0:T(8,128)}, f32[4,8,1024]{2,1,0:T(8,128)S(1)}, u32[]{:S(2)}, u32[]{:S(2)}) collective-permute-start(f32[4,8,1024]{2,1,0:T(8,128)} %get-tuple-element.30.first_ref), channel_id=1, source_target_pairs={{1,0},{2,1},{3,2},{4,3},{5,4},{6,5},{7,6},{9,8},{10,9},{11,10},{12... | collective-permute-start | bytes 393224 | tf_op jit(solution)/shard_map/ppermute | solution.py:546
  11.1 1.0 %copy-start.3 = (s32[128,1024]{1,0:T(8,128)S(1)}, s32[128,1024]{1,0:T(8,128)}, u32[]{:S(2)}) copy-start(s32[128,1024]{1,0:T(8,128)} %land_ref.3) | copy-start | bytes 1572868

commit v6 on v5

--- a/solution.py
+++ b/solution.py
@@ -63,7 +63,7 @@
         scratch_shapes=[pltpu.VMEM((2, depth, cols), jnp.int32), pltpu.SemaphoreType.DMA((2, count))],
         compiler_params=pltpu.CompilerParams(vmem_limit_bytes=62 * 1024 * 1024),
         name="borders",
-    )(tile_depth, *fields, land)
+    )(tile_depth, *(pltpu.with_memory_space_constraint(array, pltpu.HBM) for array in (*fields, land)))
 
 
 def sideways(value, lane):
@@ -107,9 +107,9 @@
     north_ref,
     tracer_ref,
     land_ref,
+    two_ref,
     one_ref,
     low_ref,
-    two_ref,
     mid_ref,
     three_ref,
     out_east,
@@ -124,9 +124,11 @@
     high,
     split,
     merge,
+    ends,
     fields,
     shore,
     rough,
+    taps,
     sems,
 ):
     levels_here, rows, cols = east_ref.shape
@@ -144,28 +146,22 @@
             for f, ref in enumerate((east_ref, north_ref, tracer_ref))
         ]
 
+    taps_copy = pltpu.make_async_copy(two_ref, taps, sems.at[4])
     shore_copy = pltpu.make_async_copy(land_ref, shore, sems.at[3])
+    taps_copy.start()
     shore_copy.start()
     for copy in bring(0):
         copy.start()
 
     channels = two_ref.shape[2]
-    blank = jnp.zeros((channels, channels), bf16)
-    for k in range(16):
-        by, bx, py, px = k // 8, k // 4 % 2, k // 2 % 2, k % 2
-        for p in range(2):
-            row, column = 2 * by + py - p, 2 * bx + px
-            pair = [
-                two_ref[row, column - par] if 0 <= row < 3 and 0 <= column - par < 3 else blank
-                for par in range(2)
-            ]
-            two[k * channels : (k + 1) * channels, p * LANES : (p + 1) * LANES] = jnp.concatenate(pair, axis=1)
     rough[...] = jnp.zeros_like(rough)
     inputs = one_ref.shape[0]
+    kernels = [[one_ref[c, r].astype(f32) * 0.5 for r in range(3)] for c in range(inputs)]
+    kernels = [[jnp.concatenate([k[r][x : x + 1] for r in range(3)], axis=0) for x in range(3)] for k in kernels]
     none = jnp.zeros((3, channels), f32)
     for c in range(inputs):
         for source in range(4):
-            pair = [one_ref[c, source - par] if 0 <= source - par < 3 else none for par in range(2)]
+            pair = [kernels[c][source - par] if 0 <= source - par < 3 else none for par in range(2)]
             pair = jnp.concatenate(pair, axis=1)
             for p in range(2):
                 start = c * 16 + source * 4 + p
@@ -177,11 +173,20 @@
         rest = rest - piece
     one[...] = rough[...].astype(bf16)
     none = jnp.zeros((4, channels), f32)
+    outputs = three_ref.shape[0]
+    kernels = [[three_ref[c, r].astype(f32) for r in range(3)] for c in range(outputs)]
+    kernels = [
+        [
+            jnp.concatenate([k[r][x : x + 1] for k in kernels] + [none[outputs:]], axis=0)
+            for x in range(3)
+        ]
+        for r in range(3)
+    ]
     for k in range(32):
         by, bx, par, p, py = k // 16, k // 8 % 2, k // 4 % 2, k // 2 % 2, k % 2
         row = 2 * by + py - p
         pair = [
-            three_ref[row, 2 * bx + px - par] if 0 <= row < 3 and 0 <= 2 * bx + px - par < 3 else none
+            kernels[row][2 * bx + px - par] if 0 <= row < 3 and 0 <= 2 * bx + px - par < 3 else none
             for px in range(2)
         ]
         start = 32 * by + 16 * bx + 8 * par + 4 * p
@@ -198,6 +203,18 @@
     for s in range(4):
         split[:, s * LANES : (s + 1) * LANES] = jnp.where(w == 2 * x - 3 + s + LANES, 1.0, 0.0).astype(bf16)
 
+    taps_copy.wait()
+    flat = [[(taps[r, c].astype(f32) * 0.5).T.astype(bf16) for c in range(3)] for r in range(3)]
+    blank = jnp.zeros((channels, channels), bf16)
+    for k in range(16):
+        by, bx, py, px = k // 8, k // 4 % 2, k // 2 % 2, k % 2
+        for p in range(2):
+            row, column = 2 * by + py - p, 2 * bx + px
+            pair = [
+                flat[row][column - par] if 0 <= row < 3 and 0 <= column - par < 3 else blank
+                for par in range(2)
+            ]
+            two[k * channels : (k + 1) * channels, p * LANES : (p + 1) * LANES] = jnp.concatenate(pair, axis=1)
     at_strip = lax.broadcasted_iota(jnp.int32, (STRIPS, LANES), 0)
     at_lane = lax.broadcasted_iota(jnp.int32, (STRIPS, LANES), 1)
     for tile in range(cols // LANES):
@@ -239,6 +256,9 @@
                 copy.start()
         for copy in copies:
             copy.wait()
+        for f in range(3):
+            ends[0, f * levels_here + level] = fields[f, PAD : PAD + 8, :]
+            ends[1, f * levels_here + level] = fields[f, PAD + rows - 8 : PAD + rows, :]
         number = (first_level + level).astype(f32)
         for start in range(0, rows, 8):
             active = jnp.where(number < reach[start : start + 8, :], 1.0, 0.0)
@@ -262,9 +282,8 @@
     high,
     split,
     merge,
+    ends,
     upper_ref,
-    first_ref,
-    last_ref,
     lower_ref,
     out_east,
     out_north,
@@ -316,7 +335,9 @@
         zero = jnp.zeros((8, cols), f32)
         rim[:, 0:LANES] = jnp.zeros((rim.shape[0], LANES), f32)
         rim[:, LANES + cols :] = jnp.zeros((rim.shape[0], rim.shape[1] - LANES - cols), f32)
-        for side, (outer, inner, start) in enumerate(((upper_ref, first_ref, -8), (last_ref, lower_ref, rows - 8))):
+        for side, (outer, inner, start) in enumerate(
+            ((upper_ref, ends.at[0], -8), (ends.at[1], lower_ref, rows - 8))
+        ):
             for f in range(3):
                 edges[f, 0:8, :] = zero
                 edges[f, 8:16, :] = outer[f * levels_here + level]
@@ -390,10 +411,15 @@
         value = jnp.dot(gathered, two[...], preferred_element_type=f32)
         top[slot, 0:rows_two, :] = gate(value + mid[...]).astype(bf16)
 
-    def layer_three(slot, base, offset):
+    def tails():
+        rows = jnp.concatenate([top[slot, half:rows_two, :] for slot in range(TURN)], axis=0)
+        return lax.dot_general(three[...], rows, (((1,), (1,)), ((), ())), preferred_element_type=f32)
+
+    def layer_three(slot, base, offset, tail):
         new = lax.dot_general(
-            three[...], top[slot], (((1,), (1,)), ((), ())), preferred_element_type=f32
+            three[...], top[slot, 0:half, :], (((1,), (1,)), ((), ())), preferred_element_type=f32
         )
+        new = jnp.concatenate([new, tail[:, slot * STRIPS : (slot + 1) * STRIPS]], axis=1)
         old = sums[...]
         wide = old[16:32, STRIPS : STRIPS + half] + new[48:64, STRIPS : STRIPS + half]
         value = old[0:16, 0:half] + new[32:48, 0:half] + wide + high[...]
@@ -435,8 +461,9 @@
         def turn(k, carry):
             at = pl.multiple_of(8 * TURN * k, 16)
             base = 2 * TURN * k
+            tail = tails()
             for i in range(TURN):
-                layer_three(i, at, 8 * i)
+                layer_three(i, at, 8 * i, tail)
                 layer_two(i)
                 if i:
                     layer_one(i - 1, i)
@@ -447,12 +474,13 @@
             return carry
 
         lax.fori_loop(0, turns, turn, 0)
+        tail = tails()
         for i in range(TURN):
-            layer_three(i, 8 * TURN * turns, 8 * i)
+            layer_three(i, 8 * TURN * turns, 8 * i, tail)
         finish(level, number)
 
 
-def ocean_step(tile_depth, fields, land, upper, first, last, lower, weights):
+def ocean_step(tile_depth, fields, land, upper, lower, weights):
     conv_one, bias_one, conv_two, bias_two, conv_three, bias_three = weights
     levels_here, rows, cols = fields[0].shape
     hidden = conv_two.shape[0]
@@ -463,9 +491,9 @@
     turns = (rows // 2 + 2) // TURN
     pitch = rows + 4 * HALO
     f32, bf16 = jnp.float32, jnp.bfloat16
-    one = conv_one.transpose(1, 3, 2, 0).astype(f32) * 0.5
-    two = conv_two.transpose(2, 3, 1, 0) * jnp.asarray(0.5, bf16)
-    three = jnp.pad(conv_three.transpose(2, 3, 0, 1).astype(f32), ((0, 0), (0, 0), (0, 4 - conv_three.shape[0]), (0, 0)))
+    one = conv_one.transpose(1, 2, 3, 0)
+    two = conv_two.transpose(2, 3, 0, 1)
+    three = conv_three.transpose(0, 2, 3, 1)
     vmem = pl.BlockSpec(memory_space=pltpu.VMEM)
     smem = pl.BlockSpec(memory_space=pltpu.SMEM)
     far = pl.BlockSpec(memory_space=pltpu.HBM)
@@ -488,23 +516,30 @@
             shape((16, half), f32),
             shape((3 * LANES, 4 * LANES), bf16),
             shape((cols, cols), bf16),
+            shape((2, 3 * levels_here, 8, cols), f32),
         ),
-        in_specs=[smem, smem] + [far] * 4 + [vmem] * 5,
-        out_specs=(vmem,) * 12,
+        in_specs=[smem, smem] + [far] * 5 + [vmem] * 4,
+        out_specs=(vmem,) * 13,
         scratch_shapes=[
             pltpu.VMEM((3, rows + 2 * PAD, cols), f32),
             pltpu.VMEM((rows, cols), jnp.int32),
             pltpu.VMEM((LANES, width), f32),
-            pltpu.SemaphoreType.DMA((4,)),
+            pltpu.VMEM(two.shape, bf16),
+            pltpu.SemaphoreType.DMA((5,)),
         ],
         cost_estimate=pl.CostEstimate(flops=20_000_000, bytes_accessed=12_000_000, transcendentals=0),
         compiler_params=pltpu.CompilerParams(vmem_limit_bytes=16 * 1024 * 1024),
         name="inside",
-    )(tile_depth, bias_three, *fields, land, one, bias_one[None], two, bias_two[None], three)
+    )(
+        *(
+            pltpu.with_memory_space_constraint(array, pltpu.HBM)
+            for array in (tile_depth, bias_three, *fields, land, two, one, bias_one[None], bias_two[None], three)
+        )
+    )
     return pl.pallas_call(
         step_kernel,
         out_shape=(field,) * 3,
-        in_specs=[vmem] * 16,
+        in_specs=[vmem] * 15,
         out_specs=(vmem,) * 3,
         scratch_shapes=[
             pltpu.VMEM((3, 32, cols), f32),
@@ -521,7 +556,7 @@
         ],
         compiler_params=pltpu.CompilerParams(vmem_limit_bytes=40 * 1024 * 1024),
         name="step",
-    )(*inside, upper, first, last, lower)
+    )(*inside, upper, lower)
 
 
 def body(
@@ -545,7 +580,7 @@
     upper = lax.ppermute(last, "tile", forward)
     lower = lax.ppermute(first, "tile", backward)
     weights = (conv_one, bias_one, conv_two, bias_two, conv_three, bias_three)
-    return ocean_step(tile_depth, fields, land, upper, first, last, lower, weights)
+    return ocean_step(tile_depth, fields, land, upper, lower, weights)
 
 
 def solution(mesh):

time: 53 us -> 50.7 us (0.957)
  local copies, waits for them, and re-layouts: 2.14 us -> 0 us
    unnamed x26 -> x0, local copies, waits for them, and re-layouts: 2.14 us -> none
    pallas_call x1, Pallas kernels: 3.65 us -> 4.62 us  [ocean_step(): pl.pallas_call(interior_kernel, out_shape=(field, field, field, shape((ro...]
    pallas_call x1, Pallas kernels: 36.9 us -> 36.3 us  [ocean_step(): pl.pallas_call(step_kernel, out_shape=(field,) * 3, in_specs=[vmem] * 15,...]
  transfers between devices with their start and end apart: 2 -> 2, of which waited for: 0 -> 0; matrix products, arithmetic and copies ran while one was open for 2% -> 0% of each run, Pallas kernels for 7% -> 9%
where the time goes in v6:
time: 50.7 us; the launch traced here: 50.4 us
  Pallas kernels  43.2 us (85%)
  starting transfers between devices  6.5 us (13%)
  between operations  0.68 us (1%)
    pallas_call x1, Pallas kernels, ocean_step(): pl.pallas_call(step_kernel, out_shape=(field,) * 3, in_specs=[vmem] * 15,...  36.3 us
    pallas_call x1, Pallas kernels, ocean_step(): pl.pallas_call(interior_kernel, out_shape=(field, field, field, shape((ro...  4.62 us
    ppermute x1, starting transfers between devices, body(): upper = lax.ppermute(last, 'tile', forward)  4.58 us
    pallas_call x1, Pallas kernels, borders(): pl.pallas_call(border_kernel, out_shape=(edge, edge), in_specs=[pl.BlockS...  2.32 us
    ppermute x1, starting transfers between devices, body(): lower = lax.ppermute(first, 'tile', backward)  1.92 us
  transfers between devices with their start and end apart: 2, of which 0 were waited for; matrix products, arithmetic and copies ran while one was open for 0% of the time, Pallas kernels for 9%

profile of v6, /device:TPU:1, one launch (start us, length us, event | category | flops | bytes accessed | tf_op | source)
XLA Modules:
  0.0 50.4 jit_solution(13441127315109854512)
XLA Ops:
  0.6 2.3 %borders.1 = (f32[4,8,1024]{2,1,0:T(8,128)}, f32[4,8,1024]{2,1,0:T(8,128)}) custom-call(s32[64]{0:T(128)} %depth_ref.3, f32[1,128,1024]{2,1,0:T(8,128)} %east_ref.3, f32[1,128,1024]{2,1,0:T(8,128)} %north_ref.3, f32[1,128,1024]{2,1,0:T(8,128)} %tracer_ref.3, s32[128,1024]{1,0:T(8,128)} %land_ref.3), custom_call_target="tpu_custom_call" | custom-call | tf_op jit(solution)/shard_map/borders/pallas_call | solution.py:58
  3.0 4.6 %collective-permute-start = (f32[4,8,1024]{2,1,0:T(8,128)}, f32[4,8,1024]{2,1,0:T(8,128)S(1)}, u32[]{:S(2)}, u32[]{:S(2)}) collective-permute-start(f32[4,8,1024]{2,1,0:T(8,128)} %get-tuple-element.31), channel_id=1, source_target_pairs={{0,1},{1,2},{2,3},{3,4},{4,5},{5,6},{6,7},{8,9},{9,10},{10,11},{11... | collective-permute-start | bytes 393224 | tf_op jit(solution)/shard_map/ppermute | solution.py:580
  7.5 1.9 %collective-permute-start.1 = (f32[4,8,1024]{2,1,0:T(8,128)}, f32[4,8,1024]{2,1,0:T(8,128)S(1)}, u32[]{:S(2)}, u32[]{:S(2)}) collective-permute-start(f32[4,8,1024]{2,1,0:T(8,128)} %get-tuple-element.32), channel_id=1, source_target_pairs={{1,0},{2,1},{3,2},{4,3},{5,4},{6,5},{7,6},{9,8},{10,9},{11,10},{12... | collective-permute-start | bytes 393224 | tf_op jit(solution)/shard_map/ppermute | solution.py:581
  9.5 4.6 %inside.1 = (f32[1,128,1024]{2,1,0:T(8,128)S(1)}, f32[1,128,1024]{2,1,0:T(8,128)S(1)}, f32[1,128,1024]{2,1,0:T(8,128)S(1)}, f32[128,1024]{1,0:T(8,128)S(1)}, f32...) custom-call(s32[64]{0:T(128)} %depth_ref.3, ...), custom_call_target="tpu_custom_call" | custom-call | flops 20000000 | bytes 12000000 | tf_op jit(solution)/shard_map/inside/pallas_call | solution.py:504
  14.1 0.0 collective-permute-done.upper_ref
  14.1 0.0 collective-permute-done.1.lower_ref
  14.1 36.3 %step.1 = (f32[1,128,1024]{2,1,0:T(8,128)}, f32[1,128,1024]{2,1,0:T(8,128)}, f32[1,128,1024]{2,1,0:T(8,128)}) custom-call(f32[1,128,1024]{2,1,0:T(8,128)S(1)} %get-tuple-element.18.east_ref, f32[1,128,1024]{2,1,0:T(8,128)S(1)} %get-tuple-element.19.north_ref, f32[1,128,1024]{2,1,0:T(8,128)S(1)} %get-tuple-element.20.tracer_ref, ...), custom_call_target="tpu_custom_call" | custom-call | tf_op jit(solution)/shard_map/step/pallas_call | solution.py:539
Async XLA Ops:
  3.0 11.2 %collective-permute-start = (f32[4,8,1024]{2,1,0:T(8,128)}, f32[4,8,1024]{2,1,0:T(8,128)S(1)}, u32[]{:S(2)}, u32[]{:S(2)}) collective-permute-start(f32[4,8,1024]{2,1,0:T(8,128)} %get-tuple-element.31), channel_id=1, source_target_pairs={{0,1},{1,2},{2,3},{3,4},{4,5},{5,6},{6,7},{8,9},{9,10},{10,11},{11... | collective-permute-start | bytes 393224 | tf_op jit(solution)/shard_map/ppermute | solution.py:580
  7.5 6.6 %collective-permute-start.1 = (f32[4,8,1024]{2,1,0:T(8,128)}, f32[4,8,1024]{2,1,0:T(8,128)S(1)}, u32[]{:S(2)}, u32[]{:S(2)}) collective-permute-start(f32[4,8,1024]{2,1,0:T(8,128)} %get-tuple-element.32), channel_id=1, source_target_pairs={{1,0},{2,1},{3,2},{4,3},{5,4},{6,5},{7,6},{9,8},{10,9},{11,10},{12... | collective-permute-start | bytes 393224 | tf_op jit(solution)/shard_map/ppermute | solution.py:581

commit v7 on v6

--- a/solution.py
+++ b/solution.py
@@ -61,9 +61,9 @@
         in_specs=[pl.BlockSpec(memory_space=pltpu.SMEM)] + [far] * 4,
         out_specs=(vmem, vmem),
         scratch_shapes=[pltpu.VMEM((2, depth, cols), jnp.int32), pltpu.SemaphoreType.DMA((2, count))],
-        compiler_params=pltpu.CompilerParams(vmem_limit_bytes=62 * 1024 * 1024),
+        compiler_params=pltpu.CompilerParams(vmem_limit_bytes=2 * 1024 * 1024),
         name="borders",
-    )(tile_depth, *(pltpu.with_memory_space_constraint(array, pltpu.HBM) for array in (*fields, land)))
+    )(*(pltpu.with_memory_space_constraint(array, pltpu.HBM) for array in (tile_depth, *fields, land)))
 
 
 def sideways(value, lane):
@@ -363,8 +363,9 @@
 
     def split_columns(level):
         for m in range(windows):
-            at = slice(2 * m * LANES, (2 * m + 3) * LANES)
-            pieces = jnp.dot(sheet[level, :, at].astype(bf16), split[...], preferred_element_type=f32)
+            wide = min(3, (LANES + cols) // LANES - 2 * m) * LANES
+            at = slice(2 * m * LANES, 2 * m * LANES + wide)
+            pieces = jnp.dot(sheet[level, :, at].astype(bf16), split[0:wide, :], preferred_element_type=f32)
             for s in range(4):
                 parts[s, m, LEAD : LEAD + 3 * pitch, :] = pieces[:, s * LANES : (s + 1) * LANES]
         for m in range(windows):

time: 50.7 us -> 49.9 us (0.984)
  Pallas kernels: 43.2 us -> 42.4 us
    pallas_call x1, Pallas kernels: 2.32 us -> 1.62 us  [borders(): pl.pallas_call(border_kernel, out_shape=(edge, edge), in_specs=[pl.BlockS...]
where the time goes in v7:
time: 49.9 us; the launch traced here: 49.6 us
  Pallas kernels  42.4 us (85%)
  starting transfers between devices  6.5 us (13%)
  between operations  0.68 us (1%)
    pallas_call x1, Pallas kernels, ocean_step(): pl.pallas_call(step_kernel, out_shape=(field,) * 3, in_specs=[vmem] * 15,...  36.2 us
    pallas_call x1, Pallas kernels, ocean_step(): pl.pallas_call(interior_kernel, out_shape=(field, field, field, shape((ro...  4.62 us
    ppermute x1, starting transfers between devices, body(): upper = lax.ppermute(last, 'tile', forward)  4.58 us
    ppermute x1, starting transfers between devices, body(): lower = lax.ppermute(first, 'tile', backward)  1.92 us
    pallas_call x1, Pallas kernels, borders(): pl.pallas_call(border_kernel, out_shape=(edge, edge), in_specs=[pl.BlockS...  1.62 us
  transfers between devices with their start and end apart: 2, of which 0 were waited for; matrix products, arithmetic and copies ran while one was open for 0% of the time, Pallas kernels for 9%

profile of v7, /device:TPU:1, one launch (start us, length us, event | category | flops | bytes accessed | tf_op | source)
XLA Modules:
  0.0 49.6 jit_solution(605896375216244065)
XLA Ops:
  0.6 1.6 %borders.1 = (f32[4,8,1024]{2,1,0:T(8,128)S(1)}, f32[4,8,1024]{2,1,0:T(8,128)S(1)}) custom-call(s32[64]{0:T(128)} %depth_ref.3, f32[1,128,1024]{2,1,0:T(8,128)} %east_ref.3, f32[1,128,1024]{2,1,0:T(8,128)} %north_ref.3, f32[1,128,1024]{2,1,0:T(8,128)} %tracer_ref.3, s32[128,1024]{1,0:T(8,128)} %land_ref.3), custom_call_target="tpu_custom_call" | custom-call | tf_op jit(solution)/shard_map/borders/pallas_call | solution.py:58
  2.3 4.6 %collective-permute-start = (f32[4,8,1024]{2,1,0:T(8,128)S(1)}, f32[4,8,1024]{2,1,0:T(8,128)S(1)}, u32[]{:S(2)}, u32[]{:S(2)}) collective-permute-start(f32[4,8,1024]{2,1,0:T(8,128)S(1)} %get-tuple-element.31), channel_id=1, source_target_pairs={{0,1},{1,2},{2,3},{3,4},{4,5},{5,6},{6,7},{8,9},{9,10},{10,11},{11... | collective-permute-start | bytes 393224 | tf_op jit(solution)/shard_map/ppermute | solution.py:581
  6.9 1.9 %collective-permute-start.1 = (f32[4,8,1024]{2,1,0:T(8,128)S(1)}, f32[4,8,1024]{2,1,0:T(8,128)S(1)}, u32[]{:S(2)}, u32[]{:S(2)}) collective-permute-start(f32[4,8,1024]{2,1,0:T(8,128)S(1)} %get-tuple-element.32), channel_id=1, source_target_pairs={{1,0},{2,1},{3,2},{4,3},{5,4},{6,5},{7,6},{9,8},{10,9},{11,10},{12... | collective-permute-start | bytes 393224 | tf_op jit(solution)/shard_map/ppermute | solution.py:582
  8.8 4.6 %inside.1 = (f32[1,128,1024]{2,1,0:T(8,128)S(1)}, f32[1,128,1024]{2,1,0:T(8,128)S(1)}, f32[1,128,1024]{2,1,0:T(8,128)S(1)}, f32[128,1024]{1,0:T(8,128)S(1)}, f32...) custom-call(s32[64]{0:T(128)} %depth_ref.3, ...), custom_call_target="tpu_custom_call" | custom-call | flops 20000000 | bytes 12000000 | tf_op jit(solution)/shard_map/inside/pallas_call | solution.py:505
  13.4 0.0 collective-permute-done.upper_ref
  13.4 0.0 collective-permute-done.1.lower_ref
  13.4 36.2 %step.1 = (f32[1,128,1024]{2,1,0:T(8,128)}, f32[1,128,1024]{2,1,0:T(8,128)}, f32[1,128,1024]{2,1,0:T(8,128)}) custom-call(f32[1,128,1024]{2,1,0:T(8,128)S(1)} %get-tuple-element.18.east_ref, f32[1,128,1024]{2,1,0:T(8,128)S(1)} %get-tuple-element.19.north_ref, f32[1,128,1024]{2,1,0:T(8,128)S(1)} %get-tuple-element.20.tracer_ref, ...), custom_call_target="tpu_custom_call" | custom-call | tf_op jit(solution)/shard_map/step/pallas_call | solution.py:540
Async XLA Ops:
  2.3 11.2 %collective-permute-start = (f32[4,8,1024]{2,1,0:T(8,128)S(1)}, f32[4,8,1024]{2,1,0:T(8,128)S(1)}, u32[]{:S(2)}, u32[]{:S(2)}) collective-permute-start(f32[4,8,1024]{2,1,0:T(8,128)S(1)} %get-tuple-element.31), channel_id=1, source_target_pairs={{0,1},{1,2},{2,3},{3,4},{4,5},{5,6},{6,7},{8,9},{9,10},{10,11},{11... | collective-permute-start | bytes 393224 | tf_op jit(solution)/shard_map/ppermute | solution.py:581
  6.9 6.6 %collective-permute-start.1 = (f32[4,8,1024]{2,1,0:T(8,128)S(1)}, f32[4,8,1024]{2,1,0:T(8,128)S(1)}, u32[]{:S(2)}, u32[]{:S(2)}) collective-permute-start(f32[4,8,1024]{2,1,0:T(8,128)S(1)} %get-tuple-element.32), channel_id=1, source_target_pairs={{1,0},{2,1},{3,2},{4,3},{5,4},{6,5},{7,6},{9,8},{10,9},{11,10},{12... | collective-permute-start | bytes 393224 | tf_op jit(solution)/shard_map/ppermute | solution.py:582
